TPU v7x, 128 devices: a whole 4x4x4 slice. The times are simulated.
128 devices in a mesh: row: 8 (over z_hi, x), col: 16 (over z_lo, y, core).
Axes of the slice: x: 4, y: 4, z: 4 (z_hi: 2, z_lo: 2; z = z_hi * 2 + z_lo), core: 2. Of those that a mesh axis runs over, the one named last changes fastest.
Arguments:
- images: float32 [256, 28, 28, 3], P(('row', 'col')), may hold values from -6 to 6
- noise_field: float32 [256, 28, 28, 3], P(('row', 'col')), may hold values from -6 to 6
- stem_weight: bfloat16 [27, 256], replicated, may hold values from -1.25 to 1.25
- level_one: bfloat16 [4, 2304, 256], replicated, may hold values from -0.125 to 0.125
- down_weight: bfloat16 [1024, 256], replicated, may hold values from -0.1875 to 0.1875
- level_two: bfloat16 [2, 2304, 256], replicated, may hold values from -0.125 to 0.125
- up_weight: bfloat16 [256, 1024], replicated, may hold values from -0.375 to 0.375
- out_weight: bfloat16 [256, 3], replicated, may hold values from -0.375 to 0.375
- embed_weight: bfloat16 [588, 6144], replicated
- embed_bias: float32 [6144], replicated
- mlp_in: bfloat16 [6144, 24576], P('col', 'row'), may hold values from -0.078125 to 0.078125
- mlp_out: bfloat16 [24576, 6144], P('row', 'col'), may hold values from -0.0390625 to 0.0390625
Outputs:
- purified: float32 [256, 28, 28, 3], P(('row', 'col'))
- encoded: bfloat16 [1024, 6144], P('row', 'col')
All inputs are finite; a program needn't handle non-finite values.
Results may differ from a plain program's by a relative error of at most 0.018.
Values may be sent and summed in bfloat16 or wider, within the bound.
No kernel may reach another device: no remote copies, remote signals or barrier semaphores. Data moves between devices by JAX's collectives and lax.ppermute only.
A program may use at most 128 MiB of HBM per device.

v0:
```python
import functools
import math

import jax
import jax.numpy as jnp
from jax import lax
from jax.experimental import pallas as pl
from jax.experimental.pallas import tpu as pltpu
from jax.sharding import Mesh, PartitionSpec as P

step_size = 0.25
noise_gain = math.sqrt(0.5)
ln_epsilon = 1e-06
PATCH = 14
W1, W2 = 32, 16
CH = 256
f32, bf16 = jnp.float32, jnp.bfloat16


def gelu(v):
    inner = v * (0.7978845608028654 + 0.035677408136300125 * (v * v))
    half = 0.5 * v
    return half + half * jnp.tanh(inner)


def score_kernel(side, count, images, noise, stem_w, l1_hbm, down_hbm, l2_hbm, up_hbm, out_w,
                 purified, pix, stem_x, stem_k, out_k, xa, xb, ca, cb, stream, coarse,
                 l1, down, l2, up, sems):
    half = side // 2
    span1, span2 = side * W1, half * W2
    pitch1, pitch2 = span1 + W1, span2 + W2
    loads = [pltpu.make_async_copy(l1_hbm.at[0], l1.at[0], sems.at[0]),
             pltpu.make_async_copy(l1_hbm.at[1], l1.at[1], sems.at[1]),
             pltpu.make_async_copy(down_hbm, down, sems.at[2]),
             pltpu.make_async_copy(l2_hbm, l2, sems.at[3]),
             pltpu.make_async_copy(up_hbm, up, sems.at[4]),
             pltpu.make_async_copy(l1_hbm.at[2], l1.at[2], sems.at[5]),
             pltpu.make_async_copy(l1_hbm.at[3], l1.at[3], sems.at[6])]
    for load in loads:
        load.start()

    chunk = span1 // 2
    per_image = 2
    mask1 = (lax.broadcasted_iota(jnp.int32, (chunk, 1), 0) % W1) < side
    mask2 = (lax.broadcasted_iota(jnp.int32, (span2, 1), 0) % W2) < half

    def read(rows):
        return jnp.concatenate([stream[0, rows, :], stream[1, rows, :]], axis=1)

    def write(rows, value):
        stream[0, rows, :] = value[:, 0:128]
        stream[1, rows, :] = value[:, 128:256]

    for i in range(count + 1):
        z1 = jnp.zeros((W1, 3 * CH), bf16)
        z2 = jnp.zeros((W2, 3 * CH), bf16)
        xa[i * pitch1:i * pitch1 + W1, :] = z1
        xb[i * pitch1:i * pitch1 + W1, :] = z1
        ca[i * pitch2:i * pitch2 + W2, :] = z2
        cb[i * pitch2:i * pitch2 + W2, :] = z2
        stem_x[i * pitch1:i * pitch1 + W1, :] = jnp.zeros((W1, 128), bf16)
    pix[...] = jnp.zeros_like(pix)
    stem_k[...] = jnp.zeros_like(stem_k)
    out_k[...] = jnp.zeros_like(out_k)
    for dy in range(3):
        stem_k[dy, 0:9, :] = stem_w[9 * dy:9 * dy + 9, :].astype(f32)
    out_k[:, 0:3] = out_w[...].astype(f32)

    for i in range(count):
        def put(y, _, i=i):
            base = pl.multiple_of(W1 + i * pitch1 + y * W1, W1)
            pix[pl.ds(base, side), 0:3] = images[i, y].astype(bf16).astype(f32)
            return 0
        lax.fori_loop(0, side, put, 0)

    def shifted(ref, base, value):
        n = value.shape[0]
        ref[pl.ds(base, n), 0:CH] = pltpu.roll(value, 1, 0).astype(bf16)
        ref[pl.ds(base, n), CH:2 * CH] = value.astype(bf16)
        ref[pl.ds(base, n), 2 * CH:3 * CH] = pltpu.roll(value, n - 1, 0).astype(bf16)

    def each(body):
        def step(t, _):
            base = W1 + (t // per_image) * pitch1 + (t % per_image) * chunk
            body(t, pl.multiple_of(base, W1))
            return 0
        lax.fori_loop(0, count * per_image, step, 0)

    def conv(ref, base, n, width, weights):
        acc = jnp.dot(ref[pl.ds(base - width, n), :], weights[0:3 * CH, :], preferred_element_type=f32)
        acc += jnp.dot(ref[pl.ds(base, n), :], weights[3 * CH:6 * CH, :], preferred_element_type=f32)
        acc += jnp.dot(ref[pl.ds(base + width, n), :], weights[6 * CH:9 * CH, :], preferred_element_type=f32)
        return acc

    def stem_cols(t, base):
        v = pix[pl.ds(base, chunk), :]
        left = pltpu.roll(v, 1, 0)
        right = pltpu.roll(v, chunk - 1, 0)
        stem_x[pl.ds(base, chunk), :] = (left + pltpu.roll(v, 3, 1) + pltpu.roll(right, 6, 1)).astype(bf16)
    each(stem_cols)

    def stem_conv(t, base):
        acc = jnp.dot(stem_x[pl.ds(base - W1, chunk), :], stem_k[0].astype(bf16), preferred_element_type=f32)
        acc += jnp.dot(stem_x[pl.ds(base, chunk), :], stem_k[1].astype(bf16), preferred_element_type=f32)
        acc += jnp.dot(stem_x[pl.ds(base + W1, chunk), :], stem_k[2].astype(bf16), preferred_element_type=f32)
        write(pl.ds(base, chunk), acc)
        shifted(xa, base, jnp.where(mask1, gelu(acc), 0.0))
    each(stem_conv)

    loads[0].wait()

    def layer0(t, base):
        s = read(pl.ds(base, chunk)) + conv(xa, base, chunk, W1, l1.at[0])
        write(pl.ds(base, chunk), s)
        shifted(xb, base, jnp.where(mask1, gelu(s), 0.0))
    each(layer0)

    loads[1].wait()

    def layer1(t, base):
        write(pl.ds(base, chunk), read(pl.ds(base, chunk)) + conv(xb, base, chunk, W1, l1.at[1]))
    each(layer1)

    loads[2].wait()
    loads[3].wait()
    loads[4].wait()
    for i in range(count):
        base1, base2 = W1 + i * pitch1, W2 + i * pitch2
        acc = None
        for b in range(2):
            cols = read(pl.ds(base1 + b, span1 // 2, stride=2)).astype(bf16).reshape(half, 2, W2, CH)
            for a in range(2):
                part = jnp.dot(cols[:, a].reshape(span2, CH), down[(2 * a + b) * CH:(2 * a + b + 1) * CH, :],
                               preferred_element_type=f32)
                acc = part if acc is None else acc + part
        coarse[base2:base2 + span2, :] = acc
        shifted(ca, base2, jnp.where(mask2, gelu(acc), 0.0))
    for i in range(count):
        base2 = W2 + i * pitch2
        s = coarse[base2:base2 + span2, :] + conv(ca, base2, span2, W2, l2.at[0])
        coarse[base2:base2 + span2, :] = s
        shifted(cb, base2, jnp.where(mask2, gelu(s), 0.0))
    for i in range(count):
        base1, base2 = W1 + i * pitch1, W2 + i * pitch2
        s = coarse[base2:base2 + span2, :] + conv(cb, base2, span2, W2, l2.at[1])
        s = s.astype(bf16)
        for a in range(2):
            for b in range(2):
                g = (2 * a + b) * CH
                part = jnp.dot(s, up[:, g:g + CH], preferred_element_type=f32)
                for y in range(half):
                    rows = pl.ds(base1 + (2 * y + a) * W1 + b, W2, stride=2)
                    write(rows, read(rows) + part[y * W2:(y + 1) * W2, :])

    def enter(t, base):
        shifted(xa, base, jnp.where(mask1, gelu(read(pl.ds(base, chunk))), 0.0))
    each(enter)

    loads[5].wait()

    def layer2(t, base):
        s = read(pl.ds(base, chunk)) + conv(xa, base, chunk, W1, l1.at[2])
        write(pl.ds(base, chunk), s)
        shifted(xb, base, jnp.where(mask1, gelu(s), 0.0))
    each(layer2)

    loads[6].wait()
    lines = chunk // W1

    def layer3(t, base):
        s = read(pl.ds(base, chunk)) + conv(xb, base, chunk, W1, l1.at[3])
        score = jnp.dot(gelu(s).astype(bf16), out_k[...].astype(bf16), preferred_element_type=f32)
        i, y0 = t // per_image, (t % per_image) * lines
        for y in range(lines):
            purified[i, y0 + y] = (images[i, y0 + y] + step_size * score[y * W1:y * W1 + side, 0:3]
                                   + noise_gain * noise[i, y0 + y])
    each(layer3)


def score_call(images, noise, stem_w, l1, down, l2, up, out_w):
    count, side = images.shape[0], images.shape[1]
    rows1 = W1 + count * (side + 1) * W1
    rows2 = W2 + count * (side // 2 + 1) * W2
    vm = pl.BlockSpec(memory_space=pltpu.VMEM)
    hb = pl.BlockSpec(memory_space=pl.ANY)
    return pl.pallas_call(
        functools.partial(score_kernel, side, count),
        out_shape=jax.ShapeDtypeStruct(images.shape, f32),
        in_specs=[vm, vm, vm, hb, hb, hb, hb, vm],
        out_specs=vm,
        scratch_shapes=[
            pltpu.VMEM((rows1, 128), f32),
            pltpu.VMEM((rows1, 128), bf16),
            pltpu.VMEM((3, 128, CH), f32),
            pltpu.VMEM((CH, 128), f32),
            pltpu.VMEM((rows1, 3 * CH), bf16),
            pltpu.VMEM((rows1, 3 * CH), bf16),
            pltpu.VMEM((rows2, 3 * CH), bf16),
            pltpu.VMEM((rows2, 3 * CH), bf16),
            pltpu.VMEM((CH // 128, rows1, 128), f32),
            pltpu.VMEM((rows2, CH), f32),
            pltpu.VMEM(l1.shape, bf16),
            pltpu.VMEM(down.shape, bf16),
            pltpu.VMEM(l2.shape, bf16),
            pltpu.VMEM(up.shape, bf16),
            pltpu.SemaphoreType.DMA((7,)),
        ],
        compiler_params=pltpu.CompilerParams(vmem_limit_bytes=48 << 20),
        cost_estimate=pl.CostEstimate(flops=10_000_000_000, transcendentals=3_000_000, bytes_accessed=12_000_000),
        name="score_net",
    )(images, noise, stem_w, l1, down, l2, up, out_w)


def embed_kernel(parts, patches, weight_hbm, bias, own_hbm, mate_hbm, hidden, kept, sent,
                 weight, own, mate, field, total, sums, squares, sems):
    core = lax.axis_index("core")
    row = lax.axis_index("zh") * lax.axis_size("x") + lax.axis_index("x")
    tokens, depth = patches.shape[0], weight_hbm.shape[0]
    blocks, span, width = own_hbm.shape
    group = weight_hbm.shape[1] // parts
    loads = [pltpu.make_async_copy(weight_hbm.at[:, pl.ds(g * group, group)], weight.at[g], sems.at[g])
             for g in range(parts)]
    loads.append(pltpu.make_async_copy(own_hbm, own, sems.at[parts]))
    loads.append(pltpu.make_async_copy(mate_hbm, mate, sems.at[parts + 1]))
    for load in loads:
        load.start()
    sums[...] = jnp.zeros_like(sums)
    squares[...] = jnp.zeros_like(squares)
    pixels = patches[:, 0:depth]
    for g in range(parts):
        loads[g].wait()

        def embed(k, _, g=g):
            at = pl.multiple_of(k * span, 128)
            there = pl.multiple_of(g * group + k * span, 128)
            e = jnp.dot(pixels, weight[g, :, pl.ds(at, span)], preferred_element_type=f32)
            e = (e + bias[:, pl.ds(there, span)]).astype(bf16)
            field[:, pl.ds(there, span)] = e
            v = e.astype(f32)
            q = v * v
            a, b = sums[...], squares[...]
            for lane in range(0, span, 128):
                a += v[:, lane:lane + 128]
                b += q[:, lane:lane + 128]
            sums[...] = a
            squares[...] = b
            return 0
        lax.fori_loop(0, group // span, embed, 0)
    count = parts * group
    mean = jnp.sum(sums[...], axis=1, keepdims=True) / count
    square = jnp.sum(squares[...], axis=1, keepdims=True) / count
    scale = lax.rsqrt(square - mean * mean + ln_epsilon)
    place = lax.axis_index("zl") * lax.axis_size("y") + lax.axis_index("y")
    share = tokens // 8
    rows = pl.ds(pl.multiple_of(row * share, share), share)
    kept[...] = field[rows, pl.ds(pl.multiple_of((2 * place + core) * span, 128), span)]
    sent[...] = field[rows, pl.ds(pl.multiple_of((2 * place + 1 - core) * span, 128), span)]
    total[...] = jnp.zeros_like(total)
    loads[parts].wait()
    loads[parts + 1].wait()

    def mix(b, _):
        for block, side in ((own, core), (mate, 1 - core)):
            at = pl.multiple_of((2 * b + side) * span, 128)
            v = field[:, pl.ds(at, span)].astype(f32)
            normed = ((v - mean) * scale).astype(bf16)
            total[...] += jnp.dot(normed, block[b], preferred_element_type=f32)
        return 0
    lax.fori_loop(0, blocks, mix, 0)
    value = gelu(total[...]).astype(bf16)
    for b in range(hidden.shape[0]):
        hidden[b] = value


def embed_call(patches, weight, bias, own, mate, copies):
    tokens, blocks, span, width = patches.shape[0], *own.shape
    features = weight.shape[1]
    parts = 4
    share = tokens // 8
    vm = pl.BlockSpec(memory_space=pltpu.VMEM)
    hb = pl.BlockSpec(memory_space=pl.ANY)
    return pl.pallas_call(
        functools.partial(embed_kernel, parts),
        out_shape=(jax.ShapeDtypeStruct((copies, tokens, width), bf16),
                   jax.ShapeDtypeStruct((share, span), bf16),
                   jax.ShapeDtypeStruct((share, span), bf16)),
        in_specs=[vm, hb, vm, hb, hb],
        out_specs=(vm, vm, vm),
        scratch_shapes=[
            pltpu.VMEM((parts, weight.shape[0], features // parts), bf16),
            pltpu.VMEM(own.shape, bf16),
            pltpu.VMEM(mate.shape, bf16),
            pltpu.VMEM((tokens, features), bf16),
            pltpu.VMEM((tokens, width), f32),
            pltpu.VMEM((tokens, 128), f32),
            pltpu.VMEM((tokens, 128), f32),
            pltpu.SemaphoreType.DMA((parts + 2,)),
        ],
        compiler_params=pltpu.CompilerParams(vmem_limit_bytes=48 << 20),
        cost_estimate=pl.CostEstimate(flops=7_000_000_000, transcendentals=200_000, bytes_accessed=20_000_000),
        name="embed_mlp",
    )(patches, weight, bias, own, mate)


def mix_kernel(hidden, own, mate, out, total):
    b = pl.program_id(0)
    span = own.shape[1]

    @pl.when(b == 0)
    def _():
        total[...] = jnp.zeros_like(total)
    h = hidden[0]
    total[:, 0:span] += jnp.dot(h, own[...], preferred_element_type=f32)
    total[:, span:2 * span] += jnp.dot(h, mate[...], preferred_element_type=f32)

    @pl.when(b == pl.num_programs(0) - 1)
    def _():
        core = lax.axis_index("core")
        share = out.shape[1]
        for r in range(out.shape[0] // 2):
            rows = slice(r * share, (r + 1) * share)
            out[2 * r + core] = total[rows, 0:span].astype(bf16)
            out[2 * r + 1 - core] = total[rows, span:2 * span].astype(bf16)


def mix_call(hidden, own, mate):
    blocks, tokens, width = hidden.shape
    span = own.shape[1]
    return pl.pallas_call(
        mix_kernel,
        grid=(blocks,),
        out_shape=jax.ShapeDtypeStruct((16, tokens // 8, span), bf16),
        in_specs=[pl.BlockSpec((1, tokens, width), lambda b: (b, 0, 0)),
                  pl.BlockSpec((width, span), lambda b: (b, 0)),
                  pl.BlockSpec((width, span), lambda b: (b, 0))],
        out_specs=pl.BlockSpec((16, tokens // 8, span), lambda b: (0, 0, 0)),
        scratch_shapes=[pltpu.VMEM((tokens, 2 * span), f32)],
        compiler_params=pltpu.CompilerParams(vmem_limit_bytes=32 << 20),
        cost_estimate=pl.CostEstimate(flops=2_400_000_000, transcendentals=0, bytes_accessed=9_000_000),
        name="mlp_out",
    )(hidden, own, mate)


def split_kernel(width, whole, blocks, sems):
    loads = [pltpu.make_async_copy(whole.at[:, pl.ds(b * width, width)], blocks.at[b], sems.at[b])
             for b in range(blocks.shape[0])]
    for load in loads:
        load.start()
    for load in loads:
        load.wait()


def split_call(whole, count):
    depth, width = whole.shape[0], whole.shape[1] // count
    hb = pl.BlockSpec(memory_space=pl.ANY)
    return pl.pallas_call(
        functools.partial(split_kernel, width),
        out_shape=jax.ShapeDtypeStruct((count, depth, width), whole.dtype),
        in_specs=[hb],
        out_specs=hb,
        scratch_shapes=[pltpu.SemaphoreType.DMA((count,))],
        cost_estimate=pl.CostEstimate(flops=0, transcendentals=0, bytes_accessed=2 * whole.size * 2),
        name="split_columns",
    )(whole)


def swap(value):
    return lax.ppermute(value, "core", [(0, 1), (1, 0)])


def patchify(pixels):
    count, side = pixels.shape[0], pixels.shape[1]
    grid = side // PATCH
    blocks = pixels.reshape(count, grid, PATCH, grid, PATCH, 3).transpose(0, 1, 3, 2, 4, 5)
    return blocks.reshape(count * grid * grid, PATCH * PATCH * 3)


def on_device(images, noise_field, stem_weight, level_one, down_weight, level_two, up_weight,
              out_weight, embed_weight, embed_bias, mlp_in, mlp_out):
    span = mlp_in.shape[0]
    own_in = lax.all_to_all(split_call(mlp_in, 8), ("zl", "y"), 0, 0)
    mate_out = swap(mlp_out)

    purified = score_call(images, noise_field, stem_weight, level_one, down_weight, level_two,
                          up_weight, out_weight)
    own_in, purified = lax.optimization_barrier((own_in, purified))
    mate_in = swap(own_in)
    patches = patchify(purified.astype(bf16))
    patches = jnp.pad(patches, ((0, 0), (0, 640 - patches.shape[1])))
    every = ("zh", "x", "zl", "y")
    tokens = lax.all_to_all(jnp.broadcast_to(patches[None], (64,) + patches.shape), every, 0, 0)
    tokens = tokens.reshape(-1, tokens.shape[-1])
    hidden, kept, sent = embed_call(tokens, embed_weight, embed_bias[None], own_in, mate_in, 8)
    other = swap(sent)
    hidden = lax.all_to_all(hidden, ("zl", "y"), 0, 0)
    shares = mix_call(hidden, mlp_out, mate_out)
    shares = lax.all_to_all(shares, ("zh", "x", "core"), 0, 0)
    mixed = jnp.sum(shares.reshape(8, 2, 8, 8, span).astype(f32), axis=0)
    core = lax.axis_index("core")
    values = jnp.where(core == 0, jnp.stack([kept, other]), jnp.stack([other, kept]))
    encoded = mixed + values.reshape(2, 8, 8, span).astype(f32)
    encoded = encoded.transpose(1, 0, 2, 3).reshape(128, span).astype(bf16)
    return purified, encoded


def solution(mesh):
    fine = Mesh(mesh.devices.reshape(2, 4, 2, 4, 2), ("zh", "x", "zl", "y", "core"))
    row, col = ("zh", "x"), ("zl", "y", "core")
    images = P(row + col, None, None, None)
    placed = (images, images) + (P(),) * 8 + (P(col, row), P(row, col))
    return jax.shard_map(on_device, mesh=fine, in_specs=placed, out_specs=(images, P(row, col)),
                         check_vma=False)
```

profile of v0, /device:TPU:1, one launch (start us, length us, event | category | flops | bytes accessed | tf_op | source)
XLA Modules:
  0.0 233.1 jit_solution(16883762537084332163)
XLA Ops:
  0.6 72.6 %split_columns.1 = bf16[8,384,384]{2,1,0:T(8,128)(2,1)} custom-call(bf16[384,3072]{1,0:T(8,128)(2,1)} %whole.1), custom_call_target="tpu_custom_call" | custom-call | bytes 4718592 | tf_op jit(solution)/shard_map/split_columns/pallas_call | solution.py:356
  73.3 6.5 %all-to-all-start = ((bf16[8,384,384]{2,1,0:T(8,128)(2,1)}), bf16[8,384,384]{2,1,0:T(8,128)(2,1)S(1)}, u32[]{:S(2)}, u32[]{:S(2)}) async-start(bf16[8,384,384]{2,1,0:T(8,128)(2,1)} %split_columns.1), calls=%async_computation | async-start | bytes 4718592 | tf_op jit(solution)/shard_map/all_to_all | solution.py:381
  79.9 1.4 copy.19.images
  81.3 1.4 copy.20.noise
  82.7 0.1 copy.21.out_w
  82.9 1.2 copy-done
  84.0 1.2 copy-done.1
  85.2 1.0 copy-done.5
  86.2 1.0 copy-done.6
  87.3 20.8 %score_net.1 = f32[2,28,28,3]{3,2,1,0:T(8,128)S(1)} custom-call(f32[2,28,28,3]{3,2,1,0:T(8,128)S(1)} %copy-done, f32[2,28,28,3]{3,2,1,0:T(8,128)S(1)} %copy-done.1, bf16[27,256]{1,0:T(8,128)(2,1)S(1)} %copy-done.8, bf16[4,2304,256]{2,1,0:T(8,128)(2,1)} %l1_hbm.1, bf16[1024,256]{1,0:T(8,128)(2,1)S(1)} %copy-done.5, bf16[2,2304,256]{2,1,0:T(8,128)(2,1)} %l2_hbm.1, ...), custom_call_target="tpu_custom_call" | custom-call | flops 10000000000 | bytes 12000000 | tf_op jit(solution)/shard_map/score_net/pallas_call | solution.py:186
  108.1 1.6 all-to-all-done.own_hbm
  109.7 0.8 collective-permute-start
  110.5 0.9 convert_element_type.23
  111.4 1.5 copy.22
  112.9 0.1 reshape.28
  113.0 1.6 copy.23
  114.5 1.5 reshape.29
  116.1 26.1 %all_to_all.20 = bf16[64,8,640]{2,1,0:T(8,128)(2,1)S(1)} all-to-all(bf16[64,8,640]{2,1,0:T(8,128)(2,1)S(1)} %broadcast_in_dim.4), channel_id=1, replica_groups=mesh['zh'=2,'x'=4,'zl'=2,'y'=4,'core'=2] {'zh','x','zl','y'}, dimensions={0} | all-to-all | bytes 1310720 | tf_op jit(solution)/shard_map/all_to_all | solution.py:391
  142.1 18.3 %embed_mlp.1 = (bf16[8,512,384]{2,1,0:T(8,128)(2,1)}, bf16[64,384]{1,0:T(8,128)(2,1)S(1)}, bf16[64,384]{1,0:T(8,128)(2,1)S(1)}) custom-call(bf16[512,640]{1,0:T(8,128)(2,1)S(1)} %bitcast.12, bf16[588,6144]{1,0:T(8,128)(2,1)} %weight_hbm.1, f32[1,6144]{1,0:T(1,128)S(1)} %bitcast.14, bf16[8,384,384]{2,1,0:T(8,128)(2,1)S(1)} %all-to-all-done.own_hbm, ...), custom_call_target="tpu_custom_call" | custom-call | flops 7000000000 | bytes 20000000 | tf_op jit(solution)/shard_map/embed_mlp/pallas_call | solution.py:282
  160.5 4.6 %all-to-all-start.2 = ((bf16[8,512,384]{2,1,0:T(8,128)(2,1)}), bf16[8,512,384]{2,1,0:T(8,128)(2,1)}, u32[]{:S(2)}, u32[]{:S(2)}) async-start(bf16[8,512,384]{2,1,0:T(8,128)(2,1)} %get-tuple-element.9), calls=%async_computation.2 | async-start | bytes 6291456 | tf_op jit(solution)/shard_map/all_to_all | solution.py:395
  165.1 2.0 collective-permute-start.1
  167.1 4.2 %collective-permute-done.1.mate = bf16[3072,384]{1,0:T(8,128)(2,1)S(1)} collective-permute-done((bf16[3072,384]{1,0:T(8,128)(2,1)S(1)}, bf16[3072,384]{1,0:T(8,128)(2,1)S(1)}, u32[]{:S(2)}, u32[]{:S(2)}) %collective-permute-start.1) | collective-permute-done | bytes 2359328 | tf_op jit(solution)/shard_map/ppermute | solution.py:368
  171.2 1.5 copy-done.3
  172.7 30.7 %all-to-all-done.2.hidden = bf16[8,512,384]{2,1,0:T(8,128)(2,1)} async-done(((bf16[8,512,384]{2,1,0:T(8,128)(2,1)}), bf16[8,512,384]{2,1,0:T(8,128)(2,1)}, u32[]{:S(2)}, u32[]{:S(2)}) %all-to-all-start.2) | async-done | bytes 3145760 | tf_op jit(solution)/shard_map/all_to_all | solution.py:395
  203.4 1.7 copy-done.4
  205.0 8.4 %mlp_out.1 = bf16[16,64,384]{2,1,0:T(8,128)(2,1)} custom-call(bf16[8,512,384]{2,1,0:T(8,128)(2,1)} %all-to-all-done.2.hidden, bf16[3072,384]{1,0:T(8,128)(2,1)S(1)} %copy-done.2, bf16[3072,384]{1,0:T(8,128)(2,1)S(1)} %copy-done.4), custom_call_target="tpu_custom_call" | custom-call | flops 2400000000 | bytes 9000000 | tf_op jit(solution)/shard_map/mlp_out/pallas_call | solution.py:329
  213.4 4.3 %all-to-all-start.3 = ((bf16[16,64,384]{2,1,0:T(8,128)(2,1)}), bf16[16,64,384]{2,1,0:T(8,128)(2,1)S(1)}, u32[]{:S(2)}, u32[]{:S(2)}) async-start(bf16[16,64,384]{2,1,0:T(8,128)(2,1)} %mlp_out.1), calls=%async_computation.3 | async-start | bytes 1572864 | tf_op jit(solution)/shard_map/all_to_all | solution.py:397
  217.7 1.1 copy.25
  218.7 0.2 collective-permute-start.2
  219.0 13.3 %all-to-all-done.3 = bf16[16,64,384]{2,1,0:T(8,128)(2,1)S(1)} async-done(((bf16[16,64,384]{2,1,0:T(8,128)(2,1)}), bf16[16,64,384]{2,1,0:T(8,128)(2,1)S(1)}, u32[]{:S(2)}, u32[]{:S(2)}) %all-to-all-start.3) | async-done | bytes 786464 | tf_op jit(solution)/shard_map/all_to_all | solution.py:397
  232.3 0.1 convert_reduce_fusion
  232.5 0.7 copy.24
  (23 shorter events, 0.1 us)
Async XLA Ops:
  73.3 6.6 %copy-start.9 = (f32[2,28,28,3]{2,0,3,1:T(2,128)S(1)}, f32[2,28,28,3]{2,0,3,1:T(2,128)}, u32[]{:S(2)}) copy-start(f32[2,28,28,3]{2,0,3,1:T(2,128)} %param.12) | copy-start | bytes 56452
  73.3 8.0 %copy-start.10 = (f32[2,28,28,3]{2,0,3,1:T(2,128)S(1)}, f32[2,28,28,3]{2,0,3,1:T(2,128)}, u32[]{:S(2)}) copy-start(f32[2,28,28,3]{2,0,3,1:T(2,128)} %param.13) | copy-start | bytes 56452
  73.3 9.4 %copy-start.11 = (bf16[256,3]{0,1:T(4,128)(2,1)S(1)}, bf16[256,3]{0,1:T(4,128)(2,1)}, u32[]{:S(2)}) copy-start(bf16[256,3]{0,1:T(4,128)(2,1)} %param.19) | copy-start | bytes 4612
  73.3 9.5 %copy-start.8 = (bf16[27,256]{1,0:T(8,128)(2,1)S(1)}, bf16[27,256]{1,0:T(8,128)(2,1)}, u32[]{:S(2)}) copy-start(bf16[27,256]{1,0:T(8,128)(2,1)} %stem_w.1) | copy-start | bytes 41476
  73.3 36.4 %all-to-all-start = ((bf16[8,384,384]{2,1,0:T(8,128)(2,1)}), bf16[8,384,384]{2,1,0:T(8,128)(2,1)S(1)}, u32[]{:S(2)}, u32[]{:S(2)}) async-start(bf16[8,384,384]{2,1,0:T(8,128)(2,1)} %split_columns.1), calls=%async_computation | async-start | bytes 4718592 | tf_op jit(solution)/shard_map/all_to_all | solution.py:381
  82.8 1.2 copy-start
  84.0 1.2 copy-start.1
  85.2 1.0 copy-start.5
  86.2 1.0 copy-start.6
  108.1 34.0 %copy-start.7 = (f32[6144]{0:T(1024)S(1)}, f32[6144]{0:T(1024)}, u32[]{:S(2)}) copy-start(f32[6144]{0:T(1024)} %param.21) | copy-start | bytes 73732
  109.7 32.4 %collective-permute-start = (bf16[8,384,384]{2,1,0:T(8,128)(2,1)S(1)}, bf16[8,384,384]{2,1,0:T(8,128)(2,1)}, u32[]{:S(2)}, u32[]{:S(2)}) collective-permute-start(bf16[8,384,384]{2,1,0:T(8,128)(2,1)S(1)} %all-to-all-done.own_hbm), channel_id=1, source_target_pairs={{0,1},{1,0},{2,3},{3,2},{4,5},{5,4},{6,7},{7,6},{8,9},{9,8},{10,11... | collective-permute-start | bytes 7077896 | tf_op jit(solution)/shard_map/ppermute | solution.py:368
  160.5 4.6 %copy-start.2 = (bf16[3072,384]{1,0:T(8,128)(2,1)S(1)}, bf16[3072,384]{1,0:T(8,128)(2,1)}, u32[]{:S(2)}) copy-start(bf16[3072,384]{1,0:T(8,128)(2,1)} %own.1) | copy-start | bytes 7077892
  160.5 42.9 %all-to-all-start.2 = ((bf16[8,512,384]{2,1,0:T(8,128)(2,1)}), bf16[8,512,384]{2,1,0:T(8,128)(2,1)}, u32[]{:S(2)}, u32[]{:S(2)}) async-start(bf16[8,512,384]{2,1,0:T(8,128)(2,1)} %get-tuple-element.9), calls=%async_computation.2 | async-start | bytes 6291456 | tf_op jit(solution)/shard_map/all_to_all | solution.py:395
  165.1 6.1 %collective-permute-start.1 = (bf16[3072,384]{1,0:T(8,128)(2,1)S(1)}, bf16[3072,384]{1,0:T(8,128)(2,1)S(1)}, u32[]{:S(2)}, u32[]{:S(2)}) collective-permute-start(bf16[3072,384]{1,0:T(8,128)(2,1)S(1)} %copy-done.2), channel_id=1, source_target_pairs={{0,1},{1,0},{2,3},{3,2},{4,5},{5,4},{6,7},{7,6},{8,9},{9,8},{10,11... | collective-permute-start | bytes 7077896 | tf_op jit(solution)/shard_map/ppermute | solution.py:368
  171.2 1.5 copy-start.3
  203.4 1.7 copy-start.4
  213.4 18.9 %all-to-all-start.3 = ((bf16[16,64,384]{2,1,0:T(8,128)(2,1)}), bf16[16,64,384]{2,1,0:T(8,128)(2,1)S(1)}, u32[]{:S(2)}, u32[]{:S(2)}) async-start(bf16[16,64,384]{2,1,0:T(8,128)(2,1)} %mlp_out.1), calls=%async_computation.3 | async-start | bytes 1572864 | tf_op jit(solution)/shard_map/all_to_all | solution.py:397
  218.7 13.7 %collective-permute-start.2 = (bf16[64,384]{1,0:T(8,128)(2,1)S(1)}, bf16[64,384]{1,0:T(8,128)(2,1)S(1)}, u32[]{:S(2)}, u32[]{:S(2)}) collective-permute-start(bf16[64,384]{1,0:T(8,128)(2,1)S(1)} %get-tuple-element.11), channel_id=1, source_target_pairs={{0,1},{1,0},{2,3},{3,2},{4,5},{5,4},{6,7},{7,6},{8,9},{9,8},{10,11... | collective-permute-start | bytes 147464 | tf_op jit(solution)/shard_map/ppermute | solution.py:368
where the time goes:
time: 238 us; the launch traced here: 233 us
  Pallas kernels  120 us (50%)
  waiting for transfers between devices  49.7 us (21%)
  blocking collectives  26.1 us (11%)
  starting transfers between devices  18.4 us (8%)
  local copies, waits for them, and re-layouts  17 us (7%)
    pallas_call x1, Pallas kernels, split_call(): pl.pallas_call(functools.partial(split_kernel, width), out_shape=jax.Shap...  72.6 us
    all_to_all x1, waiting for transfers between devices, on_device(): hidden = lax.all_to_all(hidden, ('zl', 'y'), 0, 0)  30.7 us
    all_to_all x1, blocking collectives, on_device(): lax.all_to_all(jnp.broadcast_to(patches[None], (64,) + patches.shape), ev...  26.1 us
    pallas_call x1, Pallas kernels, score_call(): pl.pallas_call(functools.partial(score_kernel, side, count), out_shape=ja...  20.8 us
    pallas_call x1, Pallas kernels, embed_call(): pl.pallas_call(functools.partial(embed_kernel, parts), out_shape=(jax.Sha...  18.3 us
    all_to_all x1, waiting for transfers between devices, on_device(): shares = lax.all_to_all(shares, ('zh', 'x', 'core'), 0, 0)  13.3 us
    unnamed x28, local copies, waits for them, and re-layouts  11.6 us
    pallas_call x1, Pallas kernels, mix_call(): pl.pallas_call(mix_kernel, grid=(blocks,), out_shape=jax.ShapeDtypeStruct...  8.4 us
  transfers between devices with their start and end apart: 6, of which 4 were waited for; matrix products, arithmetic and copies ran while one was open for 4% of the time, Pallas kernels for 9%

commit v1 on v0

--- a/solution.py
+++ b/solution.py
@@ -268,11 +268,14 @@
         return 0
     lax.fori_loop(0, blocks, mix, 0)
     value = gelu(total[...]).astype(bf16)
-    for b in range(hidden.shape[0]):
-        hidden[b] = value
-
-
-def embed_call(patches, weight, bias, own, mate, copies):
+    grouped = value.reshape(8, 2, 4 * 8, width)
+    for side in range(2):
+        part = grouped[:, side].reshape(tokens // 2, width)
+        for y in range(4):
+            hidden[4 * side + y] = part
+
+
+def embed_call(patches, weight, bias, own, mate):
     tokens, blocks, span, width = patches.shape[0], *own.shape
     features = weight.shape[1]
     parts = 4
@@ -281,7 +284,7 @@
     hb = pl.BlockSpec(memory_space=pl.ANY)
     return pl.pallas_call(
         functools.partial(embed_kernel, parts),
-        out_shape=(jax.ShapeDtypeStruct((copies, tokens, width), bf16),
+        out_shape=(jax.ShapeDtypeStruct((8, tokens // 2, width), bf16),
                    jax.ShapeDtypeStruct((share, span), bf16),
                    jax.ShapeDtypeStruct((share, span), bf16)),
         in_specs=[vm, hb, vm, hb, hb],
@@ -302,7 +305,7 @@
     )(patches, weight, bias, own, mate)
 
 
-def mix_kernel(hidden, own, mate, out, total):
+def mix_kernel(hidden, own, mate, far, far_mate, out, total):
     b = pl.program_id(0)
     span = own.shape[1]
 
@@ -310,55 +313,51 @@
     def _():
         total[...] = jnp.zeros_like(total)
     h = hidden[0]
-    total[:, 0:span] += jnp.dot(h, own[...], preferred_element_type=f32)
-    total[:, span:2 * span] += jnp.dot(h, mate[...], preferred_element_type=f32)
+    for k, weight in enumerate((own, mate, far, far_mate)):
+        total[:, k * span:(k + 1) * span] += jnp.dot(h, weight[...], preferred_element_type=f32)
 
     @pl.when(b == pl.num_programs(0) - 1)
     def _():
-        core = lax.axis_index("core")
+        core, side = lax.axis_index("core"), lax.axis_index("zl")
         share = out.shape[1]
-        for r in range(out.shape[0] // 2):
+        for r in range(out.shape[0] // 4):
             rows = slice(r * share, (r + 1) * share)
-            out[2 * r + core] = total[rows, 0:span].astype(bf16)
-            out[2 * r + 1 - core] = total[rows, span:2 * span].astype(bf16)
-
-
-def mix_call(hidden, own, mate):
+            for k in range(4):
+                to_side = side if k < 2 else 1 - side
+                to_core = core if k % 2 == 0 else 1 - core
+                out[4 * r + 2 * to_side + to_core] = total[rows, k * span:(k + 1) * span].astype(bf16)
+
+
+def mix_call(hidden, *weights):
     blocks, tokens, width = hidden.shape
-    span = own.shape[1]
+    span = weights[0].shape[1]
+    shape = (32, tokens // 8, span)
     return pl.pallas_call(
         mix_kernel,
         grid=(blocks,),
-        out_shape=jax.ShapeDtypeStruct((16, tokens // 8, span), bf16),
-        in_specs=[pl.BlockSpec((1, tokens, width), lambda b: (b, 0, 0)),
-                  pl.BlockSpec((width, span), lambda b: (b, 0)),
-                  pl.BlockSpec((width, span), lambda b: (b, 0))],
-        out_specs=pl.BlockSpec((16, tokens // 8, span), lambda b: (0, 0, 0)),
-        scratch_shapes=[pltpu.VMEM((tokens, 2 * span), f32)],
+        out_shape=jax.ShapeDtypeStruct(shape, bf16),
+        in_specs=[pl.BlockSpec((1, tokens, width), lambda b: (b, 0, 0))]
+        + [pl.BlockSpec((width, span), lambda b: (b, 0))] * 4,
+        out_specs=pl.BlockSpec(shape, lambda b: (0, 0, 0)),
+        scratch_shapes=[pltpu.VMEM((tokens, 4 * span), f32)],
         compiler_params=pltpu.CompilerParams(vmem_limit_bytes=32 << 20),
-        cost_estimate=pl.CostEstimate(flops=2_400_000_000, transcendentals=0, bytes_accessed=9_000_000),
+        cost_estimate=pl.CostEstimate(flops=2_400_000_000, transcendentals=0, bytes_accessed=12_000_000),
         name="mlp_out",
-    )(hidden, own, mate)
-
-
-def split_kernel(width, whole, blocks, sems):
-    loads = [pltpu.make_async_copy(whole.at[:, pl.ds(b * width, width)], blocks.at[b], sems.at[b])
-             for b in range(blocks.shape[0])]
-    for load in loads:
-        load.start()
-    for load in loads:
-        load.wait()
+    )(hidden, *weights)
+
+
+def split_kernel(whole, blocks):
+    blocks[0] = whole[...]
 
 
 def split_call(whole, count):
     depth, width = whole.shape[0], whole.shape[1] // count
-    hb = pl.BlockSpec(memory_space=pl.ANY)
     return pl.pallas_call(
-        functools.partial(split_kernel, width),
+        split_kernel,
+        grid=(count,),
         out_shape=jax.ShapeDtypeStruct((count, depth, width), whole.dtype),
-        in_specs=[hb],
-        out_specs=hb,
-        scratch_shapes=[pltpu.SemaphoreType.DMA((count,))],
+        in_specs=[pl.BlockSpec((depth, width), lambda b: (0, b))],
+        out_specs=pl.BlockSpec((1, depth, width), lambda b: (b, 0, 0)),
         cost_estimate=pl.CostEstimate(flops=0, transcendentals=0, bytes_accessed=2 * whole.size * 2),
         name="split_columns",
     )(whole)
@@ -379,23 +378,26 @@
               out_weight, embed_weight, embed_bias, mlp_in, mlp_out):
     span = mlp_in.shape[0]
     own_in = lax.all_to_all(split_call(mlp_in, 8), ("zl", "y"), 0, 0)
-    mate_out = swap(mlp_out)
+    far_out = lax.ppermute(mlp_out, "zl", [(0, 1), (1, 0)])
 
     purified = score_call(images, noise_field, stem_weight, level_one, down_weight, level_two,
                           up_weight, out_weight)
-    own_in, purified = lax.optimization_barrier((own_in, purified))
-    mate_in = swap(own_in)
     patches = patchify(purified.astype(bf16))
     patches = jnp.pad(patches, ((0, 0), (0, 640 - patches.shape[1])))
+    own_in, _ = lax.optimization_barrier((own_in, patches))
+    mate_in = swap(own_in)
     every = ("zh", "x", "zl", "y")
     tokens = lax.all_to_all(jnp.broadcast_to(patches[None], (64,) + patches.shape), every, 0, 0)
     tokens = tokens.reshape(-1, tokens.shape[-1])
-    hidden, kept, sent = embed_call(tokens, embed_weight, embed_bias[None], own_in, mate_in, 8)
+    hidden, kept, sent = embed_call(tokens, embed_weight, embed_bias[None], own_in, mate_in)
+    far_out, hidden = lax.optimization_barrier((far_out, hidden))
+    mate_out, far_mate_out = swap(mlp_out), swap(far_out)
     other = swap(sent)
     hidden = lax.all_to_all(hidden, ("zl", "y"), 0, 0)
-    shares = mix_call(hidden, mlp_out, mate_out)
-    shares = lax.all_to_all(shares, ("zh", "x", "core"), 0, 0)
-    mixed = jnp.sum(shares.reshape(8, 2, 8, 8, span).astype(f32), axis=0)
+    shares = mix_call(hidden, mlp_out, mate_out, far_out, far_mate_out)
+    shares = lax.all_to_all(shares, ("zh", "x", "zl", "core"), 0, 0)
+    mixed = jnp.sum(shares.reshape(8, 2, 2, 4, 8, span).astype(f32), axis=0)
+    mixed = mixed.transpose(1, 0, 2, 3, 4).reshape(2, 8, 8, span)
     core = lax.axis_index("core")
     values = jnp.where(core == 0, jnp.stack([kept, other]), jnp.stack([other, kept]))
     encoded = mixed + values.reshape(2, 8, 8, span).astype(f32)

time: 238 us -> 185 us (0.78); the launches traced: 233 us -> 184 us
  Pallas kernels: 120 us -> 52.6 us
  waiting for transfers between devices: 49.7 us -> 86.1 us
  blocking collectives: 26.1 us -> 0 us
  starting transfers between devices: 18.4 us -> 36.6 us
  local copies, waits for them, and re-layouts: 17 us -> 7.85 us
    pallas_call x1, Pallas kernels: 72.6 us -> 5.78 us  [split_call(): pl.pallas_call(split_kernel, grid=(count,), out_shape=jax.ShapeDtypeStruc...]
    all_to_all x1 -> x2, waiting for transfers between devices: 13.3 us -> 59.5 us  [the longest x1 46.3 us: on_device(): lax.all_to_all(jnp.broadcast_to(patches[None], (64,) + patches.shape), ev...]
    all_to_all x1 -> x0, blocking collectives: 26.1 us -> none  [on_device(): lax.all_to_all(jnp.broadcast_to(patches[None], (64,) + patches.shape), ev...]
    all_to_all x1 -> x2, starting transfers between devices: 4.25 us -> 19.7 us  [the longest x1 13.7 us: on_device(): lax.all_to_all(jnp.broadcast_to(patches[None], (64,) + patches.shape), ev...]
    all_to_all x1, waiting for transfers between devices: 30.7 us -> 21.5 us  [on_device(): hidden = lax.all_to_all(hidden, ('zl', 'y'), 0, 0)]
    unnamed x28 -> x20, local copies, waits for them, and re-layouts: 11.6 us -> 4.46 us
    ppermute x3 -> x4, waiting for transfers between devices: 4.17 us -> 0.01 us  [swap(): return lax.ppermute(value, 'core', [(0, 1), (1, 0)])]
    all_to_all x1, waiting for transfers between devices: 1.56 us -> 5.01 us  [on_device(): own_in = lax.all_to_all(split_call(mlp_in, 8), ('zl', 'y'), 0, 0)]
  transfers between devices with their start and end apart: 6 -> 9, of which waited for: 4 -> 4; matrix products, arithmetic and copies ran while one was open for 4% -> 3% of each run, Pallas kernels for 9% -> 20%
where the time goes in v1:
time: 185 us; the launch traced here: 184 us
  waiting for transfers between devices  86.1 us (47%)
  Pallas kernels  52.6 us (28%)
  starting transfers between devices  36.6 us (20%)
  local copies, waits for them, and re-layouts  7.85 us (4%)
    all_to_all x1, waiting for transfers between devices, on_device(): lax.all_to_all(jnp.broadcast_to(patches[None], (64,) + patches.shape), ev...  46.3 us
    all_to_all x1, waiting for transfers between devices, on_device(): hidden = lax.all_to_all(hidden, ('zl', 'y'), 0, 0)  21.5 us
    pallas_call x1, Pallas kernels, score_call(): pl.pallas_call(functools.partial(score_kernel, side, count), out_shape=ja...  20.8 us
    pallas_call x1, Pallas kernels, embed_call(): pl.pallas_call(functools.partial(embed_kernel, parts), out_shape=(jax.Sha...  16.6 us
    all_to_all x1, starting transfers between devices, on_device(): lax.all_to_all(jnp.broadcast_to(patches[None], (64,) + patches.shape), ev...  13.7 us
    all_to_all x1, waiting for transfers between devices, on_device(): shares = lax.all_to_all(shares, ('zh', 'x', 'zl', 'core'), 0, 0)  13.3 us
    pallas_call x1, Pallas kernels, mix_call(): pl.pallas_call(mix_kernel, grid=(blocks,), out_shape=jax.ShapeDtypeStruct...  9.47 us
    all_to_all x1, starting transfers between devices, on_device(): hidden = lax.all_to_all(hidden, ('zl', 'y'), 0, 0)  7.17 us
  transfers between devices with their start and end apart: 9, of which 4 were waited for; matrix products, arithmetic and copies ran while one was open for 3% of the time, Pallas kernels for 20%

profile of v1, /device:TPU:1, one launch (start us, length us, event | category | flops | bytes accessed | tf_op | source)
XLA Modules:
  0.0 184.2 jit_solution(14336340360141196975)
XLA Ops:
  0.6 5.8 %split_columns.1 = bf16[8,384,384]{2,1,0:T(8,128)(2,1)} custom-call(bf16[384,3072]{1,0:T(8,128)(2,1)} %whole.1), custom_call_target="tpu_custom_call" | custom-call | bytes 4718592 | tf_op jit(solution)/shard_map/split_columns/pallas_call | solution.py:355
  6.4 6.5 %all-to-all-start.1 = ((bf16[8,384,384]{2,1,0:T(8,128)(2,1)}), bf16[8,384,384]{2,1,0:T(8,128)(2,1)}, u32[]{:S(2)}, u32[]{:S(2)}) async-start(bf16[8,384,384]{2,1,0:T(8,128)(2,1)} %split_columns.1), calls=%async_computation.1 | async-start | bytes 4718592 | tf_op jit(solution)/shard_map/all_to_all | solution.py:380
  13.0 0.5 copy.48.images
  13.4 0.5 copy.49.noise
  13.9 0.1 copy.50.out_w
  14.1 1.0 copy-done.2
  15.1 20.8 %score_net.1 = f32[2,28,28,3]{3,2,1,0:T(8,128)S(1)} custom-call(f32[2,28,28,3]{3,2,1,0:T(8,128)S(1)} %copy.48.images, f32[2,28,28,3]{3,2,1,0:T(8,128)S(1)} %copy.49.noise, bf16[27,256]{1,0:T(8,128)(2,1)S(1)} %copy-done.4, bf16[4,2304,256]{2,1,0:T(8,128)(2,1)} %l1_hbm.1, bf16[1024,256]{1,0:T(8,128)(2,1)S(1)} %copy-done.1, bf16[2,2304,256]{2,1,0:T(8,128)(2,1)} %l2_hbm.1, ...), custom_call_target="tpu_custom_call" | custom-call | flops 10000000000 | bytes 12000000 | tf_op jit(solution)/shard_map/score_net/pallas_call | solution.py:186
  36.0 0.0 copy-start.3
  36.0 0.1 convert_element_type.23
  36.1 0.5 copy.51
  36.5 0.1 reshape.31
  36.6 0.8 copy.52
  37.4 0.5 reshape.32
  37.9 5.0 %all-to-all-done.1.own_hbm = bf16[8,384,384]{2,1,0:T(8,128)(2,1)} async-done(((bf16[8,384,384]{2,1,0:T(8,128)(2,1)}), bf16[8,384,384]{2,1,0:T(8,128)(2,1)}, u32[]{:S(2)}, u32[]{:S(2)}) %all-to-all-start.1) | async-done | bytes 2359328 | tf_op jit(solution)/shard_map/all_to_all | solution.py:380
  42.9 0.8 collective-permute-start.1
  43.8 0.3 collective-permute-start
  44.0 0.9 broadcast_in_dim.4
  44.9 13.7 %all-to-all-start = ((bf16[64,8,640]{2,1,0:T(8,128)(2,1)}), bf16[64,8,640]{2,1,0:T(8,128)(2,1)S(1)}, u32[]{:S(2)}, u32[]{:S(2)}) async-start(bf16[64,8,640]{2,1,0:T(8,128)(2,1)} %broadcast_in_dim.4), calls=%async_computation | async-start | bytes 1310720 | tf_op jit(solution)/shard_map/all_to_all | solution.py:390
  58.6 0.8 collective-permute-start.2
  59.4 46.3 %all-to-all-done = bf16[64,8,640]{2,1,0:T(8,128)(2,1)S(1)} async-done(((bf16[64,8,640]{2,1,0:T(8,128)(2,1)}), bf16[64,8,640]{2,1,0:T(8,128)(2,1)S(1)}, u32[]{:S(2)}, u32[]{:S(2)}) %all-to-all-start) | async-done | bytes 655392 | tf_op jit(solution)/shard_map/all_to_all | solution.py:390
  105.7 16.6 %embed_mlp.1 = (bf16[8,256,384]{2,1,0:T(8,128)(2,1)S(1)}, bf16[64,384]{1,0:T(8,128)(2,1)S(1)}, bf16[64,384]{1,0:T(8,128)(2,1)S(1)}) custom-call(bf16[512,640]{1,0:T(8,128)(2,1)S(1)} %bitcast.14, bf16[588,6144]{1,0:T(8,128)(2,1)} %weight_hbm.1, f32[1,6144]{1,0:T(1,128)S(1)} %bitcast.16, bf16[8,384,384]{2,1,0:T(8,128)(2,1)} %all-to-all-done.1.own_hbm, ...), custom_call_target="tpu_custom_call" | custom-call | flops 7000000000 | bytes 20000000 | tf_op jit(solution)/shard_map/embed_mlp/pallas_call | solution.py:285
  122.3 1.2 copy-done
  123.5 1.1 collective-permute-start.3
  124.6 7.2 %all-to-all-start.2 = ((bf16[8,256,384]{2,1,0:T(8,128)(2,1)}), bf16[8,256,384]{2,1,0:T(8,128)(2,1)S(1)}, u32[]{:S(2)}, u32[]{:S(2)}) async-start(bf16[8,256,384]{2,1,0:T(8,128)(2,1)} %copy-done), calls=%async_computation.2 | async-start | bytes 3145728 | tf_op jit(solution)/shard_map/all_to_all | solution.py:396
  131.8 21.5 %all-to-all-done.2.hidden = bf16[8,256,384]{2,1,0:T(8,128)(2,1)S(1)} async-done(((bf16[8,256,384]{2,1,0:T(8,128)(2,1)}), bf16[8,256,384]{2,1,0:T(8,128)(2,1)S(1)}, u32[]{:S(2)}, u32[]{:S(2)}) %all-to-all-start.2) | async-done | bytes 1572896 | tf_op jit(solution)/shard_map/all_to_all | solution.py:396
  153.3 9.5 %mlp_out.1 = bf16[32,32,384]{2,1,0:T(8,128)(2,1)} custom-call(bf16[8,256,384]{2,1,0:T(8,128)(2,1)S(1)} %all-to-all-done.2.hidden, bf16[3072,384]{1,0:T(8,128)(2,1)} %own.1, bf16[3072,384]{1,0:T(8,128)(2,1)} %collective-permute-done.2.mate, bf16[3072,384]{1,0:T(8,128)(2,1)} %collective-permute-done.far, bf16[3072,384]{1,0:T(8,128)(2,1)} %collective-permute-done.3.far_mate), custom_call_target="tpu_custom_call" | custom-call | flops 2400000000 | bytes 12000000 | tf_op jit(solution)/shard_map/mlp_out/pallas_call | solution.py:335
  162.8 6.0 %all-to-all-start.3 = ((bf16[32,32,384]{2,1,0:T(8,128)(2,1)}), bf16[32,32,384]{2,1,0:T(8,128)(2,1)S(1)}, u32[]{:S(2)}, u32[]{:S(2)}) async-start(bf16[32,32,384]{2,1,0:T(8,128)(2,1)} %mlp_out.1), calls=%async_computation.3 | async-start | bytes 1572864 | tf_op jit(solution)/shard_map/all_to_all | solution.py:398
  168.8 1.1 copy.55
  169.8 0.2 collective-permute-start.4
  170.1 13.3 %all-to-all-done.3 = bf16[32,32,384]{2,1,0:T(8,128)(2,1)S(1)} async-done(((bf16[32,32,384]{2,1,0:T(8,128)(2,1)}), bf16[32,32,384]{2,1,0:T(8,128)(2,1)S(1)}, u32[]{:S(2)}, u32[]{:S(2)}) %all-to-all-start.3) | async-done | bytes 786464 | tf_op jit(solution)/shard_map/all_to_all | solution.py:398
  183.3 0.1 convert_reduce_fusion
  183.5 0.7 copy.54
  (21 shorter events, 0.1 us)
Async XLA Ops:
  6.4 6.5 %copy-start.5 = (f32[2,28,28,3]{2,0,3,1:T(2,128)S(1)}, f32[2,28,28,3]{2,0,3,1:T(2,128)}, u32[]{:S(2)}) copy-start(f32[2,28,28,3]{2,0,3,1:T(2,128)} %param.12) | copy-start | bytes 56452
  6.4 7.0 %copy-start.6 = (f32[2,28,28,3]{2,0,3,1:T(2,128)S(1)}, f32[2,28,28,3]{2,0,3,1:T(2,128)}, u32[]{:S(2)}) copy-start(f32[2,28,28,3]{2,0,3,1:T(2,128)} %param.13) | copy-start | bytes 56452
  6.4 7.5 %copy-start.7 = (bf16[256,3]{0,1:T(4,128)(2,1)S(1)}, bf16[256,3]{0,1:T(4,128)(2,1)}, u32[]{:S(2)}) copy-start(bf16[256,3]{0,1:T(4,128)(2,1)} %param.19) | copy-start | bytes 4612
  6.4 7.7 %copy-start.1 = (bf16[1024,256]{1,0:T(8,128)(2,1)S(1)}, bf16[1024,256]{1,0:T(8,128)(2,1)}, u32[]{:S(2)}) copy-start(bf16[1024,256]{1,0:T(8,128)(2,1)} %down_hbm.1) | copy-start | bytes 1572868
  6.4 7.7 %copy-start.4 = (bf16[27,256]{1,0:T(8,128)(2,1)S(1)}, bf16[27,256]{1,0:T(8,128)(2,1)}, u32[]{:S(2)}) copy-start(bf16[27,256]{1,0:T(8,128)(2,1)} %stem_w.1) | copy-start | bytes 41476
  6.4 36.5 %all-to-all-start.1 = ((bf16[8,384,384]{2,1,0:T(8,128)(2,1)}), bf16[8,384,384]{2,1,0:T(8,128)(2,1)}, u32[]{:S(2)}, u32[]{:S(2)}) async-start(bf16[8,384,384]{2,1,0:T(8,128)(2,1)} %split_columns.1), calls=%async_computation.1 | async-start | bytes 4718592 | tf_op jit(solution)/shard_map/all_to_all | solution.py:380
  14.1 1.0 copy-start.2
  36.0 69.7 %copy-start.3 = (f32[6144]{0:T(1024)S(1)}, f32[6144]{0:T(1024)}, u32[]{:S(2)}) copy-start(f32[6144]{0:T(1024)} %param.21) | copy-start | bytes 73732
  42.9 62.8 %collective-permute-start.1 = (bf16[8,384,384]{2,1,0:T(8,128)(2,1)}, bf16[8,384,384]{2,1,0:T(8,128)(2,1)}, u32[]{:S(2)}, u32[]{:S(2)}) collective-permute-start(bf16[8,384,384]{2,1,0:T(8,128)(2,1)} %all-to-all-done.1.own_hbm), channel_id=1, source_target_pairs={{0,1},{1,0},{2,3},{3,2},{4,5},{5,4},{6,7},{7,6},{8,9},{9,8},{10,11... | collective-permute-start | bytes 7077896 | tf_op jit(solution)/shard_map/ppermute | solution.py:367
  43.8 79.7 %collective-permute-start = (bf16[3072,384]{1,0:T(8,128)(2,1)}, bf16[3072,384]{1,0:T(8,128)(2,1)}, u32[]{:S(2)}, u32[]{:S(2)}) collective-permute-start(bf16[3072,384]{1,0:T(8,128)(2,1)} %own.1), channel_id=1, source_target_pairs={{0,8},{8,0},{1,9},{9,1},{2,10},{10,2},{3,11},{11,3},{4,12},{12,4},... | collective-permute-start | bytes 7077896 | tf_op jit(solution)/shard_map/ppermute | solution.py:381
  44.9 60.8 %all-to-all-start = ((bf16[64,8,640]{2,1,0:T(8,128)(2,1)}), bf16[64,8,640]{2,1,0:T(8,128)(2,1)S(1)}, u32[]{:S(2)}, u32[]{:S(2)}) async-start(bf16[64,8,640]{2,1,0:T(8,128)(2,1)} %broadcast_in_dim.4), calls=%async_computation | async-start | bytes 1310720 | tf_op jit(solution)/shard_map/all_to_all | solution.py:390
  58.6 73.2 %collective-permute-start.2 = (bf16[3072,384]{1,0:T(8,128)(2,1)}, bf16[3072,384]{1,0:T(8,128)(2,1)}, u32[]{:S(2)}, u32[]{:S(2)}) collective-permute-start(bf16[3072,384]{1,0:T(8,128)(2,1)} %own.1), channel_id=1, source_target_pairs={{0,1},{1,0},{2,3},{3,2},{4,5},{5,4},{6,7},{7,6},{8,9},{9,8},{10,11... | collective-permute-start | bytes 7077896 | tf_op jit(solution)/shard_map/ppermute | solution.py:367
  122.3 1.2 copy-start
  123.5 29.8 %collective-permute-start.3 = (bf16[3072,384]{1,0:T(8,128)(2,1)}, bf16[3072,384]{1,0:T(8,128)(2,1)}, u32[]{:S(2)}, u32[]{:S(2)}) collective-permute-start(bf16[3072,384]{1,0:T(8,128)(2,1)} %collective-permute-done.far), channel_id=1, source_target_pairs={{0,1},{1,0},{2,3},{3,2},{4,5},{5,4},{6,7},{7,6},{8,9},{9,8},{10,11... | collective-permute-start | bytes 7077896 | tf_op jit(solution)/shard_map/ppermute | solution.py:367
  124.6 28.7 %all-to-all-start.2 = ((bf16[8,256,384]{2,1,0:T(8,128)(2,1)}), bf16[8,256,384]{2,1,0:T(8,128)(2,1)S(1)}, u32[]{:S(2)}, u32[]{:S(2)}) async-start(bf16[8,256,384]{2,1,0:T(8,128)(2,1)} %copy-done), calls=%async_computation.2 | async-start | bytes 3145728 | tf_op jit(solution)/shard_map/all_to_all | solution.py:396
  162.8 20.6 %all-to-all-start.3 = ((bf16[32,32,384]{2,1,0:T(8,128)(2,1)}), bf16[32,32,384]{2,1,0:T(8,128)(2,1)S(1)}, u32[]{:S(2)}, u32[]{:S(2)}) async-start(bf16[32,32,384]{2,1,0:T(8,128)(2,1)} %mlp_out.1), calls=%async_computation.3 | async-start | bytes 1572864 | tf_op jit(solution)/shard_map/all_to_all | solution.py:398
  169.8 13.6 %collective-permute-start.4 = (bf16[64,384]{1,0:T(8,128)(2,1)S(1)}, bf16[64,384]{1,0:T(8,128)(2,1)S(1)}, u32[]{:S(2)}, u32[]{:S(2)}) collective-permute-start(bf16[64,384]{1,0:T(8,128)(2,1)S(1)} %get-tuple-element.13), channel_id=1, source_target_pairs={{0,1},{1,0},{2,3},{3,2},{4,5},{5,4},{6,7},{7,6},{8,9},{9,8},{10,11... | collective-permute-start | bytes 147464 | tf_op jit(solution)/shard_map/ppermute | solution.py:367

commit v2 on v0

--- a/solution.py
+++ b/solution.py
@@ -212,68 +212,73 @@
 
 
 def embed_kernel(parts, patches, weight_hbm, bias, own_hbm, mate_hbm, hidden, kept, sent,
-                 weight, own, mate, field, total, sums, squares, sems):
+                 weight, mixer, total, sums, squares, sems, own_sems, mate_sems):
     core = lax.axis_index("core")
     row = lax.axis_index("zh") * lax.axis_size("x") + lax.axis_index("x")
+    place = lax.axis_index("zl") * lax.axis_size("y") + lax.axis_index("y")
     tokens, depth = patches.shape[0], weight_hbm.shape[0]
     blocks, span, width = own_hbm.shape
     group = weight_hbm.shape[1] // parts
+    count = parts * group
+    step = 512
+
+    def piece(b, side, source, sem):
+        at = pl.multiple_of((2 * b + side) * span, span)
+        return pltpu.make_async_copy(source.at[b], mixer.at[pl.ds(at, span), :], sem.at[b])
+
     loads = [pltpu.make_async_copy(weight_hbm.at[:, pl.ds(g * group, group)], weight.at[g], sems.at[g])
              for g in range(parts)]
-    loads.append(pltpu.make_async_copy(own_hbm, own, sems.at[parts]))
-    loads.append(pltpu.make_async_copy(mate_hbm, mate, sems.at[parts + 1]))
-    for load in loads:
+    pieces = [(piece(b, core, own_hbm, own_sems), piece(b, 1 - core, mate_hbm, mate_sems)) for b in range(blocks)]
+    loads[0].start()
+    for pair in pieces[:2]:
+        pair[0].start()
+        pair[1].start()
+    for load in loads[1:]:
         load.start()
-    sums[...] = jnp.zeros_like(sums)
-    squares[...] = jnp.zeros_like(squares)
+    for pair in pieces[2:]:
+        pair[0].start()
+        pair[1].start()
     pixels = patches[:, 0:depth]
-    for g in range(parts):
-        loads[g].wait()
-
-        def embed(k, _, g=g):
-            at = pl.multiple_of(k * span, 128)
-            there = pl.multiple_of(g * group + k * span, 128)
-            e = jnp.dot(pixels, weight[g, :, pl.ds(at, span)], preferred_element_type=f32)
-            e = (e + bias[:, pl.ds(there, span)]).astype(bf16)
-            field[:, pl.ds(there, span)] = e
-            v = e.astype(f32)
-            q = v * v
-            a, b = sums[...], squares[...]
-            for lane in range(0, span, 128):
-                a += v[:, lane:lane + 128]
-                b += q[:, lane:lane + 128]
-            sums[...] = a
-            squares[...] = b
-            return 0
-        lax.fori_loop(0, group // span, embed, 0)
-    count = parts * group
+    ones = jnp.ones((16, step), bf16)
+    ready = 0
+    for c in range(count // step):
+        g, at = (c * step) // group, (c * step) % group
+        if at == 0:
+            loads[g].wait()
+        e = jnp.dot(pixels, weight[g, :, at:at + step], preferred_element_type=f32)
+        e = (e + bias[:, c * step:(c + 1) * step]).astype(bf16)
+        v = e.astype(f32)
+        q = v * v
+        a = v[:, 0:128] + v[:, 128:256] + v[:, 256:384] + v[:, 384:512]
+        b = q[:, 0:128] + q[:, 128:256] + q[:, 256:384] + q[:, 384:512]
+        sums[...] = a if c == 0 else sums[...] + a
+        squares[...] = b if c == 0 else squares[...] + b
+        while ready * 2 * span < (c + 1) * step:
+            pieces[ready][0].wait()
+            pieces[ready][1].wait()
+            ready += 1
+        part = jnp.dot(jnp.concatenate([e, ones], axis=0), mixer[c * step:(c + 1) * step, :],
+                       preferred_element_type=f32)
+        total[...] = part if c == 0 else total[...] + part
+    share = tokens // 8
+    mine = patches[pl.ds(pl.multiple_of(row * share, share), share), 0:depth]
+    for out, side in ((kept, core), (sent, 1 - core)):
+        first = 2 * place + side
+        g, at = first // (group // span), first % (group // span)
+        e = jnp.dot(mine, weight[g, :, pl.ds(pl.multiple_of(at * span, 128), span)], preferred_element_type=f32)
+        out[...] = (e + bias[:, pl.ds(pl.multiple_of(first * span, 128), span)]).astype(bf16)
     mean = jnp.sum(sums[...], axis=1, keepdims=True) / count
     square = jnp.sum(squares[...], axis=1, keepdims=True) / count
     scale = lax.rsqrt(square - mean * mean + ln_epsilon)
-    place = lax.axis_index("zl") * lax.axis_size("y") + lax.axis_index("y")
-    share = tokens // 8
-    rows = pl.ds(pl.multiple_of(row * share, share), share)
-    kept[...] = field[rows, pl.ds(pl.multiple_of((2 * place + core) * span, 128), span)]
-    sent[...] = field[rows, pl.ds(pl.multiple_of((2 * place + 1 - core) * span, 128), span)]
-    total[...] = jnp.zeros_like(total)
-    loads[parts].wait()
-    loads[parts + 1].wait()
-
-    def mix(b, _):
-        for block, side in ((own, core), (mate, 1 - core)):
-            at = pl.multiple_of((2 * b + side) * span, 128)
-            v = field[:, pl.ds(at, span)].astype(f32)
-            normed = ((v - mean) * scale).astype(bf16)
-            total[...] += jnp.dot(normed, block[b], preferred_element_type=f32)
-        return 0
-    lax.fori_loop(0, blocks, mix, 0)
-    value = gelu(total[...]).astype(bf16)
+    column = total[tokens:tokens + 1, :]
+    value = gelu((total[0:tokens, :] - mean * column) * scale).astype(bf16)
     for b in range(hidden.shape[0]):
         hidden[b] = value
 
 
-def embed_call(patches, weight, bias, own, mate, copies):
-    tokens, blocks, span, width = patches.shape[0], *own.shape
+def embed_call(patches, weight, bias, own, mate):
+    tokens = patches.shape[0]
+    _, span, width = own.shape
     features = weight.shape[1]
     parts = 4
     share = tokens // 8
@@ -281,84 +286,95 @@
     hb = pl.BlockSpec(memory_space=pl.ANY)
     return pl.pallas_call(
         functools.partial(embed_kernel, parts),
-        out_shape=(jax.ShapeDtypeStruct((copies, tokens, width), bf16),
+        out_shape=(jax.ShapeDtypeStruct((8, tokens, width), bf16),
                    jax.ShapeDtypeStruct((share, span), bf16),
                    jax.ShapeDtypeStruct((share, span), bf16)),
         in_specs=[vm, hb, vm, hb, hb],
         out_specs=(vm, vm, vm),
         scratch_shapes=[
             pltpu.VMEM((parts, weight.shape[0], features // parts), bf16),
-            pltpu.VMEM(own.shape, bf16),
-            pltpu.VMEM(mate.shape, bf16),
-            pltpu.VMEM((tokens, features), bf16),
-            pltpu.VMEM((tokens, width), f32),
+            pltpu.VMEM((features, width), bf16),
+            pltpu.VMEM((tokens + 16, width), f32),
             pltpu.VMEM((tokens, 128), f32),
             pltpu.VMEM((tokens, 128), f32),
-            pltpu.SemaphoreType.DMA((parts + 2,)),
+            pltpu.SemaphoreType.DMA((parts,)),
+            pltpu.SemaphoreType.DMA((8,)),
+            pltpu.SemaphoreType.DMA((8,)),
         ],
-        compiler_params=pltpu.CompilerParams(vmem_limit_bytes=48 << 20),
+        compiler_params=pltpu.CompilerParams(vmem_limit_bytes=40 << 20),
         cost_estimate=pl.CostEstimate(flops=7_000_000_000, transcendentals=200_000, bytes_accessed=20_000_000),
         name="embed_mlp",
     )(patches, weight, bias, own, mate)
 
 
-def mix_kernel(hidden, own, mate, out, total):
-    b = pl.program_id(0)
-    span = own.shape[1]
-
-    @pl.when(b == 0)
-    def _():
-        total[...] = jnp.zeros_like(total)
-    h = hidden[0]
-    total[:, 0:span] += jnp.dot(h, own[...], preferred_element_type=f32)
-    total[:, span:2 * span] += jnp.dot(h, mate[...], preferred_element_type=f32)
-
-    @pl.when(b == pl.num_programs(0) - 1)
-    def _():
-        core = lax.axis_index("core")
-        share = out.shape[1]
-        for r in range(out.shape[0] // 2):
-            rows = slice(r * share, (r + 1) * share)
-            out[2 * r + core] = total[rows, 0:span].astype(bf16)
-            out[2 * r + 1 - core] = total[rows, span:2 * span].astype(bf16)
+def mix_kernel(hidden_hbm, own_hbm, mate_hbm, out, hidden, weight, total, sems):
+    core = lax.axis_index("core")
+    blocks, tokens, width = hidden_hbm.shape
+    span = own_hbm.shape[1]
+    parts = blocks // 2
+    deep = 2 * width
+    loads = []
+    for k in range(parts):
+        rows = pl.ds(k * deep, deep)
+        pairs = [(own_hbm.at[rows, :], weight.at[rows, pl.ds(0, span)]),
+                 (mate_hbm.at[rows, :], weight.at[rows, pl.ds(span, span)])]
+        pairs += [(hidden_hbm.at[b], hidden.at[:, pl.ds(b * width, width)]) for b in (2 * k, 2 * k + 1)]
+        loads.append([pltpu.make_async_copy(a, b, sems.at[k, n]) for n, (a, b) in enumerate(pairs)])
+        for load in loads[-1]:
+            load.start()
+    for k in range(parts):
+        for load in loads[k]:
+            load.wait()
+        at = slice(k * deep, (k + 1) * deep)
+        part = jnp.dot(hidden[:, at], weight[at, :], preferred_element_type=f32)
+        if k == 0:
+            total[...] = part
+        elif k < parts - 1:
+            total[...] += part
+        else:
+            done = (total[...] + part).astype(bf16)
+    share = out.shape[1]
+    for r in range(tokens // share):
+        rows = slice(r * share, (r + 1) * share)
+        out[2 * r + core] = done[rows, 0:span]
+        out[2 * r + 1 - core] = done[rows, span:2 * span]
 
 
 def mix_call(hidden, own, mate):
     blocks, tokens, width = hidden.shape
-    span = own.shape[1]
+    depth, span = own.shape
+    hb = pl.BlockSpec(memory_space=pl.ANY)
     return pl.pallas_call(
         mix_kernel,
-        grid=(blocks,),
         out_shape=jax.ShapeDtypeStruct((16, tokens // 8, span), bf16),
-        in_specs=[pl.BlockSpec((1, tokens, width), lambda b: (b, 0, 0)),
-                  pl.BlockSpec((width, span), lambda b: (b, 0)),
-                  pl.BlockSpec((width, span), lambda b: (b, 0))],
-        out_specs=pl.BlockSpec((16, tokens // 8, span), lambda b: (0, 0, 0)),
-        scratch_shapes=[pltpu.VMEM((tokens, 2 * span), f32)],
-        compiler_params=pltpu.CompilerParams(vmem_limit_bytes=32 << 20),
+        in_specs=[hb, hb, hb],
+        out_specs=pl.BlockSpec(memory_space=pltpu.VMEM),
+        scratch_shapes=[
+            pltpu.VMEM((tokens, depth), bf16),
+            pltpu.VMEM((depth, 2 * span), bf16),
+            pltpu.VMEM((tokens, 2 * span), f32),
+            pltpu.SemaphoreType.DMA((blocks // 2, 4)),
+        ],
+        compiler_params=pltpu.CompilerParams(vmem_limit_bytes=24 << 20),
         cost_estimate=pl.CostEstimate(flops=2_400_000_000, transcendentals=0, bytes_accessed=9_000_000),
         name="mlp_out",
     )(hidden, own, mate)
 
 
-def split_kernel(width, whole, blocks, sems):
-    loads = [pltpu.make_async_copy(whole.at[:, pl.ds(b * width, width)], blocks.at[b], sems.at[b])
-             for b in range(blocks.shape[0])]
-    for load in loads:
-        load.start()
-    for load in loads:
-        load.wait()
+def split_kernel(whole, blocks):
+    width = blocks.shape[2]
+    for b in range(blocks.shape[0]):
+        blocks[b] = whole[:, b * width:(b + 1) * width]
 
 
 def split_call(whole, count):
     depth, width = whole.shape[0], whole.shape[1] // count
-    hb = pl.BlockSpec(memory_space=pl.ANY)
     return pl.pallas_call(
-        functools.partial(split_kernel, width),
+        split_kernel,
+        grid=(count // 2,),
         out_shape=jax.ShapeDtypeStruct((count, depth, width), whole.dtype),
-        in_specs=[hb],
-        out_specs=hb,
-        scratch_shapes=[pltpu.SemaphoreType.DMA((count,))],
+        in_specs=[pl.BlockSpec((depth, 2 * width), lambda b: (0, b))],
+        out_specs=pl.BlockSpec((2, depth, width), lambda b: (b, 0, 0)),
         cost_estimate=pl.CostEstimate(flops=0, transcendentals=0, bytes_accessed=2 * whole.size * 2),
         name="split_columns",
     )(whole)
@@ -383,14 +399,14 @@
 
     purified = score_call(images, noise_field, stem_weight, level_one, down_weight, level_two,
                           up_weight, out_weight)
-    own_in, purified = lax.optimization_barrier((own_in, purified))
-    mate_in = swap(own_in)
     patches = patchify(purified.astype(bf16))
     patches = jnp.pad(patches, ((0, 0), (0, 640 - patches.shape[1])))
+    own_in, mate_out, _ = lax.optimization_barrier((own_in, mate_out, patches))
+    mate_in = swap(own_in)
     every = ("zh", "x", "zl", "y")
     tokens = lax.all_to_all(jnp.broadcast_to(patches[None], (64,) + patches.shape), every, 0, 0)
     tokens = tokens.reshape(-1, tokens.shape[-1])
-    hidden, kept, sent = embed_call(tokens, embed_weight, embed_bias[None], own_in, mate_in, 8)
+    hidden, kept, sent = embed_call(tokens, embed_weight, embed_bias[None], own_in, mate_in)
     other = swap(sent)
     hidden = lax.all_to_all(hidden, ("zl", "y"), 0, 0)
     shares = mix_call(hidden, mlp_out, mate_out)

time: 238 us -> 153 us (0.64); the launches traced: 233 us -> 152 us
  Pallas kernels: 120 us -> 44.4 us
  blocking collectives: 26.1 us -> 64.9 us
  waiting for transfers between devices: 49.7 us -> 13.3 us
  starting transfers between devices: 18.4 us -> 13.7 us
  local copies, waits for them, and re-layouts: 17 us -> 13.8 us
    pallas_call x2, Pallas kernels: 81 us -> 10.1 us  [the longest x1 6.21 us: mix_call(): pl.pallas_call(mix_kernel, out_shape=jax.ShapeDtypeStruct((16, tokens //...]
    all_to_all x0 -> x1, blocking collectives: none -> 39.7 us  [on_device(): hidden = lax.all_to_all(hidden, ('zl', 'y'), 0, 0)]
    all_to_all x1 -> x0, waiting for transfers between devices: 30.7 us -> none  [on_device(): hidden = lax.all_to_all(hidden, ('zl', 'y'), 0, 0)]
    pallas_call x1, Pallas kernels: 18.3 us -> 13.4 us  [embed_call(): pl.pallas_call(functools.partial(embed_kernel, parts), out_shape=(jax.Sha...]
    all_to_all x1 -> x0, starting transfers between devices: 4.59 us -> none  [on_device(): hidden = lax.all_to_all(hidden, ('zl', 'y'), 0, 0)]
    ppermute x3, waiting for transfers between devices: 4.17 us -> 0.01 us  [swap(): return lax.ppermute(value, 'core', [(0, 1), (1, 0)])]
    unnamed x28 -> x24, local copies, waits for them, and re-layouts: 11.6 us -> 8.51 us
  transfers between devices with their start and end apart: 6 -> 5, of which waited for: 4 -> 1; matrix products, arithmetic and copies ran while one was open for 4% -> 6% of each run, Pallas kernels for 9% -> 16%
where the time goes in v2:
time: 153 us; the launch traced here: 152 us
  blocking collectives  64.9 us (42%)
  Pallas kernels  44.4 us (29%)
  local copies, waits for them, and re-layouts  13.8 us (9%)
  starting transfers between devices  13.7 us (9%)
  waiting for transfers between devices  13.3 us (9%)
    all_to_all x1, blocking collectives, on_device(): hidden = lax.all_to_all(hidden, ('zl', 'y'), 0, 0)  39.7 us
    all_to_all x1, blocking collectives, on_device(): lax.all_to_all(jnp.broadcast_to(patches[None], (64,) + patches.shape), ev...  25.2 us
    pallas_call x1, Pallas kernels, score_call(): pl.pallas_call(functools.partial(score_kernel, side, count), out_shape=ja...  20.8 us
    pallas_call x1, Pallas kernels, embed_call(): pl.pallas_call(functools.partial(embed_kernel, parts), out_shape=(jax.Sha...  13.4 us
    all_to_all x1, waiting for transfers between devices, on_device(): shares = lax.all_to_all(shares, ('zh', 'x', 'core'), 0, 0)  13.3 us
    unnamed x24, local copies, waits for them, and re-layouts  8.51 us
    pallas_call x1, Pallas kernels, mix_call(): pl.pallas_call(mix_kernel, out_shape=jax.ShapeDtypeStruct((16, tokens //...  6.21 us
    all_to_all x1, starting transfers between devices, on_device(): shares = lax.all_to_all(shares, ('zh', 'x', 'core'), 0, 0)  5.89 us
  transfers between devices with their start and end apart: 5, of which 1 were waited for; matrix products, arithmetic and copies ran while one was open for 6% of the time, Pallas kernels for 16%

profile of v2, /device:TPU:1, one launch (start us, length us, event | category | flops | bytes accessed | tf_op | source)
XLA Modules:
  0.0 151.8 jit_solution(3989390793069794234)
XLA Ops:
  0.6 1.5 collective-permute-start
  2.1 3.9 %split_columns.1 = bf16[8,384,384]{2,1,0:T(8,128)(2,1)} custom-call(bf16[384,3072]{1,0:T(8,128)(2,1)} %whole.1), custom_call_target="tpu_custom_call" | custom-call | bytes 4718592 | tf_op jit(solution)/shard_map/split_columns/pallas_call | solution.py:372
  6.1 5.8 %all-to-all-start.1 = ((bf16[8,384,384]{2,1,0:T(8,128)(2,1)}), bf16[8,384,384]{2,1,0:T(8,128)(2,1)S(1)}, u32[]{:S(2)}, u32[]{:S(2)}) async-start(bf16[8,384,384]{2,1,0:T(8,128)(2,1)} %split_columns.1), calls=%async_computation.1 | async-start | bytes 4718592 | tf_op jit(solution)/shard_map/all_to_all | solution.py:397
  11.8 1.4 copy.26.images
  13.3 1.4 copy.27.noise
  14.7 0.1 copy.28.out_w
  14.8 1.2 copy-done
  16.0 1.2 copy-done.1
  17.2 1.0 copy-done.3
  18.2 1.0 copy-done.4
  19.3 20.8 %score_net.1 = f32[2,28,28,3]{3,2,1,0:T(8,128)S(1)} custom-call(f32[2,28,28,3]{3,2,1,0:T(8,128)S(1)} %copy-done, f32[2,28,28,3]{3,2,1,0:T(8,128)S(1)} %copy-done.1, bf16[27,256]{1,0:T(8,128)(2,1)S(1)} %copy-done.6, bf16[4,2304,256]{2,1,0:T(8,128)(2,1)} %l1_hbm.1, bf16[1024,256]{1,0:T(8,128)(2,1)S(1)} %copy-done.3, bf16[2,2304,256]{2,1,0:T(8,128)(2,1)} %l2_hbm.1, ...), custom_call_target="tpu_custom_call" | custom-call | flops 10000000000 | bytes 12000000 | tf_op jit(solution)/shard_map/score_net/pallas_call | solution.py:186
  40.1 0.0 copy-start.5
  40.1 0.8 convert_element_type.23
  41.0 1.5 copy.29
  42.4 0.1 reshape.28
  42.5 1.6 %copy.30 = bf16[2,2,2,14,14,3]{5,4,3,2,1,0:T(8,128)(2,1)} copy(bf16[2,2,2,14,14,3]{4,2,0,5,3,1:T(2,128)(2,1)S(1)} %bitcast.16) | data formatting | bytes 18816 | tf_op jit(solution)/shard_map/transpose | solution.py:390
  44.1 1.5 reshape.29
  45.6 0.0 all-to-all-done.1.own_hbm
  45.6 0.4 collective-permute-start.1
  46.0 0.1 broadcast_in_dim.4
  46.0 25.2 %all_to_all.20 = bf16[64,8,640]{2,1,0:T(8,128)(2,1)S(1)} all-to-all(bf16[64,8,640]{2,1,0:T(8,128)(2,1)S(1)} %broadcast_in_dim.4), channel_id=1, replica_groups=mesh['zh'=2,'x'=4,'zl'=2,'y'=4,'core'=2] {'zh','x','zl','y'}, dimensions={0} | all-to-all | bytes 1310720 | tf_op jit(solution)/shard_map/all_to_all | solution.py:407
  71.2 13.4 %embed_mlp.1 = (bf16[8,512,384]{2,1,0:T(8,128)(2,1)S(1)}, bf16[64,384]{1,0:T(8,128)(2,1)S(1)}, bf16[64,384]{1,0:T(8,128)(2,1)S(1)}) custom-call(bf16[512,640]{1,0:T(8,128)(2,1)S(1)} %bitcast.12, bf16[588,6144]{1,0:T(8,128)(2,1)} %weight_hbm.1, f32[1,6144]{1,0:T(1,128)S(1)} %bitcast.14, bf16[8,384,384]{2,1,0:T(8,128)(2,1)S(1)} %all-to-all-done.1.own_hbm, ...), custom_call_target="tpu_custom_call" | custom-call | flops 7000000000 | bytes 20000000 | tf_op jit(solution)/shard_map/embed_mlp/pallas_call | solution.py:287
  84.6 0.0 copy-start.2
  84.6 39.7 %all_to_all.21.hidden_hbm = bf16[8,512,384]{2,1,0:T(8,128)(2,1)S(1)} all-to-all(bf16[8,512,384]{2,1,0:T(8,128)(2,1)S(1)} %get-tuple-element.8), channel_id=1, replica_groups=mesh['zh'=2,'x'=4,'zl'=2,'y'=4,'core'=2] {'zl','y'}, dimensions={0} | all-to-all | bytes 6291456 | tf_op jit(solution)/shard_map/all_to_all | solution.py:411
  124.3 6.2 %mlp_out.1 = bf16[16,64,384]{2,1,0:T(8,128)(2,1)} custom-call(bf16[8,512,384]{2,1,0:T(8,128)(2,1)S(1)} %all_to_all.21.hidden_hbm, bf16[3072,384]{1,0:T(8,128)(2,1)S(1)} %copy-done.2, bf16[3072,384]{1,0:T(8,128)(2,1)} %collective-permute-done.mate_hbm), custom_call_target="tpu_custom_call" | custom-call | flops 2400000000 | bytes 9000000 | tf_op jit(solution)/shard_map/mlp_out/pallas_call | solution.py:347
  130.5 5.9 %all-to-all-start.3 = ((bf16[16,64,384]{2,1,0:T(8,128)(2,1)}), bf16[16,64,384]{2,1,0:T(8,128)(2,1)S(1)}, u32[]{:S(2)}, u32[]{:S(2)}) async-start(bf16[16,64,384]{2,1,0:T(8,128)(2,1)} %mlp_out.1), calls=%async_computation.3 | async-start | bytes 1572864 | tf_op jit(solution)/shard_map/all_to_all | solution.py:413
  136.4 1.1 copy.32
  137.5 0.1 collective-permute-start.2
  137.6 13.3 %all-to-all-done.3 = bf16[16,64,384]{2,1,0:T(8,128)(2,1)S(1)} async-done(((bf16[16,64,384]{2,1,0:T(8,128)(2,1)}), bf16[16,64,384]{2,1,0:T(8,128)(2,1)S(1)}, u32[]{:S(2)}, u32[]{:S(2)}) %all-to-all-start.3) | async-done | bytes 786464 | tf_op jit(solution)/shard_map/all_to_all | solution.py:413
  151.0 0.1 convert_reduce_fusion
  151.1 0.0 collective-permute-done.2
  151.1 0.7 copy.31
  (18 shorter events, 0.1 us)
Async XLA Ops:
  0.6 45.0 %collective-permute-start = (bf16[3072,384]{1,0:T(8,128)(2,1)}, bf16[3072,384]{1,0:T(8,128)(2,1)}, u32[]{:S(2)}, u32[]{:S(2)}) collective-permute-start(bf16[3072,384]{1,0:T(8,128)(2,1)} %own_hbm.1), channel_id=1, source_target_pairs={{0,1},{1,0},{2,3},{3,2},{4,5},{5,4},{6,7},{7,6},{8,9},{9,8},{10,11... | collective-permute-start | bytes 7077896 | tf_op jit(solution)/shard_map/ppermute | solution.py:384
  6.1 5.8 %copy-start.7 = (f32[2,28,28,3]{2,0,3,1:T(2,128)S(1)}, f32[2,28,28,3]{2,0,3,1:T(2,128)}, u32[]{:S(2)}) copy-start(f32[2,28,28,3]{2,0,3,1:T(2,128)} %param.12) | copy-start | bytes 56452
  6.1 7.2 %copy-start.8 = (f32[2,28,28,3]{2,0,3,1:T(2,128)S(1)}, f32[2,28,28,3]{2,0,3,1:T(2,128)}, u32[]{:S(2)}) copy-start(f32[2,28,28,3]{2,0,3,1:T(2,128)} %param.13) | copy-start | bytes 56452
  6.1 8.6 %copy-start.9 = (bf16[256,3]{0,1:T(4,128)(2,1)S(1)}, bf16[256,3]{0,1:T(4,128)(2,1)}, u32[]{:S(2)}) copy-start(bf16[256,3]{0,1:T(4,128)(2,1)} %param.19) | copy-start | bytes 4612
  6.1 8.8 %copy-start.6 = (bf16[27,256]{1,0:T(8,128)(2,1)S(1)}, bf16[27,256]{1,0:T(8,128)(2,1)}, u32[]{:S(2)}) copy-start(bf16[27,256]{1,0:T(8,128)(2,1)} %stem_w.1) | copy-start | bytes 41476
  6.1 39.5 %all-to-all-start.1 = ((bf16[8,384,384]{2,1,0:T(8,128)(2,1)}), bf16[8,384,384]{2,1,0:T(8,128)(2,1)S(1)}, u32[]{:S(2)}, u32[]{:S(2)}) async-start(bf16[8,384,384]{2,1,0:T(8,128)(2,1)} %split_columns.1), calls=%async_computation.1 | async-start | bytes 4718592 | tf_op jit(solution)/shard_map/all_to_all | solution.py:397
  14.8 1.2 copy-start
  16.0 1.2 copy-start.1
  17.2 1.0 copy-start.3
  18.2 1.0 copy-start.4
  40.1 31.1 %copy-start.5 = (f32[6144]{0:T(1024)S(1)}, f32[6144]{0:T(1024)}, u32[]{:S(2)}) copy-start(f32[6144]{0:T(1024)} %param.21) | copy-start | bytes 73732
  45.6 25.6 %collective-permute-start.1 = (bf16[8,384,384]{2,1,0:T(8,128)(2,1)S(1)}, bf16[8,384,384]{2,1,0:T(8,128)(2,1)S(1)}, u32[]{:S(2)}, u32[]{:S(2)}) collective-permute-start(bf16[8,384,384]{2,1,0:T(8,128)(2,1)S(1)} %all-to-all-done.1.own_hbm), channel_id=1, source_target_pairs={{0,1},{1,0},{2,3},{3,2},{4,5},{5,4},{6,7},{7,6},{8,9},{9,8},{10,11... | collective-permute-start | bytes 7077896 | tf_op jit(solution)/shard_map/ppermute | solution.py:384
  84.6 39.7 %copy-start.2 = (bf16[3072,384]{1,0:T(8,128)(2,1)S(1)}, bf16[3072,384]{1,0:T(8,128)(2,1)}, u32[]{:S(2)}) copy-start(bf16[3072,384]{1,0:T(8,128)(2,1)} %own_hbm.1) | copy-start | bytes 7077892
  130.5 20.4 %all-to-all-start.3 = ((bf16[16,64,384]{2,1,0:T(8,128)(2,1)}), bf16[16,64,384]{2,1,0:T(8,128)(2,1)S(1)}, u32[]{:S(2)}, u32[]{:S(2)}) async-start(bf16[16,64,384]{2,1,0:T(8,128)(2,1)} %mlp_out.1), calls=%async_computation.3 | async-start | bytes 1572864 | tf_op jit(solution)/shard_map/all_to_all | solution.py:413
  137.5 13.6 %collective-permute-start.2 = (bf16[64,384]{1,0:T(8,128)(2,1)S(1)}, bf16[64,384]{1,0:T(8,128)(2,1)S(1)}, u32[]{:S(2)}, u32[]{:S(2)}) collective-permute-start(bf16[64,384]{1,0:T(8,128)(2,1)S(1)} %get-tuple-element.11), channel_id=1, source_target_pairs={{0,1},{1,0},{2,3},{3,2},{4,5},{5,4},{6,7},{7,6},{8,9},{9,8},{10,11... | collective-permute-start | bytes 147464 | tf_op jit(solution)/shard_map/ppermute | solution.py:384

commit v3 on v2

--- a/solution.py
+++ b/solution.py
@@ -24,7 +24,7 @@
 
 
 def score_kernel(side, count, images, noise, stem_w, l1_hbm, down_hbm, l2_hbm, up_hbm, out_w,
-                 purified, pix, stem_x, stem_k, out_k, xa, xb, ca, cb, stream, coarse,
+                 purified, patches, raw, extra, pix, stem_x, stem_k, out_k, xa, xb, ca, cb, stream, coarse,
                  l1, down, l2, up, sems):
     half = side // 2
     span1, span2 = side * W1, half * W2
@@ -39,9 +39,7 @@
     for load in loads:
         load.start()
 
-    chunk = span1 // 2
-    per_image = 2
-    mask1 = (lax.broadcasted_iota(jnp.int32, (chunk, 1), 0) % W1) < side
+    mask1 = (lax.broadcasted_iota(jnp.int32, (span1, 1), 0) % W1) < side
     mask2 = (lax.broadcasted_iota(jnp.int32, (span2, 1), 0) % W2) < half
 
     def read(rows):
@@ -58,67 +56,68 @@
         xb[i * pitch1:i * pitch1 + W1, :] = z1
         ca[i * pitch2:i * pitch2 + W2, :] = z2
         cb[i * pitch2:i * pitch2 + W2, :] = z2
-        stem_x[i * pitch1:i * pitch1 + W1, :] = jnp.zeros((W1, 128), bf16)
-    pix[...] = jnp.zeros_like(pix)
+    raw[...] = jnp.zeros_like(raw)
+    extra[...] = jnp.zeros_like(extra)
     stem_k[...] = jnp.zeros_like(stem_k)
-    out_k[...] = jnp.zeros_like(out_k)
+    stem = stem_w[...].astype(f32)
     for dy in range(3):
-        stem_k[dy, 0:9, :] = stem_w[9 * dy:9 * dy + 9, :].astype(f32)
-    out_k[:, 0:3] = out_w[...].astype(f32)
-
-    for i in range(count):
-        def put(y, _, i=i):
-            base = pl.multiple_of(W1 + i * pitch1 + y * W1, W1)
-            pix[pl.ds(base, side), 0:3] = images[i, y].astype(bf16).astype(f32)
+        for dx in range(3):
+            for c in range(3):
+                k = (3 * dy + dx) * 3 + c
+                at = 128 * dx + W1 * c + dy
+                stem_k[at:at + 1, :] = stem[k:k + 1, :]
+    column = lax.broadcasted_iota(jnp.int32, (8, 128), 1)
+    colour = lax.broadcasted_iota(jnp.int32, (8, 128), 0)
+    place = ((column == W1 * colour) & (colour < 3)).astype(bf16)
+    out_k[...] = jnp.dot(out_w[...], place[0:3, :], preferred_element_type=f32).astype(bf16)
+
+    for y in range(side):
+        for c in range(3):
+            at = W1 * c + y
+            v, n = images[y, c], noise[y, c]
+            for i in range(count):
+                raw[i, at:at + 1, 0:side] = v[i:i + 1, :]
+                extra[i, at:at + 1, 0:side] = n[i:i + 1, :]
+
+    def shifted(ref, base, value):
+        n, wide = value.shape
+        ref[pl.ds(base, n), 0:wide] = pltpu.roll(value, 1, 0).astype(bf16)
+        ref[pl.ds(base, n), wide:2 * wide] = value.astype(bf16)
+        ref[pl.ds(base, n), 2 * wide:3 * wide] = pltpu.roll(value, n - 1, 0).astype(bf16)
+
+    def each(body):
+        def step(i, _):
+            body(i, pl.multiple_of(W1 + i * pitch1, W1))
             return 0
-        lax.fori_loop(0, side, put, 0)
-
-    def shifted(ref, base, value):
-        n = value.shape[0]
-        ref[pl.ds(base, n), 0:CH] = pltpu.roll(value, 1, 0).astype(bf16)
-        ref[pl.ds(base, n), CH:2 * CH] = value.astype(bf16)
-        ref[pl.ds(base, n), 2 * CH:3 * CH] = pltpu.roll(value, n - 1, 0).astype(bf16)
-
-    def each(body):
-        def step(t, _):
-            base = W1 + (t // per_image) * pitch1 + (t % per_image) * chunk
-            body(t, pl.multiple_of(base, W1))
-            return 0
-        lax.fori_loop(0, count * per_image, step, 0)
+        lax.fori_loop(0, count, step, 0)
 
     def conv(ref, base, n, width, weights):
-        acc = jnp.dot(ref[pl.ds(base - width, n), :], weights[0:3 * CH, :], preferred_element_type=f32)
-        acc += jnp.dot(ref[pl.ds(base, n), :], weights[3 * CH:6 * CH, :], preferred_element_type=f32)
-        acc += jnp.dot(ref[pl.ds(base + width, n), :], weights[6 * CH:9 * CH, :], preferred_element_type=f32)
-        return acc
-
-    def stem_cols(t, base):
-        v = pix[pl.ds(base, chunk), :]
-        left = pltpu.roll(v, 1, 0)
-        right = pltpu.roll(v, chunk - 1, 0)
-        stem_x[pl.ds(base, chunk), :] = (left + pltpu.roll(v, 3, 1) + pltpu.roll(right, 6, 1)).astype(bf16)
-    each(stem_cols)
-
-    def stem_conv(t, base):
-        acc = jnp.dot(stem_x[pl.ds(base - W1, chunk), :], stem_k[0].astype(bf16), preferred_element_type=f32)
-        acc += jnp.dot(stem_x[pl.ds(base, chunk), :], stem_k[1].astype(bf16), preferred_element_type=f32)
-        acc += jnp.dot(stem_x[pl.ds(base + W1, chunk), :], stem_k[2].astype(bf16), preferred_element_type=f32)
-        write(pl.ds(base, chunk), acc)
+        near = jnp.concatenate([ref[pl.ds(base - width, n), :], ref[pl.ds(base, n), :],
+                                ref[pl.ds(base + width, n), :]], axis=1)
+        return jnp.dot(near, weights[...], preferred_element_type=f32)
+
+    def begin(i, base):
+        across = jnp.transpose(raw[i].astype(bf16).astype(f32))[0:W1, :]
+        for y in range(side):
+            pix[y * W1:(y + 1) * W1, :] = pltpu.roll(across, (1 - y) % 128, 1)
+        shifted(stem_x, 0, pix[...])
+        acc = jnp.dot(stem_x[...], stem_k[...].astype(bf16), preferred_element_type=f32)
+        write(pl.ds(base, span1), acc)
         shifted(xa, base, jnp.where(mask1, gelu(acc), 0.0))
-    each(stem_conv)
+    each(begin)
 
     loads[0].wait()
 
-    def layer0(t, base):
-        s = read(pl.ds(base, chunk)) + conv(xa, base, chunk, W1, l1.at[0])
-        write(pl.ds(base, chunk), s)
+    def layer0(i, base):
+        s = read(pl.ds(base, span1)) + conv(xa, base, span1, W1, l1.at[0])
+        write(pl.ds(base, span1), s)
         shifted(xb, base, jnp.where(mask1, gelu(s), 0.0))
     each(layer0)
 
     loads[1].wait()
 
-    def layer1(t, base):
-        write(pl.ds(base, chunk), read(pl.ds(base, chunk)) + conv(xb, base, chunk, W1, l1.at[1]))
+    def layer1(i, base):
+        write(pl.ds(base, span1), read(pl.ds(base, span1)) + conv(xb, base, span1, W1, l1.at[1]))
     each(layer1)
 
     loads[2].wait()
@@ -126,13 +125,9 @@
     loads[4].wait()
     for i in range(count):
         base1, base2 = W1 + i * pitch1, W2 + i * pitch2
-        acc = None
-        for b in range(2):
-            cols = read(pl.ds(base1 + b, span1 // 2, stride=2)).astype(bf16).reshape(half, 2, W2, CH)
-            for a in range(2):
-                part = jnp.dot(cols[:, a].reshape(span2, CH), down[(2 * a + b) * CH:(2 * a + b + 1) * CH, :],
-                               preferred_element_type=f32)
-                acc = part if acc is None else acc + part
+        cols = [read(pl.ds(base1 + b, span1 // 2, stride=2)).astype(bf16).reshape(half, 2, W2, CH) for b in range(2)]
+        cells = jnp.concatenate([cols[b][:, a].reshape(span2, CH) for a in range(2) for b in range(2)], axis=1)
+        acc = jnp.dot(cells, down[...], preferred_element_type=f32)
         coarse[base2:base2 + span2, :] = acc
         shifted(ca, base2, jnp.where(mask2, gelu(acc), 0.0))
     for i in range(count):
@@ -152,47 +147,86 @@
                     rows = pl.ds(base1 + (2 * y + a) * W1 + b, W2, stride=2)
                     write(rows, read(rows) + part[y * W2:(y + 1) * W2, :])
 
-    def enter(t, base):
-        shifted(xa, base, jnp.where(mask1, gelu(read(pl.ds(base, chunk))), 0.0))
+    def enter(i, base):
+        shifted(xa, base, jnp.where(mask1, gelu(read(pl.ds(base, span1))), 0.0))
     each(enter)
 
     loads[5].wait()
 
-    def layer2(t, base):
-        s = read(pl.ds(base, chunk)) + conv(xa, base, chunk, W1, l1.at[2])
-        write(pl.ds(base, chunk), s)
+    def layer2(i, base):
+        s = read(pl.ds(base, span1)) + conv(xa, base, span1, W1, l1.at[2])
+        write(pl.ds(base, span1), s)
         shifted(xb, base, jnp.where(mask1, gelu(s), 0.0))
     each(layer2)
 
     loads[6].wait()
-    lines = chunk // W1
-
-    def layer3(t, base):
-        s = read(pl.ds(base, chunk)) + conv(xb, base, chunk, W1, l1.at[3])
-        score = jnp.dot(gelu(s).astype(bf16), out_k[...].astype(bf16), preferred_element_type=f32)
-        i, y0 = t // per_image, (t % per_image) * lines
-        for y in range(lines):
-            purified[i, y0 + y] = (images[i, y0 + y] + step_size * score[y * W1:y * W1 + side, 0:3]
-                                   + noise_gain * noise[i, y0 + y])
+
+    def layer3(i, base):
+        s = read(pl.ds(base, span1)) + conv(xb, base, span1, W1, l1.at[3])
+        score = jnp.dot(gelu(s).astype(bf16), out_k[...], preferred_element_type=f32)
+        across = score[0:W1, :]
+        for y in range(1, side):
+            across += pltpu.roll(score[y * W1:(y + 1) * W1, :], y, 1)
+        across = jnp.concatenate([across, jnp.zeros((128 - W1, 128), f32)], axis=0)
+        raw[i] = raw[i] + step_size * jnp.transpose(across) + noise_gain * extra[i]
     each(layer3)
 
-
-def score_call(images, noise, stem_w, l1, down, l2, up, out_w):
+    for y in range(side):
+        for c in range(3):
+            at = W1 * c + y
+            purified[y, c] = jnp.concatenate([raw[i, at:at + 1, 0:side] for i in range(count)], axis=0)
+
+    lane = lax.broadcasted_iota(jnp.int32, (128, 128), 1)
+    line = lax.broadcasted_iota(jnp.int32, (128, 128), 0)
+    wide = []
+    for i in range(count):
+        rows = None
+        for c in range(3):
+            spread = ((lane == 3 * line + c) & (line < side)).astype(bf16)
+            part = jnp.dot(raw[i, W1 * c:W1 * (c + 1), :].astype(bf16), spread, preferred_element_type=f32)
+            rows = part if rows is None else rows + part
+        wide.append(rows)
+    wide = jnp.concatenate(wide, axis=0).astype(bf16)
+    many, run = 4 * count, 3 * PATCH
+    token = lax.broadcasted_iota(jnp.int32, (many, count * W1), 0)
+    source = lax.broadcasted_iota(jnp.int32, (many, count * W1), 1)
+    first = (token // 4) * W1 + ((token // 2) % 2) * PATCH
+    lanes = lax.broadcasted_iota(jnp.int32, (many, 128), 1)
+    second = (lax.broadcasted_iota(jnp.int32, (many, 128), 0) % 2) == 1
+    pieces = [jnp.zeros((many, 128), f32) for _ in range(5)]
+    for r in range(PATCH):
+        z = jnp.dot((source == first + r).astype(bf16), wide, preferred_element_type=f32)
+        z = jnp.where(second, pltpu.roll(z, 128 - run, 1), z)
+        z = jnp.where(lanes < run, z, 0.0)
+        k, at = (run * r) // 128, (run * r) % 128
+        z = pltpu.roll(z, at, 1) if at else z
+        pieces[k] += jnp.where(lanes >= at, z, 0.0)
+        if at + run > 128:
+            pieces[k + 1] += jnp.where(lanes < at, z, 0.0)
+    tokens = jnp.concatenate(pieces, axis=1).astype(bf16)
+    for k in range(patches.shape[0]):
+        patches[k] = tokens
+
+
+def score_call(images, noise, stem_w, l1, down, l2, up, out_w, copies):
     count, side = images.shape[0], images.shape[1]
     rows1 = W1 + count * (side + 1) * W1
     rows2 = W2 + count * (side // 2 + 1) * W2
+    images, noise = images.transpose(1, 3, 0, 2), noise.transpose(1, 3, 0, 2)
     vm = pl.BlockSpec(memory_space=pltpu.VMEM)
-    hb = pl.BlockSpec(memory_space=pl.ANY)
-    return pl.pallas_call(
+    hb = pl.BlockSpec(memory_space=pltpu.HBM)
+    purified, patches = pl.pallas_call(
         functools.partial(score_kernel, side, count),
-        out_shape=jax.ShapeDtypeStruct(images.shape, f32),
+        out_shape=(jax.ShapeDtypeStruct(images.shape, f32), jax.ShapeDtypeStruct((copies, 4 * count, 640), bf16)),
         in_specs=[vm, vm, vm, hb, hb, hb, hb, vm],
-        out_specs=vm,
+        out_specs=(vm, vm),
         scratch_shapes=[
-            pltpu.VMEM((rows1, 128), f32),
-            pltpu.VMEM((rows1, 128), bf16),
-            pltpu.VMEM((3, 128, CH), f32),
-            pltpu.VMEM((CH, 128), f32),
+            pltpu.VMEM((count, 128, 128), f32),
+            pltpu.VMEM((count, 128, 128), f32),
+            pltpu.VMEM((side * W1, 128), f32),
+            pltpu.VMEM((side * W1, 3 * 128), bf16),
+            pltpu.VMEM((3 * 128, CH), f32),
+            pltpu.VMEM((CH, 128), bf16),
             pltpu.VMEM((rows1, 3 * CH), bf16),
             pltpu.VMEM((rows1, 3 * CH), bf16),
             pltpu.VMEM((rows2, 3 * CH), bf16),
@@ -205,10 +239,11 @@
             pltpu.VMEM(up.shape, bf16),
             pltpu.SemaphoreType.DMA((7,)),
         ],
-        compiler_params=pltpu.CompilerParams(vmem_limit_bytes=48 << 20),
+        compiler_params=pltpu.CompilerParams(vmem_limit_bytes=58 << 20),
         cost_estimate=pl.CostEstimate(flops=10_000_000_000, transcendentals=3_000_000, bytes_accessed=12_000_000),
         name="score_net",
     )(images, noise, stem_w, l1, down, l2, up, out_w)
+    return purified.transpose(2, 0, 3, 1), patches
 
 
 def embed_kernel(parts, patches, weight_hbm, bias, own_hbm, mate_hbm, hidden, kept, sent,
@@ -283,7 +318,7 @@
     parts = 4
     share = tokens // 8
     vm = pl.BlockSpec(memory_space=pltpu.VMEM)
-    hb = pl.BlockSpec(memory_space=pl.ANY)
+    hb = pl.BlockSpec(memory_space=pltpu.HBM)
     return pl.pallas_call(
         functools.partial(embed_kernel, parts),
         out_shape=(jax.ShapeDtypeStruct((8, tokens, width), bf16),
@@ -301,7 +336,7 @@
             pltpu.SemaphoreType.DMA((8,)),
             pltpu.SemaphoreType.DMA((8,)),
         ],
-        compiler_params=pltpu.CompilerParams(vmem_limit_bytes=40 << 20),
+        compiler_params=pltpu.CompilerParams(vmem_limit_bytes=58 << 20),
         cost_estimate=pl.CostEstimate(flops=7_000_000_000, transcendentals=200_000, bytes_accessed=20_000_000),
         name="embed_mlp",
     )(patches, weight, bias, own, mate)
@@ -343,7 +378,7 @@
 def mix_call(hidden, own, mate):
     blocks, tokens, width = hidden.shape
     depth, span = own.shape
-    hb = pl.BlockSpec(memory_space=pl.ANY)
+    hb = pl.BlockSpec(memory_space=pltpu.HBM)
     return pl.pallas_call(
         mix_kernel,
         out_shape=jax.ShapeDtypeStruct((16, tokens // 8, span), bf16),
@@ -355,26 +390,31 @@
             pltpu.VMEM((tokens, 2 * span), f32),
             pltpu.SemaphoreType.DMA((blocks // 2, 4)),
         ],
-        compiler_params=pltpu.CompilerParams(vmem_limit_bytes=24 << 20),
+        compiler_params=pltpu.CompilerParams(vmem_limit_bytes=58 << 20),
         cost_estimate=pl.CostEstimate(flops=2_400_000_000, transcendentals=0, bytes_accessed=9_000_000),
         name="mlp_out",
     )(hidden, own, mate)
 
 
-def split_kernel(whole, blocks):
+def split_kernel(whole, blocks, sems):
     width = blocks.shape[2]
-    for b in range(blocks.shape[0]):
-        blocks[b] = whole[:, b * width:(b + 1) * width]
+    loads = [pltpu.make_async_copy(whole.at[:, pl.ds(b * width, width)], blocks.at[b], sems.at[b])
+             for b in range(blocks.shape[0])]
+    for load in loads:
+        load.start()
+    for load in loads:
+        load.wait()
 
 
 def split_call(whole, count):
     depth, width = whole.shape[0], whole.shape[1] // count
     return pl.pallas_call(
         split_kernel,
-        grid=(count // 2,),
         out_shape=jax.ShapeDtypeStruct((count, depth, width), whole.dtype),
-        in_specs=[pl.BlockSpec((depth, 2 * width), lambda b: (0, b))],
-        out_specs=pl.BlockSpec((2, depth, width), lambda b: (b, 0, 0)),
+        in_specs=[pl.BlockSpec(memory_space=pltpu.HBM)],
+        out_specs=pl.BlockSpec(memory_space=pltpu.VMEM),
+        scratch_shapes=[pltpu.SemaphoreType.DMA((count,))],
+        compiler_params=pltpu.CompilerParams(vmem_limit_bytes=58 << 20),
         cost_estimate=pl.CostEstimate(flops=0, transcendentals=0, bytes_accessed=2 * whole.size * 2),
         name="split_columns",
     )(whole)
@@ -382,13 +422,6 @@
 
 def swap(value):
     return lax.ppermute(value, "core", [(0, 1), (1, 0)])
-
-
-def patchify(pixels):
-    count, side = pixels.shape[0], pixels.shape[1]
-    grid = side // PATCH
-    blocks = pixels.reshape(count, grid, PATCH, grid, PATCH, 3).transpose(0, 1, 3, 2, 4, 5)
-    return blocks.reshape(count * grid * grid, PATCH * PATCH * 3)
 
 
 def on_device(images, noise_field, stem_weight, level_one, down_weight, level_two, up_weight,
@@ -397,14 +430,11 @@
     own_in = lax.all_to_all(split_call(mlp_in, 8), ("zl", "y"), 0, 0)
     mate_out = swap(mlp_out)
 
-    purified = score_call(images, noise_field, stem_weight, level_one, down_weight, level_two,
-                          up_weight, out_weight)
-    patches = patchify(purified.astype(bf16))
-    patches = jnp.pad(patches, ((0, 0), (0, 640 - patches.shape[1])))
-    own_in, mate_out, _ = lax.optimization_barrier((own_in, mate_out, patches))
+    purified, patches = score_call(images, noise_field, stem_weight, level_one, down_weight, level_two,
+                                   up_weight, out_weight, 64)
+    own_in, mate_out, _ = lax.optimization_barrier((own_in, mate_out, purified))
     mate_in = swap(own_in)
-    every = ("zh", "x", "zl", "y")
-    tokens = lax.all_to_all(jnp.broadcast_to(patches[None], (64,) + patches.shape), every, 0, 0)
+    tokens = lax.all_to_all(patches, ("zh", "x", "zl", "y"), 0, 0)
     tokens = tokens.reshape(-1, tokens.shape[-1])
     hidden, kept, sent = embed_call(tokens, embed_weight, embed_bias[None], own_in, mate_in)
     other = swap(sent)

time: 153 us -> 159 us (1.039)
  local copies, waits for them, and re-layouts: 13.8 us -> 2.93 us
  waiting for transfers between devices: 13.3 us -> 23.1 us
  blocking collectives: 64.9 us -> 70.3 us
  Pallas kernels: 44.4 us -> 47.2 us
    all_to_all x1, waiting for transfers between devices: 0.01 us -> 8.8 us  [on_device(): own_in = lax.all_to_all(split_call(mlp_in, 8), ('zl', 'y'), 0, 0)]
    unnamed x24 -> x11, local copies, waits for them, and re-layouts: 8.51 us -> 2.28 us
    all_to_all x1, blocking collectives: 25.2 us -> 28.9 us  [on_device(): tokens = lax.all_to_all(patches, ('zh', 'x', 'zl', 'y'), 0, 0)]
    pallas_call x1, Pallas kernels: 13.4 us -> 17.2 us  [embed_call(): pl.pallas_call(functools.partial(embed_kernel, parts), out_shape=(jax.Sha...]
    all_to_all x1, blocking collectives: 39.7 us -> 41.4 us  [on_device(): hidden = lax.all_to_all(hidden, ('zl', 'y'), 0, 0)]
  transfers between devices with their start and end apart: 5 -> 5, of which waited for: 1 -> 2; matrix products, arithmetic and copies ran while one was open for 6% -> 1% of each run, Pallas kernels for 16% -> 15%
where the time goes in v3:
time: 159 us; the launch traced here: 158 us
  blocking collectives  70.3 us (44%)
  Pallas kernels  47.2 us (30%)
  waiting for transfers between devices  23.1 us (15%)
  starting transfers between devices  14 us (9%)
  local copies, waits for them, and re-layouts  2.93 us (2%)
    all_to_all x1, blocking collectives, on_device(): hidden = lax.all_to_all(hidden, ('zl', 'y'), 0, 0)  41.4 us
    all_to_all x1, blocking collectives, on_device(): tokens = lax.all_to_all(patches, ('zh', 'x', 'zl', 'y'), 0, 0)  28.9 us
    pallas_call x1, Pallas kernels, score_call(): pl.pallas_call(functools.partial(score_kernel, side, count), out_shape=(j...  20.4 us
    pallas_call x1, Pallas kernels, embed_call(): pl.pallas_call(functools.partial(embed_kernel, parts), out_shape=(jax.Sha...  17.2 us
    all_to_all x1, waiting for transfers between devices, on_device(): shares = lax.all_to_all(shares, ('zh', 'x', 'core'), 0, 0)  14.3 us
    all_to_all x1, waiting for transfers between devices, on_device(): own_in = lax.all_to_all(split_call(mlp_in, 8), ('zl', 'y'), 0, 0)  8.8 us
    pallas_call x1, Pallas kernels, mix_call(): pl.pallas_call(mix_kernel, out_shape=jax.ShapeDtypeStruct((16, tokens //...  6.55 us
    all_to_all x1, starting transfers between devices, on_device(): shares = lax.all_to_all(shares, ('zh', 'x', 'core'), 0, 0)  5.75 us
  transfers between devices with their start and end apart: 5, of which 2 were waited for; matrix products, arithmetic and copies ran while one was open for 1% of the time, Pallas kernels for 15%

profile of v3, /device:TPU:1, one launch (start us, length us, event | category | flops | bytes accessed | tf_op | source)
XLA Modules:
  0.0 158.4 jit_solution(2113831280709993296)
XLA Ops:
  0.6 1.5 collective-permute-start
  2.1 3.1 %split_columns.1 = bf16[8,384,384]{2,1,0:T(8,128)(2,1)} custom-call(bf16[384,3072]{1,0:T(8,128)(2,1)} %whole.1), custom_call_target="tpu_custom_call" | custom-call | bytes 4718592 | tf_op jit(solution)/shard_map/split_columns/pallas_call | solution.py:411
  5.3 0.0 copy-start.2
  5.3 5.6 %all-to-all-start.1 = ((bf16[8,384,384]{2,1,0:T(8,128)(2,1)}), bf16[8,384,384]{2,1,0:T(8,128)(2,1)S(1)}, u32[]{:S(2)}, u32[]{:S(2)}) async-start(bf16[8,384,384]{2,1,0:T(8,128)(2,1)} %split_columns.1), calls=%async_computation.1 | async-start | bytes 4718592 | tf_op jit(solution)/shard_map/all_to_all | solution.py:430
  10.9 0.0 copy-done.2
  10.9 0.8 copy.14.out_w
  11.7 20.4 %score_net.1 = (f32[28,3,2,28]{3,2,1,0:T(2,128)}, bf16[64,8,640]{2,1,0:T(8,128)(2,1)}) custom-call(f32[28,3,2,28]{3,2,1,0:T(2,128)} %bitcast.17, f32[28,3,2,28]{3,2,1,0:T(2,128)} %bitcast.18, bf16[27,256]{1,0:T(8,128)(2,1)} %stem_w.1, bf16[4,2304,256]{2,1,0:T(8,128)(2,1)} %l1_hbm.1, bf16[1024,256]{1,0:T(8,128)(2,1)} %down_hbm.1, ...), custom_call_target="tpu_custom_call" | custom-call | flops 10000000000 | bytes 12000000 | tf_op jit(solution)/shard_map/score_net/pallas_call | solution.py:218
  32.0 8.8 %all-to-all-done.1.own_hbm = bf16[8,384,384]{2,1,0:T(8,128)(2,1)S(1)} async-done(((bf16[8,384,384]{2,1,0:T(8,128)(2,1)}), bf16[8,384,384]{2,1,0:T(8,128)(2,1)S(1)}, u32[]{:S(2)}, u32[]{:S(2)}) %all-to-all-start.1) | async-done | bytes 2359328 | tf_op jit(solution)/shard_map/all_to_all | solution.py:430
  40.9 0.0 copy-start
  40.9 0.0 collective-permute-done.mate_hbm
  40.9 0.8 collective-permute-start.1
  41.6 28.9 %all_to_all.20 = bf16[64,8,640]{2,1,0:T(8,128)(2,1)} all-to-all(bf16[64,8,640]{2,1,0:T(8,128)(2,1)} %get-tuple-element.10), channel_id=1, replica_groups=mesh['zh'=2,'x'=4,'zl'=2,'y'=4,'core'=2] {'zh','x','zl','y'}, dimensions={0} | all-to-all | bytes 1310720 | tf_op jit(solution)/shard_map/all_to_all | solution.py:437
  70.6 0.0 collective-permute-done.1.mate_hbm
  70.6 0.0 copy-start.3
  70.6 0.0 copy-done
  70.6 1.5 copy-done.3
  72.1 17.2 %embed_mlp.1 = (bf16[8,512,384]{2,1,0:T(8,128)(2,1)}, bf16[64,384]{1,0:T(8,128)(2,1)}, bf16[64,384]{1,0:T(8,128)(2,1)}) custom-call(bf16[512,640]{1,0:T(8,128)(2,1)} %bitcast.13, bf16[588,6144]{1,0:T(8,128)(2,1)} %weight_hbm.1, f32[1,6144]{1,0:T(1,128)} %bitcast.19, bf16[8,384,384]{2,1,0:T(8,128)(2,1)} %copy-done, bf16[8,384,384]{2,1,0:T(8,128)(2,1)} %copy-done.3), custom_call_target="tpu_custom_call" | custom-call | flops 7000000000 | bytes 20000000 | tf_op jit(solution)/shard_map/embed_mlp/pallas_call | solution.py:322
  89.2 41.4 %all_to_all.21.hidden_hbm = bf16[8,512,384]{2,1,0:T(8,128)(2,1)} all-to-all(bf16[8,512,384]{2,1,0:T(8,128)(2,1)} %get-tuple-element.12), channel_id=1, replica_groups=mesh['zh'=2,'x'=4,'zl'=2,'y'=4,'core'=2] {'zl','y'}, dimensions={0} | all-to-all | bytes 6291456 | tf_op jit(solution)/shard_map/all_to_all | solution.py:441
  130.6 0.0 copy-start.4
  130.6 6.5 %mlp_out.1 = bf16[16,64,384]{2,1,0:T(8,128)(2,1)} custom-call(bf16[8,512,384]{2,1,0:T(8,128)(2,1)} %all_to_all.21.hidden_hbm, bf16[3072,384]{1,0:T(8,128)(2,1)} %own_hbm.1, bf16[3072,384]{1,0:T(8,128)(2,1)} %collective-permute-done.mate_hbm), custom_call_target="tpu_custom_call" | custom-call | flops 2400000000 | bytes 9000000 | tf_op jit(solution)/shard_map/mlp_out/pallas_call | solution.py:382
  137.1 0.0 copy-start.1
  137.2 5.8 %all-to-all-start.3 = ((bf16[16,64,384]{2,1,0:T(8,128)(2,1)}), bf16[16,64,384]{2,1,0:T(8,128)(2,1)S(1)}, u32[]{:S(2)}, u32[]{:S(2)}) async-start(bf16[16,64,384]{2,1,0:T(8,128)(2,1)} %mlp_out.1), calls=%async_computation.3 | async-start | bytes 1572864 | tf_op jit(solution)/shard_map/all_to_all | solution.py:443
  142.9 0.0 copy-done.4
  142.9 0.3 collective-permute-start.2
  143.2 14.3 %all-to-all-done.3 = bf16[16,64,384]{2,1,0:T(8,128)(2,1)S(1)} async-done(((bf16[16,64,384]{2,1,0:T(8,128)(2,1)}), bf16[16,64,384]{2,1,0:T(8,128)(2,1)S(1)}, u32[]{:S(2)}, u32[]{:S(2)}) %all-to-all-start.3) | async-done | bytes 786464 | tf_op jit(solution)/shard_map/all_to_all | solution.py:443
  157.5 0.1 convert_reduce_fusion
  157.6 0.0 collective-permute-done.2
  157.7 0.0 copy-done.1
  157.7 0.7 copy.15
  (1 shorter events, 0.0 us)
Async XLA Ops:
  0.6 40.2 %collective-permute-start = (bf16[3072,384]{1,0:T(8,128)(2,1)}, bf16[3072,384]{1,0:T(8,128)(2,1)}, u32[]{:S(2)}, u32[]{:S(2)}) collective-permute-start(bf16[3072,384]{1,0:T(8,128)(2,1)} %own_hbm.1), channel_id=1, source_target_pairs={{0,1},{1,0},{2,3},{3,2},{4,5},{5,4},{6,7},{7,6},{8,9},{9,8},{10,11... | collective-permute-start | bytes 7077896 | tf_op jit(solution)/shard_map/ppermute | solution.py:424
  5.3 5.7 %copy-start.2 = (bf16[256,3]{0,1:T(4,128)(2,1)S(1)}, bf16[256,3]{0,1:T(4,128)(2,1)}, u32[]{:S(2)}) copy-start(bf16[256,3]{0,1:T(4,128)(2,1)} %param.19) | copy-start | bytes 4612
  5.3 35.6 %all-to-all-start.1 = ((bf16[8,384,384]{2,1,0:T(8,128)(2,1)}), bf16[8,384,384]{2,1,0:T(8,128)(2,1)S(1)}, u32[]{:S(2)}, u32[]{:S(2)}) async-start(bf16[8,384,384]{2,1,0:T(8,128)(2,1)} %split_columns.1), calls=%async_computation.1 | async-start | bytes 4718592 | tf_op jit(solution)/shard_map/all_to_all | solution.py:430
  40.9 29.7 %copy-start = (bf16[8,384,384]{2,1,0:T(8,128)(2,1)}, bf16[8,384,384]{2,1,0:T(8,128)(2,1)S(1)}, u32[]{:S(2)}) copy-start(bf16[8,384,384]{2,1,0:T(8,128)(2,1)S(1)} %all-to-all-done.1.own_hbm) | copy-start | bytes 7077892
  40.9 29.7 %collective-permute-start.1 = (bf16[8,384,384]{2,1,0:T(8,128)(2,1)S(1)}, bf16[8,384,384]{2,1,0:T(8,128)(2,1)S(1)}, u32[]{:S(2)}, u32[]{:S(2)}) collective-permute-start(bf16[8,384,384]{2,1,0:T(8,128)(2,1)S(1)} %all-to-all-done.1.own_hbm), channel_id=1, source_target_pairs={{0,1},{1,0},{2,3},{3,2},{4,5},{5,4},{6,7},{7,6},{8,9},{9,8},{10,11... | collective-permute-start | bytes 7077896 | tf_op jit(solution)/shard_map/ppermute | solution.py:424
  70.6 1.5 copy-start.3
  130.6 12.3 %copy-start.4 = (bf16[64,384]{1,0:T(8,128)(2,1)S(1)}, bf16[64,384]{1,0:T(8,128)(2,1)}, u32[]{:S(2)}) copy-start(bf16[64,384]{1,0:T(8,128)(2,1)} %get-tuple-element.15) | copy-start | bytes 147460
  137.1 20.5 %copy-start.1 = (bf16[64,384]{1,0:T(8,128)(2,1)S(1)}, bf16[64,384]{1,0:T(8,128)(2,1)}, u32[]{:S(2)}) copy-start(bf16[64,384]{1,0:T(8,128)(2,1)} %get-tuple-element.14) | copy-start | bytes 147460
  137.2 20.4 %all-to-all-start.3 = ((bf16[16,64,384]{2,1,0:T(8,128)(2,1)}), bf16[16,64,384]{2,1,0:T(8,128)(2,1)S(1)}, u32[]{:S(2)}, u32[]{:S(2)}) async-start(bf16[16,64,384]{2,1,0:T(8,128)(2,1)} %mlp_out.1), calls=%async_computation.3 | async-start | bytes 1572864 | tf_op jit(solution)/shard_map/all_to_all | solution.py:443
  142.9 14.7 %collective-permute-start.2 = (bf16[64,384]{1,0:T(8,128)(2,1)S(1)}, bf16[64,384]{1,0:T(8,128)(2,1)S(1)}, u32[]{:S(2)}, u32[]{:S(2)}) collective-permute-start(bf16[64,384]{1,0:T(8,128)(2,1)S(1)} %copy-done.4), channel_id=1, source_target_pairs={{0,1},{1,0},{2,3},{3,2},{4,5},{5,4},{6,7},{7,6},{8,9},{9,8},{10,11... | collective-permute-start | bytes 147464 | tf_op jit(solution)/shard_map/ppermute | solution.py:424

commit v4 on v3

--- a/solution.py
+++ b/solution.py
@@ -246,100 +246,97 @@
     return purified.transpose(2, 0, 3, 1), patches
 
 
-def embed_kernel(parts, patches, weight_hbm, bias, own_hbm, mate_hbm, hidden, kept, sent,
-                 weight, mixer, total, sums, squares, sems, own_sems, mate_sems):
+def embed_kernel(flip, patches, weight_hbm, bias, mixer_hbm, *refs):
+    if flip:
+        (total_in, sums_in, squares_in, hidden, sent, total, sums, squares,
+         weight, offset, mixer, sems, mixer_sems) = refs
+    else:
+        total, sums, squares, sent, weight, offset, mixer, sems, mixer_sems = refs
     core = lax.axis_index("core")
+    side = 1 - core if flip else core
     row = lax.axis_index("zh") * lax.axis_size("x") + lax.axis_index("x")
     place = lax.axis_index("zl") * lax.axis_size("y") + lax.axis_index("y")
-    tokens, depth = patches.shape[0], weight_hbm.shape[0]
-    blocks, span, width = own_hbm.shape
-    group = weight_hbm.shape[1] // parts
-    count = parts * group
-    step = 512
-
-    def piece(b, side, source, sem):
-        at = pl.multiple_of((2 * b + side) * span, span)
-        return pltpu.make_async_copy(source.at[b], mixer.at[pl.ds(at, span), :], sem.at[b])
-
-    loads = [pltpu.make_async_copy(weight_hbm.at[:, pl.ds(g * group, group)], weight.at[g], sems.at[g])
-             for g in range(parts)]
-    pieces = [(piece(b, core, own_hbm, own_sems), piece(b, 1 - core, mate_hbm, mate_sems)) for b in range(blocks)]
-    loads[0].start()
-    for pair in pieces[:2]:
-        pair[0].start()
-        pair[1].start()
-    for load in loads[1:]:
-        load.start()
-    for pair in pieces[2:]:
-        pair[0].start()
-        pair[1].start()
+    depth, features = weight_hbm.shape
+    blocks, span, width = mixer_hbm.shape
+    tokens = patches.shape[0]
+    step = 1024
+
+    def first(b):
+        return pl.multiple_of((2 * b + side) * span, 128)
+    loads = [pltpu.make_async_copy(weight_hbm.at[:, pl.ds(first(b), span)], weight.at[:, pl.ds(b * span, span)], sems.at[b])
+             for b in range(blocks)]
+    mixes = [pltpu.make_async_copy(mixer_hbm.at[b], mixer.at[pl.ds(b * span, span), :], mixer_sems.at[b])
+             for b in range(blocks)]
+    for b in range(blocks):
+        loads[b].start()
+        mixes[b].start()
+    for b in range(blocks):
+        offset[:, b * span:(b + 1) * span] = bias[:, pl.ds(first(b), span)]
     pixels = patches[:, 0:depth]
     ones = jnp.ones((16, step), bf16)
     ready = 0
-    for c in range(count // step):
-        g, at = (c * step) // group, (c * step) % group
-        if at == 0:
-            loads[g].wait()
-        e = jnp.dot(pixels, weight[g, :, at:at + step], preferred_element_type=f32)
-        e = (e + bias[:, c * step:(c + 1) * step]).astype(bf16)
+    for c in range(blocks * span // step):
+        at = slice(c * step, (c + 1) * step)
+        while ready * span < (c + 1) * step:
+            loads[ready].wait()
+            mixes[ready].wait()
+            ready += 1
+        e = jnp.dot(pixels, weight[:, at], preferred_element_type=f32)
+        e = (e + offset[:, at]).astype(bf16)
         v = e.astype(f32)
         q = v * v
-        a = v[:, 0:128] + v[:, 128:256] + v[:, 256:384] + v[:, 384:512]
-        b = q[:, 0:128] + q[:, 128:256] + q[:, 256:384] + q[:, 384:512]
-        sums[...] = a if c == 0 else sums[...] + a
-        squares[...] = b if c == 0 else squares[...] + b
-        while ready * 2 * span < (c + 1) * step:
-            pieces[ready][0].wait()
-            pieces[ready][1].wait()
-            ready += 1
-        part = jnp.dot(jnp.concatenate([e, ones], axis=0), mixer[c * step:(c + 1) * step, :],
-                       preferred_element_type=f32)
-        total[...] = part if c == 0 else total[...] + part
+        a = sum(v[:, k:k + 128] for k in range(128, step, 128)) + v[:, 0:128]
+        b = sum(q[:, k:k + 128] for k in range(128, step, 128)) + q[:, 0:128]
+        part = jnp.dot(jnp.concatenate([e, ones], axis=0), mixer[at, :], preferred_element_type=f32)
+        if c:
+            a, b, part = a + sums[...], b + squares[...], part + total[...]
+        elif flip:
+            a, b, part = a + sums_in[...], b + squares_in[...], part + total_in[...]
+        sums[...], squares[...], total[...] = a, b, part
     share = tokens // 8
     mine = patches[pl.ds(pl.multiple_of(row * share, share), share), 0:depth]
-    for out, side in ((kept, core), (sent, 1 - core)):
-        first = 2 * place + side
-        g, at = first // (group // span), first % (group // span)
-        e = jnp.dot(mine, weight[g, :, pl.ds(pl.multiple_of(at * span, 128), span)], preferred_element_type=f32)
-        out[...] = (e + bias[:, pl.ds(pl.multiple_of(first * span, 128), span)]).astype(bf16)
-    mean = jnp.sum(sums[...], axis=1, keepdims=True) / count
-    square = jnp.sum(squares[...], axis=1, keepdims=True) / count
-    scale = lax.rsqrt(square - mean * mean + ln_epsilon)
-    column = total[tokens:tokens + 1, :]
-    value = gelu((total[0:tokens, :] - mean * column) * scale).astype(bf16)
-    for b in range(hidden.shape[0]):
-        hidden[b] = value
-
-
-def embed_call(patches, weight, bias, own, mate):
-    tokens = patches.shape[0]
-    _, span, width = own.shape
-    features = weight.shape[1]
-    parts = 4
-    share = tokens // 8
+    at = pl.ds(pl.multiple_of(place * span, 128), span)
+    sent[...] = (jnp.dot(mine, weight[:, at], preferred_element_type=f32) + offset[:, at]).astype(bf16)
+    if flip:
+        mean = jnp.sum(sums[...], axis=1, keepdims=True) / features
+        square = jnp.sum(squares[...], axis=1, keepdims=True) / features
+        scale = lax.rsqrt(square - mean * mean + ln_epsilon)
+        column = total[tokens:tokens + 1, :]
+        value = gelu((total[0:tokens, :] - mean * column) * scale).astype(bf16)
+        for b in range(hidden.shape[0]):
+            hidden[b] = value
+
+
+def embed_call(patches, weight, bias, mixer, carry):
+    tokens, depth = patches.shape[0], weight.shape[0]
+    blocks, span, width = mixer.shape
+    flip = 1 if carry else 0
+    sent = jax.ShapeDtypeStruct((tokens // 8, span), bf16)
+    state = [(tokens + 16, width), (tokens, 128), (tokens, 128)]
     vm = pl.BlockSpec(memory_space=pltpu.VMEM)
     hb = pl.BlockSpec(memory_space=pltpu.HBM)
+    if flip:
+        shapes = (jax.ShapeDtypeStruct((8, tokens, width), bf16), sent)
+        scratch = [pltpu.VMEM(shape, f32) for shape in state]
+    else:
+        shapes = tuple(jax.ShapeDtypeStruct(shape, f32) for shape in state) + (sent,)
+        scratch = []
     return pl.pallas_call(
-        functools.partial(embed_kernel, parts),
-        out_shape=(jax.ShapeDtypeStruct((8, tokens, width), bf16),
-                   jax.ShapeDtypeStruct((share, span), bf16),
-                   jax.ShapeDtypeStruct((share, span), bf16)),
-        in_specs=[vm, hb, vm, hb, hb],
-        out_specs=(vm, vm, vm),
-        scratch_shapes=[
-            pltpu.VMEM((parts, weight.shape[0], features // parts), bf16),
-            pltpu.VMEM((features, width), bf16),
-            pltpu.VMEM((tokens + 16, width), f32),
-            pltpu.VMEM((tokens, 128), f32),
-            pltpu.VMEM((tokens, 128), f32),
-            pltpu.SemaphoreType.DMA((parts,)),
-            pltpu.SemaphoreType.DMA((8,)),
-            pltpu.SemaphoreType.DMA((8,)),
+        functools.partial(embed_kernel, flip),
+        out_shape=shapes,
+        in_specs=[vm, hb, vm, hb] + [vm] * len(carry),
+        out_specs=(vm,) * len(shapes),
+        scratch_shapes=scratch + [
+            pltpu.VMEM((depth, blocks * span), bf16),
+            pltpu.VMEM((1, blocks * span), f32),
+            pltpu.VMEM((blocks * span, width), bf16),
+            pltpu.SemaphoreType.DMA((blocks,)),
+            pltpu.SemaphoreType.DMA((blocks,)),
         ],
         compiler_params=pltpu.CompilerParams(vmem_limit_bytes=58 << 20),
-        cost_estimate=pl.CostEstimate(flops=7_000_000_000, transcendentals=200_000, bytes_accessed=20_000_000),
-        name="embed_mlp",
-    )(patches, weight, bias, own, mate)
+        cost_estimate=pl.CostEstimate(flops=3_500_000_000, transcendentals=100_000, bytes_accessed=8_000_000),
+        name="embed_mate" if flip else "embed_own",
+    )(patches, weight, bias, mixer, *carry)
 
 
 def mix_kernel(hidden_hbm, own_hbm, mate_hbm, out, hidden, weight, total, sems):
@@ -432,11 +429,13 @@
 
     purified, patches = score_call(images, noise_field, stem_weight, level_one, down_weight, level_two,
                                    up_weight, out_weight, 64)
-    own_in, mate_out, _ = lax.optimization_barrier((own_in, mate_out, purified))
+    mate_out, patches = lax.optimization_barrier((mate_out, patches))
+    tokens = lax.all_to_all(patches, ("zh", "x", "zl", "y"), 0, 0)
+    own_in, tokens = lax.optimization_barrier((own_in, tokens))
+    tokens = tokens.reshape(-1, tokens.shape[-1])
     mate_in = swap(own_in)
-    tokens = lax.all_to_all(patches, ("zh", "x", "zl", "y"), 0, 0)
-    tokens = tokens.reshape(-1, tokens.shape[-1])
-    hidden, kept, sent = embed_call(tokens, embed_weight, embed_bias[None], own_in, mate_in)
+    *carry, kept = embed_call(tokens, embed_weight, embed_bias[None], own_in, ())
+    hidden, sent = embed_call(tokens, embed_weight, embed_bias[None], mate_in, tuple(carry))
     other = swap(sent)
     hidden = lax.all_to_all(hidden, ("zl", "y"), 0, 0)
     shares = mix_call(hidden, mlp_out, mate_out)

time: 159 us -> 161 us (1.013)
  Pallas kernels: 47.2 us -> 48.9 us
    ppermute x3, starting transfers between devices: 2.56 us -> 4.89 us  [swap(): return lax.ppermute(value, 'core', [(0, 1), (1, 0)])]
    pallas_call x1 -> x2, Pallas kernels: 17.2 us -> 18.9 us  [embed_call(): pl.pallas_call(functools.partial(embed_kernel, flip), out_shape=shapes, i...]
    all_to_all x1, blocking collectives: 28.9 us -> 27.3 us  [on_device(): tokens = lax.all_to_all(patches, ('zh', 'x', 'zl', 'y'), 0, 0)]
  transfers between devices with their start and end apart: 5 -> 5, of which waited for: 2 -> 2; matrix products, arithmetic and copies ran while one was open for 1% -> 1% of each run, Pallas kernels for 15% -> 20%
where the time goes in v4:
time: 161 us
  blocking collectives  70.1 us (44%)
  Pallas kernels  48.9 us (30%)
  waiting for transfers between devices  23.1 us (14%)
  starting transfers between devices  14.8 us (9%)
  local copies, waits for them, and re-layouts  2.88 us (2%)
    all_to_all x1, blocking collectives, on_device(): hidden = lax.all_to_all(hidden, ('zl', 'y'), 0, 0)  42.9 us
    all_to_all x1, blocking collectives, on_device(): tokens = lax.all_to_all(patches, ('zh', 'x', 'zl', 'y'), 0, 0)  27.3 us
    pallas_call x1, Pallas kernels, score_call(): pl.pallas_call(functools.partial(score_kernel, side, count), out_shape=(j...  20.4 us
    pallas_call x2, Pallas kernels, embed_call(): pl.pallas_call(functools.partial(embed_kernel, flip), out_shape=shapes, i...  18.9 us
    all_to_all x1, waiting for transfers between devices, on_device(): shares = lax.all_to_all(shares, ('zh', 'x', 'core'), 0, 0)  14.3 us
    all_to_all x1, waiting for transfers between devices, on_device(): own_in = lax.all_to_all(split_call(mlp_in, 8), ('zl', 'y'), 0, 0)  8.78 us
    pallas_call x1, Pallas kernels, mix_call(): pl.pallas_call(mix_kernel, out_shape=jax.ShapeDtypeStruct((16, tokens //...  6.55 us
    all_to_all x1, starting transfers between devices, on_device(): own_in = lax.all_to_all(split_call(mlp_in, 8), ('zl', 'y'), 0, 0)  5.64 us
  transfers between devices with their start and end apart: 5, of which 2 were waited for; matrix products, arithmetic and copies ran while one was open for 1% of the time, Pallas kernels for 20%

profile of v4, /device:TPU:1, one launch (start us, length us, event | category | flops | bytes accessed | tf_op | source)
XLA Modules:
  0.0 160.8 jit_solution(2830219846149805178)
XLA Ops:
  0.6 1.5 collective-permute-start
  2.1 3.1 %split_columns.1 = bf16[8,384,384]{2,1,0:T(8,128)(2,1)} custom-call(bf16[384,3072]{1,0:T(8,128)(2,1)} %whole.1), custom_call_target="tpu_custom_call" | custom-call | bytes 4718592 | tf_op jit(solution)/shard_map/split_columns/pallas_call | solution.py:408
  5.2 0.0 copy-start.2
  5.2 5.6 %all-to-all-start = ((bf16[8,384,384]{2,1,0:T(8,128)(2,1)}), bf16[8,384,384]{2,1,0:T(8,128)(2,1)S(1)}, u32[]{:S(2)}, u32[]{:S(2)}) async-start(bf16[8,384,384]{2,1,0:T(8,128)(2,1)} %split_columns.1), calls=%async_computation | async-start | bytes 4718592 | tf_op jit(solution)/shard_map/all_to_all | solution.py:427
  10.9 0.0 copy-done.2
  10.9 0.8 copy.14.out_w
  11.6 20.4 %score_net.1 = (f32[28,3,2,28]{3,2,1,0:T(2,128)}, bf16[64,8,640]{2,1,0:T(8,128)(2,1)}) custom-call(f32[28,3,2,28]{3,2,1,0:T(2,128)} %bitcast.18, f32[28,3,2,28]{3,2,1,0:T(2,128)} %bitcast.19, bf16[27,256]{1,0:T(8,128)(2,1)} %stem_w.1, bf16[4,2304,256]{2,1,0:T(8,128)(2,1)} %l1_hbm.1, bf16[1024,256]{1,0:T(8,128)(2,1)} %down_hbm.1, ...), custom_call_target="tpu_custom_call" | custom-call | flops 10000000000 | bytes 12000000 | tf_op jit(solution)/shard_map/score_net/pallas_call | solution.py:218
  32.0 0.0 collective-permute-done.mate_hbm
  32.0 8.8 %all-to-all-done.mixer_hbm = bf16[8,384,384]{2,1,0:T(8,128)(2,1)S(1)} async-done(((bf16[8,384,384]{2,1,0:T(8,128)(2,1)}), bf16[8,384,384]{2,1,0:T(8,128)(2,1)S(1)}, u32[]{:S(2)}, u32[]{:S(2)}) %all-to-all-start) | async-done | bytes 2359328 | tf_op jit(solution)/shard_map/all_to_all | solution.py:427
  40.8 0.0 copy-start
  40.8 27.3 %all_to_all.20 = bf16[64,8,640]{2,1,0:T(8,128)(2,1)} all-to-all(bf16[64,8,640]{2,1,0:T(8,128)(2,1)} %get-tuple-element.16), channel_id=1, replica_groups=mesh['zh'=2,'x'=4,'zl'=2,'y'=4,'core'=2] {'zh','x','zl','y'}, dimensions={0} | all-to-all | bytes 1310720 | tf_op jit(solution)/shard_map/all_to_all | solution.py:433
  68.1 3.1 %collective-permute-start.1 = (bf16[8,384,384]{2,1,0:T(8,128)(2,1)S(1)}, bf16[8,384,384]{2,1,0:T(8,128)(2,1)S(1)}, u32[]{:S(2)}, u32[]{:S(2)}) collective-permute-start(bf16[8,384,384]{2,1,0:T(8,128)(2,1)S(1)} %all-to-all-done.mixer_hbm), channel_id=1, source_target_pairs={{0,1},{1,0},{2,3},{3,2},{4,5},{5,4},{6,7},{7,6},{8,9},{9,8},{10,11... | collective-permute-start | bytes 7077896 | tf_op jit(solution)/shard_map/ppermute | solution.py:421
  71.2 0.0 copy-done
  71.2 8.4 %embed_own.1 = (f32[528,384]{1,0:T(8,128)}, f32[512,128]{1,0:T(8,128)}, f32[512,128]{1,0:T(8,128)}, bf16[64,384]{1,0:T(8,128)(2,1)}) custom-call(bf16[512,640]{1,0:T(8,128)(2,1)} %bitcast.13, bf16[588,6144]{1,0:T(8,128)(2,1)} %weight_hbm.3, f32[1,6144]{1,0:T(1,128)} %bitcast.20, bf16[8,384,384]{2,1,0:T(8,128)(2,1)} %copy-done), custom_call_target="tpu_custom_call" | custom-call | flops 3500000000 | bytes 8000000 | tf_op jit(solution)/shard_map/embed_own/pallas_call | solution.py:324
  79.6 0.0 collective-permute-done.1.mixer_hbm
  79.6 0.0 copy-start.3
  79.6 1.4 copy-done.3
  81.1 10.5 %embed_mate.1 = (bf16[8,512,384]{2,1,0:T(8,128)(2,1)}, bf16[64,384]{1,0:T(8,128)(2,1)}) custom-call(bf16[512,640]{1,0:T(8,128)(2,1)} %bitcast.14, bf16[588,6144]{1,0:T(8,128)(2,1)} %weight_hbm.3, f32[1,6144]{1,0:T(1,128)} %bitcast.21, bf16[8,384,384]{2,1,0:T(8,128)(2,1)} %copy-done.3, f32[528,384]{1,0:T(8,128)} %get-tuple-element.19.refs_0_, ...), custom_call_target="tpu_custom_call" | custom-call | flops 3500000000 | bytes 8000000 | tf_op jit(solution)/shard_map/embed_mate/pallas_call | solution.py:324
  91.6 42.9 %all_to_all.21.hidden_hbm = bf16[8,512,384]{2,1,0:T(8,128)(2,1)} all-to-all(bf16[8,512,384]{2,1,0:T(8,128)(2,1)} %get-tuple-element.22), channel_id=1, replica_groups=mesh['zh'=2,'x'=4,'zl'=2,'y'=4,'core'=2] {'zl','y'}, dimensions={0} | all-to-all | bytes 6291456 | tf_op jit(solution)/shard_map/all_to_all | solution.py:440
  134.5 0.0 copy-start.4
  134.5 6.6 %mlp_out.1 = bf16[16,64,384]{2,1,0:T(8,128)(2,1)} custom-call(bf16[8,512,384]{2,1,0:T(8,128)(2,1)} %all_to_all.21.hidden_hbm, bf16[3072,384]{1,0:T(8,128)(2,1)} %own_hbm.1, bf16[3072,384]{1,0:T(8,128)(2,1)} %collective-permute-done.mate_hbm), custom_call_target="tpu_custom_call" | custom-call | flops 2400000000 | bytes 9000000 | tf_op jit(solution)/shard_map/mlp_out/pallas_call | solution.py:379
  141.0 0.0 copy-start.1
  141.0 4.3 %all-to-all-start.3 = ((bf16[16,64,384]{2,1,0:T(8,128)(2,1)}), bf16[16,64,384]{2,1,0:T(8,128)(2,1)S(1)}, u32[]{:S(2)}, u32[]{:S(2)}) async-start(bf16[16,64,384]{2,1,0:T(8,128)(2,1)} %mlp_out.1), calls=%async_computation.3 | async-start | bytes 1572864 | tf_op jit(solution)/shard_map/all_to_all | solution.py:442
  145.3 0.0 copy-done.4
  145.3 0.3 collective-permute-start.2
  145.6 14.3 %all-to-all-done.3 = bf16[16,64,384]{2,1,0:T(8,128)(2,1)S(1)} async-done(((bf16[16,64,384]{2,1,0:T(8,128)(2,1)}), bf16[16,64,384]{2,1,0:T(8,128)(2,1)S(1)}, u32[]{:S(2)}, u32[]{:S(2)}) %all-to-all-start.3) | async-done | bytes 786464 | tf_op jit(solution)/shard_map/all_to_all | solution.py:442
  159.9 0.1 convert_reduce_fusion
  160.0 0.0 collective-permute-done.2
  160.1 0.0 copy-done.1
  160.1 0.7 copy.15
  (1 shorter events, 0.0 us)
Async XLA Ops:
  0.6 31.4 %collective-permute-start = (bf16[3072,384]{1,0:T(8,128)(2,1)}, bf16[3072,384]{1,0:T(8,128)(2,1)}, u32[]{:S(2)}, u32[]{:S(2)}) collective-permute-start(bf16[3072,384]{1,0:T(8,128)(2,1)} %own_hbm.1), channel_id=1, source_target_pairs={{0,1},{1,0},{2,3},{3,2},{4,5},{5,4},{6,7},{7,6},{8,9},{9,8},{10,11... | collective-permute-start | bytes 7077896 | tf_op jit(solution)/shard_map/ppermute | solution.py:421
  5.2 5.7 %copy-start.2 = (bf16[256,3]{0,1:T(4,128)(2,1)S(1)}, bf16[256,3]{0,1:T(4,128)(2,1)}, u32[]{:S(2)}) copy-start(bf16[256,3]{0,1:T(4,128)(2,1)} %param.19) | copy-start | bytes 4612
  5.2 35.6 %all-to-all-start = ((bf16[8,384,384]{2,1,0:T(8,128)(2,1)}), bf16[8,384,384]{2,1,0:T(8,128)(2,1)S(1)}, u32[]{:S(2)}, u32[]{:S(2)}) async-start(bf16[8,384,384]{2,1,0:T(8,128)(2,1)} %split_columns.1), calls=%async_computation | async-start | bytes 4718592 | tf_op jit(solution)/shard_map/all_to_all | solution.py:427
  40.8 30.4 %copy-start = (bf16[8,384,384]{2,1,0:T(8,128)(2,1)}, bf16[8,384,384]{2,1,0:T(8,128)(2,1)S(1)}, u32[]{:S(2)}) copy-start(bf16[8,384,384]{2,1,0:T(8,128)(2,1)S(1)} %all-to-all-done.mixer_hbm) | copy-start | bytes 7077892
  68.1 11.5 %collective-permute-start.1 = (bf16[8,384,384]{2,1,0:T(8,128)(2,1)S(1)}, bf16[8,384,384]{2,1,0:T(8,128)(2,1)S(1)}, u32[]{:S(2)}, u32[]{:S(2)}) collective-permute-start(bf16[8,384,384]{2,1,0:T(8,128)(2,1)S(1)} %all-to-all-done.mixer_hbm), channel_id=1, source_target_pairs={{0,1},{1,0},{2,3},{3,2},{4,5},{5,4},{6,7},{7,6},{8,9},{9,8},{10,11... | collective-permute-start | bytes 7077896 | tf_op jit(solution)/shard_map/ppermute | solution.py:421
  79.6 1.5 copy-start.3
  134.5 10.8 %copy-start.4 = (bf16[64,384]{1,0:T(8,128)(2,1)S(1)}, bf16[64,384]{1,0:T(8,128)(2,1)}, u32[]{:S(2)}) copy-start(bf16[64,384]{1,0:T(8,128)(2,1)} %get-tuple-element.25) | copy-start | bytes 147460
  141.0 19.0 %copy-start.1 = (bf16[64,384]{1,0:T(8,128)(2,1)S(1)}, bf16[64,384]{1,0:T(8,128)(2,1)}, u32[]{:S(2)}) copy-start(bf16[64,384]{1,0:T(8,128)(2,1)} %get-tuple-element.24) | copy-start | bytes 147460
  141.0 18.9 %all-to-all-start.3 = ((bf16[16,64,384]{2,1,0:T(8,128)(2,1)}), bf16[16,64,384]{2,1,0:T(8,128)(2,1)S(1)}, u32[]{:S(2)}, u32[]{:S(2)}) async-start(bf16[16,64,384]{2,1,0:T(8,128)(2,1)} %mlp_out.1), calls=%async_computation.3 | async-start | bytes 1572864 | tf_op jit(solution)/shard_map/all_to_all | solution.py:442
  145.3 14.7 %collective-permute-start.2 = (bf16[64,384]{1,0:T(8,128)(2,1)S(1)}, bf16[64,384]{1,0:T(8,128)(2,1)S(1)}, u32[]{:S(2)}, u32[]{:S(2)}) collective-permute-start(bf16[64,384]{1,0:T(8,128)(2,1)S(1)} %copy-done.4), channel_id=1, source_target_pairs={{0,1},{1,0},{2,3},{3,2},{4,5},{5,4},{6,7},{7,6},{8,9},{9,8},{10,11... | collective-permute-start | bytes 147464 | tf_op jit(solution)/shard_map/ppermute | solution.py:421

commit v5 on v4

--- a/solution.py
+++ b/solution.py
@@ -204,11 +204,10 @@
         if at + run > 128:
             pieces[k + 1] += jnp.where(lanes < at, z, 0.0)
     tokens = jnp.concatenate(pieces, axis=1).astype(bf16)
-    for k in range(patches.shape[0]):
-        patches[k] = tokens
-
-
-def score_call(images, noise, stem_w, l1, down, l2, up, out_w, copies):
+    patches[...] = tokens
+
+
+def score_call(images, noise, stem_w, l1, down, l2, up, out_w):
     count, side = images.shape[0], images.shape[1]
     rows1 = W1 + count * (side + 1) * W1
     rows2 = W2 + count * (side // 2 + 1) * W2
@@ -217,7 +216,7 @@
     hb = pl.BlockSpec(memory_space=pltpu.HBM)
     purified, patches = pl.pallas_call(
         functools.partial(score_kernel, side, count),
-        out_shape=(jax.ShapeDtypeStruct(images.shape, f32), jax.ShapeDtypeStruct((copies, 4 * count, 640), bf16)),
+        out_shape=(jax.ShapeDtypeStruct(images.shape, f32), jax.ShapeDtypeStruct((4 * count, 640), bf16)),
         in_specs=[vm, vm, vm, hb, hb, hb, hb, vm],
         out_specs=(vm, vm),
         scratch_shapes=[
@@ -246,16 +245,16 @@
     return purified.transpose(2, 0, 3, 1), patches
 
 
-def embed_kernel(flip, patches, weight_hbm, bias, mixer_hbm, *refs):
+def embed_kernel(flip, piece0, piece1, piece2, piece3, weight_hbm, bias, mixer_hbm, *refs):
     if flip:
         (total_in, sums_in, squares_in, hidden, sent, total, sums, squares,
-         weight, offset, mixer, sems, mixer_sems) = refs
+         patches, weight, offset, mixer, sems, mixer_sems, piece_sems) = refs
     else:
-        total, sums, squares, sent, weight, offset, mixer, sems, mixer_sems = refs
+        total, sums, squares, sent, patches, weight, offset, mixer, sems, mixer_sems, piece_sems = refs
     core = lax.axis_index("core")
     side = 1 - core if flip else core
-    row = lax.axis_index("zh") * lax.axis_size("x") + lax.axis_index("x")
-    place = lax.axis_index("zl") * lax.axis_size("y") + lax.axis_index("y")
+    level, line, lines = lax.axis_index("zl"), lax.axis_index("y"), lax.axis_size("y")
+    place = level * lines + line
     depth, features = weight_hbm.shape
     blocks, span, width = mixer_hbm.shape
     tokens = patches.shape[0]
@@ -267,11 +266,23 @@
              for b in range(blocks)]
     mixes = [pltpu.make_async_copy(mixer_hbm.at[b], mixer.at[pl.ds(b * span, span), :], mixer_sems.at[b])
              for b in range(blocks)]
+    share = tokens // 8
+    moves = []
+    for k, piece in enumerate((piece0, piece1, piece2, piece3)):
+        for part in range(2):
+            to = (level + part) % 2 * lines + (line + lines - k) % lines
+            moves.append(pltpu.make_async_copy(
+                piece.at[pl.ds(part * share, share), :],
+                patches.at[pl.ds(pl.multiple_of(to * share, share), share), :], piece_sems.at[2 * k + part]))
+    for move in moves:
+        move.start()
     for b in range(blocks):
         loads[b].start()
         mixes[b].start()
     for b in range(blocks):
         offset[:, b * span:(b + 1) * span] = bias[:, pl.ds(first(b), span)]
+    for move in moves:
+        move.wait()
     pixels = patches[:, 0:depth]
     ones = jnp.ones((16, step), bf16)
     ready = 0
@@ -293,8 +304,7 @@
         elif flip:
             a, b, part = a + sums_in[...], b + squares_in[...], part + total_in[...]
         sums[...], squares[...], total[...] = a, b, part
-    share = tokens // 8
-    mine = patches[pl.ds(pl.multiple_of(row * share, share), share), 0:depth]
+    mine = jnp.concatenate([patches[b * share:b * share + 8, 0:depth].astype(f32) for b in range(8)], axis=0).astype(bf16)
     at = pl.ds(pl.multiple_of(place * span, 128), span)
     sent[...] = (jnp.dot(mine, weight[:, at], preferred_element_type=f32) + offset[:, at]).astype(bf16)
     if flip:
@@ -307,10 +317,11 @@
             hidden[b] = value
 
 
-def embed_call(patches, weight, bias, mixer, carry):
-    tokens, depth = patches.shape[0], weight.shape[0]
+def embed_call(pieces, weight, bias, mixer, carry):
+    tokens, depth = 4 * pieces[0].shape[0], weight.shape[0]
     blocks, span, width = mixer.shape
     flip = 1 if carry else 0
+    free = pl.BlockSpec(memory_space=pl.ANY)
     sent = jax.ShapeDtypeStruct((tokens // 8, span), bf16)
     state = [(tokens + 16, width), (tokens, 128), (tokens, 128)]
     vm = pl.BlockSpec(memory_space=pltpu.VMEM)
@@ -324,19 +335,21 @@
     return pl.pallas_call(
         functools.partial(embed_kernel, flip),
         out_shape=shapes,
-        in_specs=[vm, hb, vm, hb] + [vm] * len(carry),
+        in_specs=[free] * 4 + [hb, vm, free] + [vm] * len(carry),
         out_specs=(vm,) * len(shapes),
         scratch_shapes=scratch + [
+            pltpu.VMEM((tokens, pieces[0].shape[1]), bf16),
             pltpu.VMEM((depth, blocks * span), bf16),
             pltpu.VMEM((1, blocks * span), f32),
             pltpu.VMEM((blocks * span, width), bf16),
             pltpu.SemaphoreType.DMA((blocks,)),
             pltpu.SemaphoreType.DMA((blocks,)),
+            pltpu.SemaphoreType.DMA((8,)),
         ],
         compiler_params=pltpu.CompilerParams(vmem_limit_bytes=58 << 20),
         cost_estimate=pl.CostEstimate(flops=3_500_000_000, transcendentals=100_000, bytes_accessed=8_000_000),
         name="embed_mate" if flip else "embed_own",
-    )(patches, weight, bias, mixer, *carry)
+    )(*pieces, weight, bias, mixer, *carry)
 
 
 def mix_kernel(hidden_hbm, own_hbm, mate_hbm, out, hidden, weight, total, sems):
@@ -364,12 +377,14 @@
         elif k < parts - 1:
             total[...] += part
         else:
-            done = (total[...] + part).astype(bf16)
+            done = total[...] + part
     share = out.shape[1]
-    for r in range(tokens // share):
-        rows = slice(r * share, (r + 1) * share)
-        out[2 * r + core] = done[rows, 0:span]
-        out[2 * r + 1 - core] = done[rows, span:2 * span]
+    high, across, size = lax.axis_index("zh"), lax.axis_index("x"), lax.axis_size("x")
+    for q in range(tokens // share):
+        rows = jnp.concatenate([done[b * share + q * 8:b * share + q * 8 + 8, :] for b in range(8)], axis=0).astype(bf16)
+        r = (high + q // size) % 2 * size + (across + size - q % size) % size
+        out[2 * r + core] = rows[:, 0:span]
+        out[2 * r + 1 - core] = rows[:, span:2 * span]
 
 
 def mix_call(hidden, own, mate):
@@ -417,6 +432,11 @@
     )(whole)
 
 
+def shift(value, axis, k):
+    n = lax.axis_size(axis)
+    return lax.ppermute(value, axis, [(i, (i + k) % n) for i in range(n)])
+
+
 def swap(value):
     return lax.ppermute(value, "core", [(0, 1), (1, 0)])
 
@@ -428,14 +448,16 @@
     mate_out = swap(mlp_out)
 
     purified, patches = score_call(images, noise_field, stem_weight, level_one, down_weight, level_two,
-                                   up_weight, out_weight, 64)
+                                   up_weight, out_weight)
     mate_out, patches = lax.optimization_barrier((mate_out, patches))
-    tokens = lax.all_to_all(patches, ("zh", "x", "zl", "y"), 0, 0)
-    own_in, tokens = lax.optimization_barrier((own_in, tokens))
-    tokens = tokens.reshape(-1, tokens.shape[-1])
+    patches = jnp.concatenate([patches] + [shift(patches, "x", k) for k in (1, 2, 3)], axis=0)
+    patches = jnp.concatenate([patches, shift(patches, "zh", 1)], axis=0)
+    patches = jnp.concatenate([patches, shift(patches, "zl", 1)], axis=0)
+    pieces = [patches] + [shift(patches, "y", k) for k in (1, 2, 3)]
+    own_in, *pieces = lax.optimization_barrier((own_in, *pieces))
     mate_in = swap(own_in)
-    *carry, kept = embed_call(tokens, embed_weight, embed_bias[None], own_in, ())
-    hidden, sent = embed_call(tokens, embed_weight, embed_bias[None], mate_in, tuple(carry))
+    *carry, kept = embed_call(pieces, embed_weight, embed_bias[None], own_in, ())
+    hidden, sent = embed_call(pieces, embed_weight, embed_bias[None], mate_in, tuple(carry))
     other = swap(sent)
     hidden = lax.all_to_all(hidden, ("zl", "y"), 0, 0)
     shares = mix_call(hidden, mlp_out, mate_out)

time: 161 us -> 157 us (0.975)
  blocking collectives: 70.1 us -> 42 us
  starting transfers between devices: 14.8 us -> 35.8 us
  Pallas kernels: 48.9 us -> 50.7 us
    all_to_all x1 -> x0, blocking collectives: 27.3 us -> none  [on_device(): tokens = lax.all_to_all(patches, ('zh', 'x', 'zl', 'y'), 0, 0)]
    ppermute x0 -> x8, starting transfers between devices: none -> 14.5 us  [shift(): return lax.ppermute(value, axis, [(i, (i + k) % n) for i in range(n)])]
    all_to_all x1, waiting for transfers between devices: 8.78 us -> 0.01 us  [on_device(): own_in = lax.all_to_all(split_call(mlp_in, 8), ('zl', 'y'), 0, 0)]
    ppermute x0 -> x8, waiting for transfers between devices: none -> 8.56 us  [shift(): return lax.ppermute(value, axis, [(i, (i + k) % n) for i in range(n)])]
    all_to_all x1, starting transfers between devices: 4.25 us -> 9.22 us  [on_device(): shares = lax.all_to_all(shares, ('zh', 'x', 'core'), 0, 0)]
    pallas_call x2, Pallas kernels: 18.9 us -> 20.8 us  [embed_call(): pl.pallas_call(functools.partial(embed_kernel, flip), out_shape=shapes, i...]
  transfers between devices with their start and end apart: 5 -> 13, of which waited for: 2 -> 7; matrix products, arithmetic and copies ran while one was open for 1% -> 2% of each run, Pallas kernels for 20% -> 21%
where the time goes in v5:
time: 157 us
  Pallas kernels  50.7 us (32%)
  blocking collectives  42 us (27%)
  starting transfers between devices  35.8 us (23%)
  waiting for transfers between devices  22.9 us (15%)
  local copies, waits for them, and re-layouts  3.69 us (2%)
    all_to_all x1, blocking collectives, on_device(): hidden = lax.all_to_all(hidden, ('zl', 'y'), 0, 0)  42 us
    pallas_call x2, Pallas kernels, embed_call(): pl.pallas_call(functools.partial(embed_kernel, flip), out_shape=shapes, i...  20.8 us
    pallas_call x1, Pallas kernels, score_call(): pl.pallas_call(functools.partial(score_kernel, side, count), out_shape=(j...  20.1 us
    ppermute x8, starting transfers between devices, shift(): return lax.ppermute(value, axis, [(i, (i + k) % n) for i in range(n)])  14.5 us
    all_to_all x1, waiting for transfers between devices, on_device(): shares = lax.all_to_all(shares, ('zh', 'x', 'core'), 0, 0)  14.3 us
    all_to_all x1, starting transfers between devices, on_device(): shares = lax.all_to_all(shares, ('zh', 'x', 'core'), 0, 0)  9.22 us
    ppermute x8, waiting for transfers between devices, shift(): return lax.ppermute(value, axis, [(i, (i + k) % n) for i in range(n)])  8.56 us
    pallas_call x1, Pallas kernels, mix_call(): pl.pallas_call(mix_kernel, out_shape=jax.ShapeDtypeStruct((16, tokens //...  6.61 us
  transfers between devices with their start and end apart: 13, of which 7 were waited for; matrix products, arithmetic and copies ran while one was open for 2% of the time, Pallas kernels for 21%

profile of v5, /device:TPU:1, one launch (start us, length us, event | category | flops | bytes accessed | tf_op | source)
XLA Modules:
  0.0 156.7 jit_solution(7835758652156449945)
XLA Ops:
  0.6 1.5 collective-permute-start
  2.1 3.1 %split_columns.1 = bf16[8,384,384]{2,1,0:T(8,128)(2,1)} custom-call(bf16[384,3072]{1,0:T(8,128)(2,1)} %whole.1), custom_call_target="tpu_custom_call" | custom-call | bytes 4718592 | tf_op jit(solution)/shard_map/split_columns/pallas_call | solution.py:423
  5.3 5.6 %all-to-all-start = ((bf16[8,384,384]{2,1,0:T(8,128)(2,1)}), bf16[8,384,384]{2,1,0:T(8,128)(2,1)S(1)}, u32[]{:S(2)}, u32[]{:S(2)}) async-start(bf16[8,384,384]{2,1,0:T(8,128)(2,1)} %split_columns.1), calls=%async_computation | async-start | bytes 4718592 | tf_op jit(solution)/shard_map/all_to_all | solution.py:447
  10.9 0.8 copy.14.out_w
  11.7 20.1 %score_net.1 = (f32[28,3,2,28]{3,2,1,0:T(2,128)}, bf16[8,640]{1,0:T(8,128)(2,1)}) custom-call(f32[28,3,2,28]{3,2,1,0:T(2,128)} %bitcast.15, f32[28,3,2,28]{3,2,1,0:T(2,128)} %bitcast.16, bf16[27,256]{1,0:T(8,128)(2,1)} %stem_w.1, bf16[4,2304,256]{2,1,0:T(8,128)(2,1)} %l1_hbm.1, bf16[1024,256]{1,0:T(8,128)(2,1)} %down_hbm.1, bf16[2,2304,256]{2,1,0:T(8,128)(2,1)} %l2_hbm.1, ...), custom_call_target="tpu_custom_call" | custom-call | flops 10000000000 | bytes 12000000 | tf_op jit(solution)/shard_map/score_net/pallas_call | solution.py:217
  31.8 1.3 collective-permute-start.1
  33.1 2.5 %collective-permute-start.2 = (bf16[8,640]{1,0:T(8,128)(2,1)}, bf16[8,640]{1,0:T(8,128)(2,1)S(1)}, u32[]{:S(2)}, u32[]{:S(2)}) collective-permute-start(bf16[8,640]{1,0:T(8,128)(2,1)} %get-tuple-element.19), channel_id=1, source_target_pairs={{0,32},{16,48},{32,0},{48,16},{1,33},{17,49},{33,1},{49,17},{2,34}... | collective-permute-start | bytes 30728 | tf_op jit(solution)/shard_map/ppermute | solution.py:437
  35.5 1.2 collective-permute-start.3
  36.7 0.7 constant_dynamic-update-slice_fusion.4
  37.4 0.2 collective-permute-done.2
  37.6 0.9 collective-permute-done.3
  38.5 0.7 pad_maximum_fusion
  39.2 3.3 %collective-permute-start.4 = (bf16[32,640]{1,0:T(8,128)(2,1)S(1)}, bf16[32,640]{1,0:T(8,128)(2,1)S(1)}, u32[]{:S(2)}, u32[]{:S(2)}) collective-permute-start(bf16[32,640]{1,0:T(8,128)(2,1)S(1)} %pad_maximum_fusion), channel_id=1, source_target_pairs={{0,64},{64,0},{1,65},{65,1},{2,66},{66,2},{3,67},{67,3},{4,68},{68... | collective-permute-start | bytes 122888 | tf_op jit(solution)/shard_map/ppermute | solution.py:437
  42.6 1.4 collective-permute-done.4
  44.0 1.2 collective-permute-start.5
  45.2 2.6 %collective-permute-done.5 = bf16[64,640]{1,0:T(8,128)(2,1)S(1)} collective-permute-done((bf16[64,640]{1,0:T(8,128)(2,1)S(1)}, bf16[64,640]{1,0:T(8,128)(2,1)S(1)}, u32[]{:S(2)}, u32[]{:S(2)}) %collective-permute-start.5) | collective-permute-done | bytes 81952 | tf_op jit(solution)/shard_map/ppermute | solution.py:437
  47.8 1.5 collective-permute-start.6
  49.3 2.5 %collective-permute-start.7 = (bf16[128,640]{1,0:T(8,128)(2,1)S(1)}, bf16[128,640]{1,0:T(8,128)(2,1)S(1)}, u32[]{:S(2)}, u32[]{:S(2)}) collective-permute-start(bf16[128,640]{1,0:T(8,128)(2,1)S(1)} %constant_dynamic-update-slice_fusion.5.piece0), channel_id=1, source_target_pairs={{0,4},{2,6},{4,0},{6,2},{1,5},{3,7},{5,1},{7,3},{8,12},{10,14},{12... | collective-permute-start | bytes 491528 | tf_op jit(solution)/shard_map/ppermute | solution.py:437
  51.8 1.1 collective-permute-start.8
  52.9 0.4 collective-permute-done.6.piece1
  53.3 3.0 %collective-permute-done.7.piece2 = bf16[128,640]{1,0:T(8,128)(2,1)S(1)} collective-permute-done((bf16[128,640]{1,0:T(8,128)(2,1)S(1)}, bf16[128,640]{1,0:T(8,128)(2,1)S(1)}, u32[]{:S(2)}, u32[]{:S(2)}) %collective-permute-start.7) | collective-permute-done | bytes 163872 | tf_op jit(solution)/shard_map/ppermute | solution.py:437
  56.4 4.8 %collective-permute-start.9 = (bf16[8,384,384]{2,1,0:T(8,128)(2,1)S(1)}, bf16[8,384,384]{2,1,0:T(8,128)(2,1)S(1)}, u32[]{:S(2)}, u32[]{:S(2)}) collective-permute-start(bf16[8,384,384]{2,1,0:T(8,128)(2,1)S(1)} %all-to-all-done.mixer_hbm), channel_id=1, source_target_pairs={{0,1},{1,0},{2,3},{3,2},{4,5},{5,4},{6,7},{7,6},{8,9},{9,8},{10,11... | collective-permute-start | bytes 7077896 | tf_op jit(solution)/shard_map/ppermute | solution.py:441
  61.2 9.3 %embed_own.1 = (f32[528,384]{1,0:T(8,128)}, f32[512,128]{1,0:T(8,128)}, f32[512,128]{1,0:T(8,128)}, bf16[64,384]{1,0:T(8,128)(2,1)}) custom-call(bf16[128,640]{1,0:T(8,128)(2,1)} %copy-done.3, bf16[128,640]{1,0:T(8,128)(2,1)} %copy-done.5, bf16[128,640]{1,0:T(8,128)(2,1)} %copy-done.6, bf16[128,640]{1,0:T(8,128)(2,1)} %copy-done.7, ...), custom_call_target="tpu_custom_call" | custom-call | flops 3500000000 | bytes 8000000 | tf_op jit(solution)/shard_map/embed_own/pallas_call | solution.py:335
  70.5 1.5 copy-done.4
  71.9 11.6 %embed_mate.1 = (bf16[8,512,384]{2,1,0:T(8,128)(2,1)}, bf16[64,384]{1,0:T(8,128)(2,1)}) custom-call(bf16[128,640]{1,0:T(8,128)(2,1)} %copy-done.3, bf16[128,640]{1,0:T(8,128)(2,1)} %copy-done.5, bf16[128,640]{1,0:T(8,128)(2,1)} %copy-done.6, bf16[128,640]{1,0:T(8,128)(2,1)} %copy-done.7, bf16[588,6144]{1,0:T(8,128)(2,1)} %weight_hbm.3, f32[1,6144]{1,0:T(1,128)} %bitcast.18, ...), custom_call_target="tpu_custom_call" | custom-call | flops 3500000000 | bytes 8000000 | tf_op jit(solution)/shard_map/embed_mate/pallas_call | solution.py:335
  83.5 42.0 %all_to_all.15.hidden_hbm = bf16[8,512,384]{2,1,0:T(8,128)(2,1)} all-to-all(bf16[8,512,384]{2,1,0:T(8,128)(2,1)} %get-tuple-element.28), channel_id=1, replica_groups=mesh['zh'=2,'x'=4,'zl'=2,'y'=4,'core'=2] {'zl','y'}, dimensions={0} | all-to-all | bytes 6291456 | tf_op jit(solution)/shard_map/all_to_all | solution.py:462
  125.6 6.6 %mlp_out.1 = bf16[16,64,384]{2,1,0:T(8,128)(2,1)} custom-call(bf16[8,512,384]{2,1,0:T(8,128)(2,1)} %all_to_all.15.hidden_hbm, bf16[3072,384]{1,0:T(8,128)(2,1)} %own_hbm.1, bf16[3072,384]{1,0:T(8,128)(2,1)} %collective-permute-done.mate_hbm), custom_call_target="tpu_custom_call" | custom-call | flops 2400000000 | bytes 9000000 | tf_op jit(solution)/shard_map/mlp_out/pallas_call | solution.py:394
  132.2 9.2 %all-to-all-start.2 = ((bf16[16,64,384]{2,1,0:T(8,128)(2,1)}), bf16[16,64,384]{2,1,0:T(8,128)(2,1)S(1)}, u32[]{:S(2)}, u32[]{:S(2)}) async-start(bf16[16,64,384]{2,1,0:T(8,128)(2,1)} %mlp_out.1), calls=%async_computation.2 | async-start | bytes 1572864 | tf_op jit(solution)/shard_map/all_to_all | solution.py:464
  141.4 0.2 collective-permute-start.10
  141.6 14.3 %all-to-all-done.2 = bf16[16,64,384]{2,1,0:T(8,128)(2,1)S(1)} async-done(((bf16[16,64,384]{2,1,0:T(8,128)(2,1)}), bf16[16,64,384]{2,1,0:T(8,128)(2,1)S(1)}, u32[]{:S(2)}, u32[]{:S(2)}) %all-to-all-start.2) | async-done | bytes 786464 | tf_op jit(solution)/shard_map/all_to_all | solution.py:464
  155.9 0.1 convert_reduce_fusion
  156.1 0.7 copy.15
  (29 shorter events, 0.1 us)
Async XLA Ops:
  0.6 31.1 %collective-permute-start = (bf16[3072,384]{1,0:T(8,128)(2,1)}, bf16[3072,384]{1,0:T(8,128)(2,1)}, u32[]{:S(2)}, u32[]{:S(2)}) collective-permute-start(bf16[3072,384]{1,0:T(8,128)(2,1)} %own_hbm.1), channel_id=1, source_target_pairs={{0,1},{1,0},{2,3},{3,2},{4,5},{5,4},{6,7},{7,6},{8,9},{9,8},{10,11... | collective-permute-start | bytes 7077896 | tf_op jit(solution)/shard_map/ppermute | solution.py:441
  5.2 5.7 %copy-start.2 = (bf16[256,3]{0,1:T(4,128)(2,1)S(1)}, bf16[256,3]{0,1:T(4,128)(2,1)}, u32[]{:S(2)}) copy-start(bf16[256,3]{0,1:T(4,128)(2,1)} %param.19) | copy-start | bytes 4612
  5.3 47.6 %all-to-all-start = ((bf16[8,384,384]{2,1,0:T(8,128)(2,1)}), bf16[8,384,384]{2,1,0:T(8,128)(2,1)S(1)}, u32[]{:S(2)}, u32[]{:S(2)}) async-start(bf16[8,384,384]{2,1,0:T(8,128)(2,1)} %split_columns.1), calls=%async_computation | async-start | bytes 4718592 | tf_op jit(solution)/shard_map/all_to_all | solution.py:447
  31.8 5.6 %collective-permute-start.1 = (bf16[8,640]{1,0:T(8,128)(2,1)}, bf16[8,640]{1,0:T(8,128)(2,1)S(1)}, u32[]{:S(2)}, u32[]{:S(2)}) collective-permute-start(bf16[8,640]{1,0:T(8,128)(2,1)} %get-tuple-element.19), channel_id=1, source_target_pairs={{0,16},{16,32},{32,48},{48,0},{1,17},{17,33},{33,49},{49,1},{2,18}... | collective-permute-start | bytes 30728 | tf_op jit(solution)/shard_map/ppermute | solution.py:437
  33.1 4.5 %collective-permute-start.2 = (bf16[8,640]{1,0:T(8,128)(2,1)}, bf16[8,640]{1,0:T(8,128)(2,1)S(1)}, u32[]{:S(2)}, u32[]{:S(2)}) collective-permute-start(bf16[8,640]{1,0:T(8,128)(2,1)} %get-tuple-element.19), channel_id=1, source_target_pairs={{0,32},{16,48},{32,0},{48,16},{1,33},{17,49},{33,1},{49,17},{2,34}... | collective-permute-start | bytes 30728 | tf_op jit(solution)/shard_map/ppermute | solution.py:437
  35.5 3.0 %collective-permute-start.3 = (bf16[8,640]{1,0:T(8,128)(2,1)}, bf16[8,640]{1,0:T(8,128)(2,1)S(1)}, u32[]{:S(2)}, u32[]{:S(2)}) collective-permute-start(bf16[8,640]{1,0:T(8,128)(2,1)} %get-tuple-element.19), channel_id=1, source_target_pairs={{0,48},{16,0},{32,16},{48,32},{1,49},{17,1},{33,17},{49,33},{2,50}... | collective-permute-start | bytes 30728 | tf_op jit(solution)/shard_map/ppermute | solution.py:437
  39.2 4.7 %collective-permute-start.4 = (bf16[32,640]{1,0:T(8,128)(2,1)S(1)}, bf16[32,640]{1,0:T(8,128)(2,1)S(1)}, u32[]{:S(2)}, u32[]{:S(2)}) collective-permute-start(bf16[32,640]{1,0:T(8,128)(2,1)S(1)} %pad_maximum_fusion), channel_id=1, source_target_pairs={{0,64},{64,0},{1,65},{65,1},{2,66},{66,2},{3,67},{67,3},{4,68},{68... | collective-permute-start | bytes 122888 | tf_op jit(solution)/shard_map/ppermute | solution.py:437
  44.0 3.8 %collective-permute-start.5 = (bf16[64,640]{1,0:T(8,128)(2,1)S(1)}, bf16[64,640]{1,0:T(8,128)(2,1)S(1)}, u32[]{:S(2)}, u32[]{:S(2)}) collective-permute-start(bf16[64,640]{1,0:T(8,128)(2,1)S(1)} %get-tuple-element.32), channel_id=1, source_target_pairs={{0,8},{8,0},{1,9},{9,1},{2,10},{10,2},{3,11},{11,3},{4,12},{12,4},... | collective-permute-start | bytes 245768 | tf_op jit(solution)/shard_map/ppermute | solution.py:437
  47.8 13.4 %copy-start.3 = (bf16[128,640]{1,0:T(8,128)(2,1)}, bf16[128,640]{1,0:T(8,128)(2,1)S(1)}, u32[]{:S(2)}) copy-start(bf16[128,640]{1,0:T(8,128)(2,1)S(1)} %constant_dynamic-update-slice_fusion.5.piece0) | copy-start | bytes 491524
  47.8 5.5 %collective-permute-start.6 = (bf16[128,640]{1,0:T(8,128)(2,1)S(1)}, bf16[128,640]{1,0:T(8,128)(2,1)S(1)}, u32[]{:S(2)}, u32[]{:S(2)}) collective-permute-start(bf16[128,640]{1,0:T(8,128)(2,1)S(1)} %constant_dynamic-update-slice_fusion.5.piece0), channel_id=1, source_target_pairs={{0,2},{2,4},{4,6},{6,0},{1,3},{3,5},{5,7},{7,1},{8,10},{10,12},{12... | collective-permute-start | bytes 491528 | tf_op jit(solution)/shard_map/ppermute | solution.py:437
  49.3 7.0 %collective-permute-start.7 = (bf16[128,640]{1,0:T(8,128)(2,1)S(1)}, bf16[128,640]{1,0:T(8,128)(2,1)S(1)}, u32[]{:S(2)}, u32[]{:S(2)}) collective-permute-start(bf16[128,640]{1,0:T(8,128)(2,1)S(1)} %constant_dynamic-update-slice_fusion.5.piece0), channel_id=1, source_target_pairs={{0,4},{2,6},{4,0},{6,2},{1,5},{3,7},{5,1},{7,3},{8,12},{10,14},{12... | collective-permute-start | bytes 491528 | tf_op jit(solution)/shard_map/ppermute | solution.py:437
  51.8 4.6 %collective-permute-start.8 = (bf16[128,640]{1,0:T(8,128)(2,1)S(1)}, bf16[128,640]{1,0:T(8,128)(2,1)S(1)}, u32[]{:S(2)}, u32[]{:S(2)}) collective-permute-start(bf16[128,640]{1,0:T(8,128)(2,1)S(1)} %constant_dynamic-update-slice_fusion.5.piece0), channel_id=1, source_target_pairs={{0,6},{2,0},{4,2},{6,4},{1,7},{3,1},{5,3},{7,5},{8,14},{10,8},{12,... | collective-permute-start | bytes 491528 | tf_op jit(solution)/shard_map/ppermute | solution.py:437
  52.9 8.3 %copy-start = (bf16[8,384,384]{2,1,0:T(8,128)(2,1)}, bf16[8,384,384]{2,1,0:T(8,128)(2,1)S(1)}, u32[]{:S(2)}) copy-start(bf16[8,384,384]{2,1,0:T(8,128)(2,1)S(1)} %all-to-all-done.mixer_hbm) | copy-start | bytes 7077892
  53.3 7.9 %copy-start.5 = (bf16[128,640]{1,0:T(8,128)(2,1)}, bf16[128,640]{1,0:T(8,128)(2,1)S(1)}, u32[]{:S(2)}) copy-start(bf16[128,640]{1,0:T(8,128)(2,1)S(1)} %collective-permute-done.6.piece1) | copy-start | bytes 491524
  56.4 4.8 %copy-start.6 = (bf16[128,640]{1,0:T(8,128)(2,1)}, bf16[128,640]{1,0:T(8,128)(2,1)S(1)}, u32[]{:S(2)}) copy-start(bf16[128,640]{1,0:T(8,128)(2,1)S(1)} %collective-permute-done.7.piece2) | copy-start | bytes 491524
  56.4 4.8 %copy-start.7 = (bf16[128,640]{1,0:T(8,128)(2,1)}, bf16[128,640]{1,0:T(8,128)(2,1)S(1)}, u32[]{:S(2)}) copy-start(bf16[128,640]{1,0:T(8,128)(2,1)S(1)} %collective-permute-done.8.piece3) | copy-start | bytes 491524
  56.4 14.1 %collective-permute-start.9 = (bf16[8,384,384]{2,1,0:T(8,128)(2,1)S(1)}, bf16[8,384,384]{2,1,0:T(8,128)(2,1)S(1)}, u32[]{:S(2)}, u32[]{:S(2)}) collective-permute-start(bf16[8,384,384]{2,1,0:T(8,128)(2,1)S(1)} %all-to-all-done.mixer_hbm), channel_id=1, source_target_pairs={{0,1},{1,0},{2,3},{3,2},{4,5},{5,4},{6,7},{7,6},{8,9},{9,8},{10,11... | collective-permute-start | bytes 7077896 | tf_op jit(solution)/shard_map/ppermute | solution.py:441
  70.5 1.5 copy-start.4
  125.6 15.8 %copy-start.8 = (bf16[64,384]{1,0:T(8,128)(2,1)S(1)}, bf16[64,384]{1,0:T(8,128)(2,1)}, u32[]{:S(2)}) copy-start(bf16[64,384]{1,0:T(8,128)(2,1)} %get-tuple-element.31) | copy-start | bytes 147460
  132.2 23.8 %copy-start.1 = (bf16[64,384]{1,0:T(8,128)(2,1)S(1)}, bf16[64,384]{1,0:T(8,128)(2,1)}, u32[]{:S(2)}) copy-start(bf16[64,384]{1,0:T(8,128)(2,1)} %get-tuple-element.30) | copy-start | bytes 147460
  132.2 23.7 %all-to-all-start.2 = ((bf16[16,64,384]{2,1,0:T(8,128)(2,1)}), bf16[16,64,384]{2,1,0:T(8,128)(2,1)S(1)}, u32[]{:S(2)}, u32[]{:S(2)}) async-start(bf16[16,64,384]{2,1,0:T(8,128)(2,1)} %mlp_out.1), calls=%async_computation.2 | async-start | bytes 1572864 | tf_op jit(solution)/shard_map/all_to_all | solution.py:464
  141.4 14.6 %collective-permute-start.10 = (bf16[64,384]{1,0:T(8,128)(2,1)S(1)}, bf16[64,384]{1,0:T(8,128)(2,1)S(1)}, u32[]{:S(2)}, u32[]{:S(2)}) collective-permute-start(bf16[64,384]{1,0:T(8,128)(2,1)S(1)} %copy-done.8), channel_id=1, source_target_pairs={{0,1},{1,0},{2,3},{3,2},{4,5},{5,4},{6,7},{7,6},{8,9},{9,8},{10,11... | collective-permute-start | bytes 147464 | tf_op jit(solution)/shard_map/ppermute | solution.py:441

commit v6 on v5

--- a/solution.py
+++ b/solution.py
@@ -346,7 +346,7 @@
             pltpu.SemaphoreType.DMA((blocks,)),
             pltpu.SemaphoreType.DMA((8,)),
         ],
-        compiler_params=pltpu.CompilerParams(vmem_limit_bytes=58 << 20),
+        compiler_params=pltpu.CompilerParams(vmem_limit_bytes=40 << 20),
         cost_estimate=pl.CostEstimate(flops=3_500_000_000, transcendentals=100_000, bytes_accessed=8_000_000),
         name="embed_mate" if flip else "embed_own",
     )(*pieces, weight, bias, mixer, *carry)
@@ -402,7 +402,7 @@
             pltpu.VMEM((tokens, 2 * span), f32),
             pltpu.SemaphoreType.DMA((blocks // 2, 4)),
         ],
-        compiler_params=pltpu.CompilerParams(vmem_limit_bytes=58 << 20),
+        compiler_params=pltpu.CompilerParams(vmem_limit_bytes=24 << 20),
         cost_estimate=pl.CostEstimate(flops=2_400_000_000, transcendentals=0, bytes_accessed=9_000_000),
         name="mlp_out",
     )(hidden, own, mate)

time: 157 us -> 153 us (0.975)
  Pallas kernels: 50.7 us -> 44.7 us
  local copies, waits for them, and re-layouts: 3.69 us -> 5.28 us
    pallas_call x2, Pallas kernels: 20.8 us -> 15 us  [embed_call(): pl.pallas_call(functools.partial(embed_kernel, flip), out_shape=shapes, i...]
    unnamed x23 -> x13, local copies, waits for them, and re-layouts: 3.01 us -> 4.6 us
  transfers between devices with their start and end apart: 13 -> 13, of which waited for: 7 -> 7; matrix products, arithmetic and copies ran while one was open for 2% -> 2% of each run, Pallas kernels for 21% -> 20%
where the time goes in v6:
time: 153 us; the launch traced here: 152 us
  Pallas kernels  44.7 us (29%)
  blocking collectives  42.8 us (28%)
  starting transfers between devices  34.7 us (23%)
  waiting for transfers between devices  22.9 us (15%)
  local copies, waits for them, and re-layouts  5.28 us (3%)
    all_to_all x1, blocking collectives, on_device(): hidden = lax.all_to_all(hidden, ('zl', 'y'), 0, 0)  42.8 us
    pallas_call x1, Pallas kernels, score_call(): pl.pallas_call(functools.partial(score_kernel, side, count), out_shape=(j...  20.3 us
    pallas_call x2, Pallas kernels, embed_call(): pl.pallas_call(functools.partial(embed_kernel, flip), out_shape=shapes, i...  15 us
    ppermute x8, starting transfers between devices, shift(): return lax.ppermute(value, axis, [(i, (i + k) % n) for i in range(n)])  14.5 us
    all_to_all x1, waiting for transfers between devices, on_device(): shares = lax.all_to_all(shares, ('zh', 'x', 'core'), 0, 0)  14.3 us
    ppermute x8, waiting for transfers between devices, shift(): return lax.ppermute(value, axis, [(i, (i + k) % n) for i in range(n)])  8.57 us
    all_to_all x1, starting transfers between devices, on_device(): shares = lax.all_to_all(shares, ('zh', 'x', 'core'), 0, 0)  8.12 us
    ppermute x3, starting transfers between devices, swap(): return lax.ppermute(value, 'core', [(0, 1), (1, 0)])  6.49 us
  transfers between devices with their start and end apart: 13, of which 7 were waited for; matrix products, arithmetic and copies ran while one was open for 2% of the time, Pallas kernels for 20%

profile of v6, /device:TPU:1, one launch (start us, length us, event | category | flops | bytes accessed | tf_op | source)
XLA Modules:
  0.0 152.0 jit_solution(14077049864724013700)
XLA Ops:
  0.6 1.5 collective-permute-start
  2.1 3.1 %split_columns.1 = bf16[8,384,384]{2,1,0:T(8,128)(2,1)} custom-call(bf16[384,3072]{1,0:T(8,128)(2,1)} %whole.1), custom_call_target="tpu_custom_call" | custom-call | bytes 4718592 | tf_op jit(solution)/shard_map/split_columns/pallas_call | solution.py:423
  5.3 5.6 %all-to-all-start = ((bf16[8,384,384]{2,1,0:T(8,128)(2,1)}), bf16[8,384,384]{2,1,0:T(8,128)(2,1)S(1)}, u32[]{:S(2)}, u32[]{:S(2)}) async-start(bf16[8,384,384]{2,1,0:T(8,128)(2,1)} %split_columns.1), calls=%async_computation | async-start | bytes 4718592 | tf_op jit(solution)/shard_map/all_to_all | solution.py:447
  10.9 0.8 copy.14.out_w
  11.7 20.3 %score_net.1 = (f32[28,3,2,28]{3,2,1,0:T(2,128)}, bf16[8,640]{1,0:T(8,128)(2,1)}) custom-call(f32[28,3,2,28]{3,2,1,0:T(2,128)} %bitcast.17, f32[28,3,2,28]{3,2,1,0:T(2,128)} %bitcast.18, bf16[27,256]{1,0:T(8,128)(2,1)} %stem_w.1, bf16[4,2304,256]{2,1,0:T(8,128)(2,1)} %l1_hbm.1, bf16[1024,256]{1,0:T(8,128)(2,1)} %down_hbm.1, bf16[2,2304,256]{2,1,0:T(8,128)(2,1)} %l2_hbm.1, ...), custom_call_target="tpu_custom_call" | custom-call | flops 10000000000 | bytes 12000000 | tf_op jit(solution)/shard_map/score_net/pallas_call | solution.py:217
  32.0 1.3 collective-permute-start.1
  33.2 2.4 %collective-permute-start.2 = (bf16[8,640]{1,0:T(8,128)(2,1)}, bf16[8,640]{1,0:T(8,128)(2,1)S(1)}, u32[]{:S(2)}, u32[]{:S(2)}) collective-permute-start(bf16[8,640]{1,0:T(8,128)(2,1)} %get-tuple-element.19), channel_id=1, source_target_pairs={{0,32},{16,48},{32,0},{48,16},{1,33},{17,49},{33,1},{49,17},{2,34}... | collective-permute-start | bytes 30728 | tf_op jit(solution)/shard_map/ppermute | solution.py:437
  35.7 1.2 collective-permute-start.3
  36.8 0.7 constant_dynamic-update-slice_fusion.4
  37.6 0.2 collective-permute-done.2
  37.8 0.9 collective-permute-done.3
  38.7 0.7 pad_maximum_fusion
  39.4 3.3 %collective-permute-start.4 = (bf16[32,640]{1,0:T(8,128)(2,1)S(1)}, bf16[32,640]{1,0:T(8,128)(2,1)S(1)}, u32[]{:S(2)}, u32[]{:S(2)}) collective-permute-start(bf16[32,640]{1,0:T(8,128)(2,1)S(1)} %pad_maximum_fusion), channel_id=1, source_target_pairs={{0,64},{64,0},{1,65},{65,1},{2,66},{66,2},{3,67},{67,3},{4,68},{68... | collective-permute-start | bytes 122888 | tf_op jit(solution)/shard_map/ppermute | solution.py:437
  42.8 1.4 collective-permute-done.4
  44.1 1.2 collective-permute-start.5
  45.3 2.6 %collective-permute-done.5 = bf16[64,640]{1,0:T(8,128)(2,1)S(1)} collective-permute-done((bf16[64,640]{1,0:T(8,128)(2,1)S(1)}, bf16[64,640]{1,0:T(8,128)(2,1)S(1)}, u32[]{:S(2)}, u32[]{:S(2)}) %collective-permute-start.5) | collective-permute-done | bytes 81952 | tf_op jit(solution)/shard_map/ppermute | solution.py:437
  48.0 1.5 %collective-permute-start.6 = (bf16[128,640]{1,0:T(8,128)(2,1)S(1)}, bf16[128,640]{1,0:T(8,128)(2,1)S(1)}, u32[]{:S(2)}, u32[]{:S(2)}) collective-permute-start(bf16[128,640]{1,0:T(8,128)(2,1)S(1)} %constant_dynamic-update-slice_fusion.5.piece0), channel_id=1, source_target_pairs={{0,2},{2,4},{4,6},{6,0},{1,3},{3,5},{5,7},{7,1},{8,10},{10,12},{12... | collective-permute-start | bytes 491528 | tf_op jit(solution)/shard_map/ppermute | solution.py:437
  49.5 2.5 %collective-permute-start.7 = (bf16[128,640]{1,0:T(8,128)(2,1)S(1)}, bf16[128,640]{1,0:T(8,128)(2,1)S(1)}, u32[]{:S(2)}, u32[]{:S(2)}) collective-permute-start(bf16[128,640]{1,0:T(8,128)(2,1)S(1)} %constant_dynamic-update-slice_fusion.5.piece0), channel_id=1, source_target_pairs={{0,4},{2,6},{4,0},{6,2},{1,5},{3,7},{5,1},{7,3},{8,12},{10,14},{12... | collective-permute-start | bytes 491528 | tf_op jit(solution)/shard_map/ppermute | solution.py:437
  52.0 1.1 collective-permute-start.8
  53.1 0.4 collective-permute-done.6.piece1
  53.5 3.0 %collective-permute-done.7.piece2 = bf16[128,640]{1,0:T(8,128)(2,1)S(1)} collective-permute-done((bf16[128,640]{1,0:T(8,128)(2,1)S(1)}, bf16[128,640]{1,0:T(8,128)(2,1)S(1)}, u32[]{:S(2)}, u32[]{:S(2)}) %collective-permute-start.7) | collective-permute-done | bytes 163872 | tf_op jit(solution)/shard_map/ppermute | solution.py:437
  56.5 4.8 %collective-permute-start.9 = (bf16[8,384,384]{2,1,0:T(8,128)(2,1)S(1)}, bf16[8,384,384]{2,1,0:T(8,128)(2,1)S(1)}, u32[]{:S(2)}, u32[]{:S(2)}) collective-permute-start(bf16[8,384,384]{2,1,0:T(8,128)(2,1)S(1)} %all-to-all-done.mixer_hbm), channel_id=1, source_target_pairs={{0,1},{1,0},{2,3},{3,2},{4,5},{5,4},{6,7},{7,6},{8,9},{9,8},{10,11... | collective-permute-start | bytes 7077896 | tf_op jit(solution)/shard_map/ppermute | solution.py:441
  61.3 3.1 %copy-done = bf16[588,6144]{1,0:T(8,128)(2,1)S(1)} copy-done((bf16[588,6144]{1,0:T(8,128)(2,1)S(1)}, bf16[588,6144]{1,0:T(8,128)(2,1)}, u32[]{:S(2)}) %copy-start) | copy-done | bytes 7225368
  64.4 7.0 %embed_own.1 = (f32[528,384]{1,0:T(8,128)S(1)}, f32[512,128]{1,0:T(8,128)S(1)}, f32[512,128]{1,0:T(8,128)S(1)}, bf16[64,384]{1,0:T(8,128)(2,1)S(1)}) custom-call(bf16[128,640]{1,0:T(8,128)(2,1)S(1)} %constant_dynamic-update-slice_fusion.5.piece0, bf16[128,640]{1,0:T(8,128)(2,1)S(1)} %collective-permute-done.6.piece1, ...), custom_call_target="tpu_custom_call" | custom-call | flops 3500000000 | bytes 8000000 | tf_op jit(solution)/shard_map/embed_own/pallas_call | solution.py:335
  71.4 8.1 %embed_mate.1 = (bf16[8,512,384]{2,1,0:T(8,128)(2,1)S(1)}, bf16[64,384]{1,0:T(8,128)(2,1)S(1)}) custom-call(bf16[128,640]{1,0:T(8,128)(2,1)S(1)} %constant_dynamic-update-slice_fusion.5.piece0, bf16[128,640]{1,0:T(8,128)(2,1)S(1)} %collective-permute-done.6.piece1, bf16[128,640]{1,0:T(8,128)(2,1)S(1)} %collective-permute-done.7.piece2, ...), custom_call_target="tpu_custom_call" | custom-call | flops 3500000000 | bytes 8000000 | tf_op jit(solution)/shard_map/embed_mate/pallas_call | solution.py:335
  79.5 42.8 %all_to_all.15.hidden_hbm = bf16[8,512,384]{2,1,0:T(8,128)(2,1)S(1)} all-to-all(bf16[8,512,384]{2,1,0:T(8,128)(2,1)S(1)} %get-tuple-element.28), channel_id=1, replica_groups=mesh['zh'=2,'x'=4,'zl'=2,'y'=4,'core'=2] {'zl','y'}, dimensions={0} | all-to-all | bytes 6291456 | tf_op jit(solution)/shard_map/all_to_all | solution.py:462
  122.3 6.3 %mlp_out.1 = bf16[16,64,384]{2,1,0:T(8,128)(2,1)} custom-call(bf16[8,512,384]{2,1,0:T(8,128)(2,1)S(1)} %all_to_all.15.hidden_hbm, bf16[3072,384]{1,0:T(8,128)(2,1)S(1)} %copy-done.1, bf16[3072,384]{1,0:T(8,128)(2,1)} %collective-permute-done.mate_hbm), custom_call_target="tpu_custom_call" | custom-call | flops 2400000000 | bytes 9000000 | tf_op jit(solution)/shard_map/mlp_out/pallas_call | solution.py:394
  128.6 8.1 %all-to-all-start.2 = ((bf16[16,64,384]{2,1,0:T(8,128)(2,1)}), bf16[16,64,384]{2,1,0:T(8,128)(2,1)S(1)}, u32[]{:S(2)}, u32[]{:S(2)}) async-start(bf16[16,64,384]{2,1,0:T(8,128)(2,1)} %mlp_out.1), calls=%async_computation.2 | async-start | bytes 1572864 | tf_op jit(solution)/shard_map/all_to_all | solution.py:464
  136.7 0.2 collective-permute-start.10
  136.9 14.3 %all-to-all-done.2 = bf16[16,64,384]{2,1,0:T(8,128)(2,1)S(1)} async-done(((bf16[16,64,384]{2,1,0:T(8,128)(2,1)}), bf16[16,64,384]{2,1,0:T(8,128)(2,1)S(1)}, u32[]{:S(2)}, u32[]{:S(2)}) %all-to-all-start.2) | async-done | bytes 786464 | tf_op jit(solution)/shard_map/all_to_all | solution.py:464
  151.2 0.1 convert_reduce_fusion
  151.4 0.7 copy.15
  (19 shorter events, 0.1 us)
Async XLA Ops:
  0.6 31.3 %collective-permute-start = (bf16[3072,384]{1,0:T(8,128)(2,1)}, bf16[3072,384]{1,0:T(8,128)(2,1)}, u32[]{:S(2)}, u32[]{:S(2)}) collective-permute-start(bf16[3072,384]{1,0:T(8,128)(2,1)} %own_hbm.1), channel_id=1, source_target_pairs={{0,1},{1,0},{2,3},{3,2},{4,5},{5,4},{6,7},{7,6},{8,9},{9,8},{10,11... | collective-permute-start | bytes 7077896 | tf_op jit(solution)/shard_map/ppermute | solution.py:441
  5.2 5.7 %copy-start.3 = (bf16[256,3]{0,1:T(4,128)(2,1)S(1)}, bf16[256,3]{0,1:T(4,128)(2,1)}, u32[]{:S(2)}) copy-start(bf16[256,3]{0,1:T(4,128)(2,1)} %param.19) | copy-start | bytes 4612
  5.3 47.8 %all-to-all-start = ((bf16[8,384,384]{2,1,0:T(8,128)(2,1)}), bf16[8,384,384]{2,1,0:T(8,128)(2,1)S(1)}, u32[]{:S(2)}, u32[]{:S(2)}) async-start(bf16[8,384,384]{2,1,0:T(8,128)(2,1)} %split_columns.1), calls=%async_computation | async-start | bytes 4718592 | tf_op jit(solution)/shard_map/all_to_all | solution.py:447
  11.7 49.7 %copy-start.2 = (f32[6144]{0:T(1024)S(1)}, f32[6144]{0:T(1024)}, u32[]{:S(2)}) copy-start(f32[6144]{0:T(1024)} %param.21) | copy-start | bytes 73732
  32.0 5.6 %collective-permute-start.1 = (bf16[8,640]{1,0:T(8,128)(2,1)}, bf16[8,640]{1,0:T(8,128)(2,1)S(1)}, u32[]{:S(2)}, u32[]{:S(2)}) collective-permute-start(bf16[8,640]{1,0:T(8,128)(2,1)} %get-tuple-element.19), channel_id=1, source_target_pairs={{0,16},{16,32},{32,48},{48,0},{1,17},{17,33},{33,49},{49,1},{2,18}... | collective-permute-start | bytes 30728 | tf_op jit(solution)/shard_map/ppermute | solution.py:437
  33.2 4.5 %collective-permute-start.2 = (bf16[8,640]{1,0:T(8,128)(2,1)}, bf16[8,640]{1,0:T(8,128)(2,1)S(1)}, u32[]{:S(2)}, u32[]{:S(2)}) collective-permute-start(bf16[8,640]{1,0:T(8,128)(2,1)} %get-tuple-element.19), channel_id=1, source_target_pairs={{0,32},{16,48},{32,0},{48,16},{1,33},{17,49},{33,1},{49,17},{2,34}... | collective-permute-start | bytes 30728 | tf_op jit(solution)/shard_map/ppermute | solution.py:437
  35.7 3.0 %collective-permute-start.3 = (bf16[8,640]{1,0:T(8,128)(2,1)}, bf16[8,640]{1,0:T(8,128)(2,1)S(1)}, u32[]{:S(2)}, u32[]{:S(2)}) collective-permute-start(bf16[8,640]{1,0:T(8,128)(2,1)} %get-tuple-element.19), channel_id=1, source_target_pairs={{0,48},{16,0},{32,16},{48,32},{1,49},{17,1},{33,17},{49,33},{2,50}... | collective-permute-start | bytes 30728 | tf_op jit(solution)/shard_map/ppermute | solution.py:437
  39.4 4.7 %collective-permute-start.4 = (bf16[32,640]{1,0:T(8,128)(2,1)S(1)}, bf16[32,640]{1,0:T(8,128)(2,1)S(1)}, u32[]{:S(2)}, u32[]{:S(2)}) collective-permute-start(bf16[32,640]{1,0:T(8,128)(2,1)S(1)} %pad_maximum_fusion), channel_id=1, source_target_pairs={{0,64},{64,0},{1,65},{65,1},{2,66},{66,2},{3,67},{67,3},{4,68},{68... | collective-permute-start | bytes 122888 | tf_op jit(solution)/shard_map/ppermute | solution.py:437
  44.1 3.8 %collective-permute-start.5 = (bf16[64,640]{1,0:T(8,128)(2,1)S(1)}, bf16[64,640]{1,0:T(8,128)(2,1)S(1)}, u32[]{:S(2)}, u32[]{:S(2)}) collective-permute-start(bf16[64,640]{1,0:T(8,128)(2,1)S(1)} %get-tuple-element.32), channel_id=1, source_target_pairs={{0,8},{8,0},{1,9},{9,1},{2,10},{10,2},{3,11},{11,3},{4,12},{12,4},... | collective-permute-start | bytes 245768 | tf_op jit(solution)/shard_map/ppermute | solution.py:437
  48.0 5.5 %collective-permute-start.6 = (bf16[128,640]{1,0:T(8,128)(2,1)S(1)}, bf16[128,640]{1,0:T(8,128)(2,1)S(1)}, u32[]{:S(2)}, u32[]{:S(2)}) collective-permute-start(bf16[128,640]{1,0:T(8,128)(2,1)S(1)} %constant_dynamic-update-slice_fusion.5.piece0), channel_id=1, source_target_pairs={{0,2},{2,4},{4,6},{6,0},{1,3},{3,5},{5,7},{7,1},{8,10},{10,12},{12... | collective-permute-start | bytes 491528 | tf_op jit(solution)/shard_map/ppermute | solution.py:437
  49.5 7.0 %collective-permute-start.7 = (bf16[128,640]{1,0:T(8,128)(2,1)S(1)}, bf16[128,640]{1,0:T(8,128)(2,1)S(1)}, u32[]{:S(2)}, u32[]{:S(2)}) collective-permute-start(bf16[128,640]{1,0:T(8,128)(2,1)S(1)} %constant_dynamic-update-slice_fusion.5.piece0), channel_id=1, source_target_pairs={{0,4},{2,6},{4,0},{6,2},{1,5},{3,7},{5,1},{7,3},{8,12},{10,14},{12... | collective-permute-start | bytes 491528 | tf_op jit(solution)/shard_map/ppermute | solution.py:437
  52.0 4.6 %collective-permute-start.8 = (bf16[128,640]{1,0:T(8,128)(2,1)S(1)}, bf16[128,640]{1,0:T(8,128)(2,1)S(1)}, u32[]{:S(2)}, u32[]{:S(2)}) collective-permute-start(bf16[128,640]{1,0:T(8,128)(2,1)S(1)} %constant_dynamic-update-slice_fusion.5.piece0), channel_id=1, source_target_pairs={{0,6},{2,0},{4,2},{6,4},{1,7},{3,1},{5,3},{7,5},{8,14},{10,8},{12,... | collective-permute-start | bytes 491528 | tf_op jit(solution)/shard_map/ppermute | solution.py:437
  56.5 14.9 %collective-permute-start.9 = (bf16[8,384,384]{2,1,0:T(8,128)(2,1)S(1)}, bf16[8,384,384]{2,1,0:T(8,128)(2,1)S(1)}, u32[]{:S(2)}, u32[]{:S(2)}) collective-permute-start(bf16[8,384,384]{2,1,0:T(8,128)(2,1)S(1)} %all-to-all-done.mixer_hbm), channel_id=1, source_target_pairs={{0,1},{1,0},{2,3},{3,2},{4,5},{5,4},{6,7},{7,6},{8,9},{9,8},{10,11... | collective-permute-start | bytes 7077896 | tf_op jit(solution)/shard_map/ppermute | solution.py:441
  61.3 3.1 %copy-start = (bf16[588,6144]{1,0:T(8,128)(2,1)S(1)}, bf16[588,6144]{1,0:T(8,128)(2,1)}, u32[]{:S(2)}) copy-start(bf16[588,6144]{1,0:T(8,128)(2,1)} %weight_hbm.3) | copy-start | bytes 21676036
  79.5 42.8 %copy-start.1 = (bf16[3072,384]{1,0:T(8,128)(2,1)S(1)}, bf16[3072,384]{1,0:T(8,128)(2,1)}, u32[]{:S(2)}) copy-start(bf16[3072,384]{1,0:T(8,128)(2,1)} %own_hbm.1) | copy-start | bytes 7077892
  128.6 22.6 %all-to-all-start.2 = ((bf16[16,64,384]{2,1,0:T(8,128)(2,1)}), bf16[16,64,384]{2,1,0:T(8,128)(2,1)S(1)}, u32[]{:S(2)}, u32[]{:S(2)}) async-start(bf16[16,64,384]{2,1,0:T(8,128)(2,1)} %mlp_out.1), calls=%async_computation.2 | async-start | bytes 1572864 | tf_op jit(solution)/shard_map/all_to_all | solution.py:464
  136.7 14.6 %collective-permute-start.10 = (bf16[64,384]{1,0:T(8,128)(2,1)S(1)}, bf16[64,384]{1,0:T(8,128)(2,1)S(1)}, u32[]{:S(2)}, u32[]{:S(2)}) collective-permute-start(bf16[64,384]{1,0:T(8,128)(2,1)S(1)} %get-tuple-element.31), channel_id=1, source_target_pairs={{0,1},{1,0},{2,3},{3,2},{4,5},{5,4},{6,7},{7,6},{8,9},{9,8},{10,11... | collective-permute-start | bytes 147464 | tf_op jit(solution)/shard_map/ppermute | solution.py:441

commit v7 on v6

--- a/solution.py
+++ b/solution.py
@@ -313,8 +313,7 @@
         scale = lax.rsqrt(square - mean * mean + ln_epsilon)
         column = total[tokens:tokens + 1, :]
         value = gelu((total[0:tokens, :] - mean * column) * scale).astype(bf16)
-        for b in range(hidden.shape[0]):
-            hidden[b] = value
+        hidden[...] = value
 
 
 def embed_call(pieces, weight, bias, mixer, carry):
@@ -327,7 +326,7 @@
     vm = pl.BlockSpec(memory_space=pltpu.VMEM)
     hb = pl.BlockSpec(memory_space=pltpu.HBM)
     if flip:
-        shapes = (jax.ShapeDtypeStruct((8, tokens, width), bf16), sent)
+        shapes = (jax.ShapeDtypeStruct((tokens, width), bf16), sent)
         scratch = [pltpu.VMEM(shape, f32) for shape in state]
     else:
         shapes = tuple(jax.ShapeDtypeStruct(shape, f32) for shape in state) + (sent,)
@@ -352,33 +351,33 @@
     )(*pieces, weight, bias, mixer, *carry)
 
 
-def mix_kernel(hidden_hbm, own_hbm, mate_hbm, out, hidden, weight, total, sems):
+def mix_kernel(places, begin, end, *refs):
+    refs = list(refs)
+    total_in = None if begin else refs.pop(0)
+    hidden = [refs.pop(0) for _ in places]
+    own_hbm, mate_hbm, out, weight, sems = refs
     core = lax.axis_index("core")
-    blocks, tokens, width = hidden_hbm.shape
+    level, line, lines = lax.axis_index("zl"), lax.axis_index("y"), lax.axis_size("y")
     span = own_hbm.shape[1]
-    parts = blocks // 2
-    deep = 2 * width
+    width = hidden[0].shape[1]
     loads = []
-    for k in range(parts):
-        rows = pl.ds(k * deep, deep)
-        pairs = [(own_hbm.at[rows, :], weight.at[rows, pl.ds(0, span)]),
-                 (mate_hbm.at[rows, :], weight.at[rows, pl.ds(span, span)])]
-        pairs += [(hidden_hbm.at[b], hidden.at[:, pl.ds(b * width, width)]) for b in (2 * k, 2 * k + 1)]
-        loads.append([pltpu.make_async_copy(a, b, sems.at[k, n]) for n, (a, b) in enumerate(pairs)])
-        for load in loads[-1]:
-            load.start()
-    for k in range(parts):
-        for load in loads[k]:
-            load.wait()
-        at = slice(k * deep, (k + 1) * deep)
-        part = jnp.dot(hidden[:, at], weight[at, :], preferred_element_type=f32)
-        if k == 0:
-            total[...] = part
-        elif k < parts - 1:
-            total[...] += part
-        else:
-            done = total[...] + part
+    for n, (z, y) in enumerate(places):
+        at = ((level + z) % 2 * lines + (line + y) % lines) * width
+        for k, source in enumerate((own_hbm, mate_hbm)):
+            loads.append(pltpu.make_async_copy(source.at[pl.ds(pl.multiple_of(at, width), width), :],
+                                               weight.at[pl.ds(n * width, width), pl.ds(k * span, span)], sems.at[n, k]))
+            loads[-1].start()
+    for load in loads:
+        load.wait()
+    h = jnp.concatenate([block[...] for block in hidden], axis=1)
+    done = jnp.dot(h, weight[...], preferred_element_type=f32)
+    if not begin:
+        done += total_in[...]
+    if not end:
+        out[...] = done
+        return
     share = out.shape[1]
+    tokens = done.shape[0]
     high, across, size = lax.axis_index("zh"), lax.axis_index("x"), lax.axis_size("x")
     for q in range(tokens // share):
         rows = jnp.concatenate([done[b * share + q * 8:b * share + q * 8 + 8, :] for b in range(8)], axis=0).astype(bf16)
@@ -387,25 +386,29 @@
         out[2 * r + 1 - core] = rows[:, span:2 * span]
 
 
-def mix_call(hidden, own, mate):
-    blocks, tokens, width = hidden.shape
-    depth, span = own.shape
+def mix_call(total, blocks, own, mate, end=False):
+    places = tuple(place for place, _ in blocks)
+    hidden = [block for _, block in blocks]
+    tokens, width = hidden[0].shape
+    span = own.shape[1]
+    begin = total is None
+    shape = jax.ShapeDtypeStruct((16, tokens // 8, span), bf16) if end else jax.ShapeDtypeStruct((tokens, 2 * span), f32)
+    vm = pl.BlockSpec(memory_space=pltpu.VMEM)
     hb = pl.BlockSpec(memory_space=pltpu.HBM)
     return pl.pallas_call(
-        mix_kernel,
-        out_shape=jax.ShapeDtypeStruct((16, tokens // 8, span), bf16),
-        in_specs=[hb, hb, hb],
-        out_specs=pl.BlockSpec(memory_space=pltpu.VMEM),
+        functools.partial(mix_kernel, places, begin, end),
+        out_shape=shape,
+        in_specs=[vm] * (len(hidden) + (not begin)) + [hb, hb],
+        out_specs=vm,
         scratch_shapes=[
-            pltpu.VMEM((tokens, depth), bf16),
-            pltpu.VMEM((depth, 2 * span), bf16),
-            pltpu.VMEM((tokens, 2 * span), f32),
-            pltpu.SemaphoreType.DMA((blocks // 2, 4)),
+            pltpu.VMEM((len(places) * width, 2 * span), bf16),
+            pltpu.SemaphoreType.DMA((len(places), 2)),
         ],
         compiler_params=pltpu.CompilerParams(vmem_limit_bytes=24 << 20),
-        cost_estimate=pl.CostEstimate(flops=2_400_000_000, transcendentals=0, bytes_accessed=9_000_000),
-        name="mlp_out",
-    )(hidden, own, mate)
+        cost_estimate=pl.CostEstimate(flops=2 * len(places) * tokens * width * 2 * span, transcendentals=0,
+                                      bytes_accessed=len(places) * (tokens + 2 * span) * width * 2 + tokens * span * 8),
+        name="mlp_out_" + str(len(places)),
+    )(*([] if begin else [total]), *hidden, own, mate)
 
 
 def split_kernel(whole, blocks, sems):
@@ -459,8 +462,17 @@
     *carry, kept = embed_call(pieces, embed_weight, embed_bias[None], own_in, ())
     hidden, sent = embed_call(pieces, embed_weight, embed_bias[None], mate_in, tuple(carry))
     other = swap(sent)
-    hidden = lax.all_to_all(hidden, ("zl", "y"), 0, 0)
-    shares = mix_call(hidden, mlp_out, mate_out)
+    far = shift(hidden, "zl", 1)
+    below = shift(hidden, "y", 1)
+    above = shift(hidden, "y", 3)
+    across = shift(below, "y", 1)
+    far_above = shift(far, "y", 3)
+    far_below = shift(below, "zl", 1)
+    total = mix_call(None, [((0, 0), hidden), ((1, 0), far), ((0, 3), below), ((0, 1), above)], mlp_out, mate_out)
+    half = hidden.shape[0] // 2
+    last = jnp.concatenate([shift(far_below[:half], "y", 1), shift(far_above[half:], "y", 3)], axis=0)
+    total = mix_call(total, [((0, 2), across), ((1, 1), far_above), ((1, 3), far_below)], mlp_out, mate_out)
+    shares = mix_call(total, [((1, 2), last)], mlp_out, mate_out, end=True)
     shares = lax.all_to_all(shares, ("zh", "x", "core"), 0, 0)
     mixed = jnp.sum(shares.reshape(8, 2, 8, 8, span).astype(f32), axis=0)
     core = lax.axis_index("core")

time: 153 us -> 139 us (0.908)
  blocking collectives: 42.8 us -> 0 us
  waiting for transfers between devices: 22.9 us -> 41.7 us
  starting transfers between devices: 34.7 us -> 47.3 us
  Pallas kernels: 44.7 us -> 42.9 us
    all_to_all x1 -> x0, blocking collectives: 42.8 us -> none  [on_device(): hidden = lax.all_to_all(hidden, ('zl', 'y'), 0, 0)]
    ppermute x8 -> x16, waiting for transfers between devices: 8.57 us -> 27.4 us  [shift(): return lax.ppermute(value, axis, [(i, (i + k) % n) for i in range(n)])]
    ppermute x8 -> x16, starting transfers between devices: 14.5 us -> 25.9 us  [shift(): return lax.ppermute(value, axis, [(i, (i + k) % n) for i in range(n)])]
    pallas_call x1 -> x3, Pallas kernels: 6.28 us -> 4.85 us  [mix_call(): pl.pallas_call(functools.partial(mix_kernel, places, begin, end), out_sha...]
  transfers between devices with their start and end apart: 13 -> 21, of which waited for: 7 -> 11; matrix products, arithmetic and copies ran while one was open for 2% -> 2% of each run, Pallas kernels for 20% -> 24%
where the time goes in v7:
time: 139 us
  starting transfers between devices  47.3 us (34%)
  Pallas kernels  42.9 us (31%)
  waiting for transfers between devices  41.7 us (30%)
  local copies, waits for them, and re-layouts  5.32 us (4%)
    ppermute x16, waiting for transfers between devices, shift(): return lax.ppermute(value, axis, [(i, (i + k) % n) for i in range(n)])  27.4 us
    ppermute x16, starting transfers between devices, shift(): return lax.ppermute(value, axis, [(i, (i + k) % n) for i in range(n)])  25.9 us
    pallas_call x1, Pallas kernels, score_call(): pl.pallas_call(functools.partial(score_kernel, side, count), out_shape=(j...  20.1 us
    pallas_call x2, Pallas kernels, embed_call(): pl.pallas_call(functools.partial(embed_kernel, flip), out_shape=shapes, i...  14.8 us
    all_to_all x1, waiting for transfers between devices, on_device(): shares = lax.all_to_all(shares, ('zh', 'x', 'core'), 0, 0)  14.3 us
    all_to_all x1, starting transfers between devices, on_device(): shares = lax.all_to_all(shares, ('zh', 'x', 'core'), 0, 0)  9.27 us
    ppermute x3, starting transfers between devices, swap(): return lax.ppermute(value, 'core', [(0, 1), (1, 0)])  6.5 us
    all_to_all x1, starting transfers between devices, on_device(): own_in = lax.all_to_all(split_call(mlp_in, 8), ('zl', 'y'), 0, 0)  5.64 us
  transfers between devices with their start and end apart: 21, of which 11 were waited for; matrix products, arithmetic and copies ran while one was open for 2% of the time, Pallas kernels for 24%

profile of v7, /device:TPU:1, one launch (start us, length us, event | category | flops | bytes accessed | tf_op | source)
XLA Modules:
  0.0 138.9 jit_solution(11139337292025415375)
XLA Ops:
  0.6 1.5 %collective-permute-start = (bf16[3072,384]{1,0:T(8,128)(2,1)}, bf16[3072,384]{1,0:T(8,128)(2,1)S(1)}, u32[]{:S(2)}, u32[]{:S(2)}) collective-permute-start(bf16[3072,384]{1,0:T(8,128)(2,1)} %refs_2_.1), channel_id=1, source_target_pairs={{0,1},{1,0},{2,3},{3,2},{4,5},{5,4},{6,7},{7,6},{8,9},{9,8},{10,11... | collective-permute-start | bytes 7077896 | tf_op jit(solution)/shard_map/ppermute | solution.py:444
  2.1 3.1 %split_columns.1 = bf16[8,384,384]{2,1,0:T(8,128)(2,1)} custom-call(bf16[384,3072]{1,0:T(8,128)(2,1)} %whole.1), custom_call_target="tpu_custom_call" | custom-call | bytes 4718592 | tf_op jit(solution)/shard_map/split_columns/pallas_call | solution.py:426
  5.3 5.6 %all-to-all-start = ((bf16[8,384,384]{2,1,0:T(8,128)(2,1)}), bf16[8,384,384]{2,1,0:T(8,128)(2,1)}, u32[]{:S(2)}, u32[]{:S(2)}) async-start(bf16[8,384,384]{2,1,0:T(8,128)(2,1)} %split_columns.1), calls=%async_computation | async-start | bytes 4718592 | tf_op jit(solution)/shard_map/all_to_all | solution.py:450
  11.7 20.1 %score_net.1 = (f32[28,3,2,28]{3,2,1,0:T(2,128)}, bf16[8,640]{1,0:T(8,128)(2,1)}) custom-call(f32[28,3,2,28]{3,2,1,0:T(2,128)} %bitcast.17, f32[28,3,2,28]{3,2,1,0:T(2,128)} %bitcast.18, bf16[27,256]{1,0:T(8,128)(2,1)} %stem_w.1, bf16[4,2304,256]{2,1,0:T(8,128)(2,1)} %l1_hbm.1, bf16[1024,256]{1,0:T(8,128)(2,1)} %down_hbm.1, bf16[2,2304,256]{2,1,0:T(8,128)(2,1)} %l2_hbm.1, ...), custom_call_target="tpu_custom_call" | custom-call | flops 10000000000 | bytes 12000000 | tf_op jit(solution)/shard_map/score_net/pallas_call | solution.py:217
  31.8 1.3 collective-permute-start.1
  33.1 2.4 %collective-permute-start.2 = (bf16[8,640]{1,0:T(8,128)(2,1)}, bf16[8,640]{1,0:T(8,128)(2,1)S(1)}, u32[]{:S(2)}, u32[]{:S(2)}) collective-permute-start(bf16[8,640]{1,0:T(8,128)(2,1)} %get-tuple-element.19), channel_id=1, source_target_pairs={{0,32},{16,48},{32,0},{48,16},{1,33},{17,49},{33,1},{49,17},{2,34}... | collective-permute-start | bytes 30728 | tf_op jit(solution)/shard_map/ppermute | solution.py:440
  35.5 1.2 collective-permute-start.3
  39.4 3.3 %collective-permute-start.4 = (bf16[32,640]{1,0:T(8,128)(2,1)S(1)}, bf16[32,640]{1,0:T(8,128)(2,1)S(1)}, u32[]{:S(2)}, u32[]{:S(2)}) collective-permute-start(bf16[32,640]{1,0:T(8,128)(2,1)S(1)} %pad_maximum_fusion.1), channel_id=1, source_target_pairs={{0,64},{64,0},{1,65},{65,1},{2,66},{66,2},{3,67},{67,3},{4,68},{68... | collective-permute-start | bytes 122888 | tf_op jit(solution)/shard_map/ppermute | solution.py:440
  42.7 1.4 collective-permute-done.4
  44.1 1.2 collective-permute-start.5
  45.3 2.6 %collective-permute-done.5 = bf16[64,640]{1,0:T(8,128)(2,1)S(1)} collective-permute-done((bf16[64,640]{1,0:T(8,128)(2,1)S(1)}, bf16[64,640]{1,0:T(8,128)(2,1)S(1)}, u32[]{:S(2)}, u32[]{:S(2)}) %collective-permute-start.5) | collective-permute-done | bytes 81952 | tf_op jit(solution)/shard_map/ppermute | solution.py:440
  47.9 1.5 %collective-permute-start.6 = (bf16[128,640]{1,0:T(8,128)(2,1)S(1)}, bf16[128,640]{1,0:T(8,128)(2,1)S(1)}, u32[]{:S(2)}, u32[]{:S(2)}) collective-permute-start(bf16[128,640]{1,0:T(8,128)(2,1)S(1)} %constant_dynamic-update-slice_fusion.5.piece0), channel_id=1, source_target_pairs={{0,2},{2,4},{4,6},{6,0},{1,3},{3,5},{5,7},{7,1},{8,10},{10,12},{12... | collective-permute-start | bytes 491528 | tf_op jit(solution)/shard_map/ppermute | solution.py:440
  49.4 2.4 %collective-permute-start.7 = (bf16[128,640]{1,0:T(8,128)(2,1)S(1)}, bf16[128,640]{1,0:T(8,128)(2,1)S(1)}, u32[]{:S(2)}, u32[]{:S(2)}) collective-permute-start(bf16[128,640]{1,0:T(8,128)(2,1)S(1)} %constant_dynamic-update-slice_fusion.5.piece0), channel_id=1, source_target_pairs={{0,4},{2,6},{4,0},{6,2},{1,5},{3,7},{5,1},{7,3},{8,12},{10,14},{12... | collective-permute-start | bytes 491528 | tf_op jit(solution)/shard_map/ppermute | solution.py:440
  51.8 1.2 collective-permute-start.8
  53.4 3.0 %collective-permute-done.7.piece2 = bf16[128,640]{1,0:T(8,128)(2,1)S(1)} collective-permute-done((bf16[128,640]{1,0:T(8,128)(2,1)S(1)}, bf16[128,640]{1,0:T(8,128)(2,1)S(1)}, u32[]{:S(2)}, u32[]{:S(2)}) %collective-permute-start.7) | collective-permute-done | bytes 163872 | tf_op jit(solution)/shard_map/ppermute | solution.py:440
  56.4 4.8 %collective-permute-start.9 = (bf16[8,384,384]{2,1,0:T(8,128)(2,1)}, bf16[8,384,384]{2,1,0:T(8,128)(2,1)S(1)}, u32[]{:S(2)}, u32[]{:S(2)}) collective-permute-start(bf16[8,384,384]{2,1,0:T(8,128)(2,1)} %all-to-all-done.mixer_hbm), channel_id=1, source_target_pairs={{0,1},{1,0},{2,3},{3,2},{4,5},{5,4},{6,7},{7,6},{8,9},{9,8},{10,11... | collective-permute-start | bytes 7077896 | tf_op jit(solution)/shard_map/ppermute | solution.py:444
  61.2 3.1 %copy-done.1 = bf16[588,6144]{1,0:T(8,128)(2,1)S(1)} copy-done((bf16[588,6144]{1,0:T(8,128)(2,1)S(1)}, bf16[588,6144]{1,0:T(8,128)(2,1)}, u32[]{:S(2)}) %copy-start.1) | copy-done | bytes 7225368
  64.3 7.1 %embed_own.1 = (f32[528,384]{1,0:T(8,128)S(1)}, f32[512,128]{1,0:T(8,128)S(1)}, f32[512,128]{1,0:T(8,128)S(1)}, bf16[64,384]{1,0:T(8,128)(2,1)S(1)}) custom-call(bf16[128,640]{1,0:T(8,128)(2,1)S(1)} %constant_dynamic-update-slice_fusion.5.piece0, bf16[128,640]{1,0:T(8,128)(2,1)S(1)} %collective-permute-done.6.piece1, ...), custom_call_target="tpu_custom_call" | custom-call | flops 3500000000 | bytes 8000000 | tf_op jit(solution)/shard_map/embed_own/pallas_call | solution.py:334
  71.3 7.8 %embed_mate.1 = (bf16[512,384]{1,0:T(8,128)(2,1)S(1)}, bf16[64,384]{1,0:T(8,128)(2,1)S(1)}) custom-call(bf16[128,640]{1,0:T(8,128)(2,1)S(1)} %constant_dynamic-update-slice_fusion.5.piece0, bf16[128,640]{1,0:T(8,128)(2,1)S(1)} %collective-permute-done.6.piece1, bf16[128,640]{1,0:T(8,128)(2,1)S(1)} %collective-permute-done.7.piece2, ...), custom_call_target="tpu_custom_call" | custom-call | flops 3500000000 | bytes 8000000 | tf_op jit(solution)/shard_map/embed_mate/pallas_call | solution.py:334
  79.1 1.2 collective-permute-start.10
  80.3 1.4 %collective-permute-start.11 = (bf16[512,384]{1,0:T(8,128)(2,1)S(1)}, bf16[512,384]{1,0:T(8,128)(2,1)S(1)}, u32[]{:S(2)}, u32[]{:S(2)}) collective-permute-start(bf16[512,384]{1,0:T(8,128)(2,1)S(1)} %get-tuple-element.28.refs_0_), channel_id=1, source_target_pairs={{0,2},{2,4},{4,6},{6,0},{1,3},{3,5},{5,7},{7,1},{8,10},{10,12},{12... | collective-permute-start | bytes 1179656 | tf_op jit(solution)/shard_map/ppermute | solution.py:440
  81.8 8.2 %collective-permute-done.10.refs_1_ = bf16[512,384]{1,0:T(8,128)(2,1)S(1)} collective-permute-done((bf16[512,384]{1,0:T(8,128)(2,1)S(1)}, bf16[512,384]{1,0:T(8,128)(2,1)S(1)}, u32[]{:S(2)}, u32[]{:S(2)}) %collective-permute-start.10) | collective-permute-done | bytes 393248 | tf_op jit(solution)/shard_map/ppermute | solution.py:440
  89.9 2.4 %collective-permute-start.14 = (bf16[512,384]{1,0:T(8,128)(2,1)S(1)}, bf16[512,384]{1,0:T(8,128)(2,1)S(1)}, u32[]{:S(2)}, u32[]{:S(2)}) collective-permute-start(bf16[512,384]{1,0:T(8,128)(2,1)S(1)} %collective-permute-done.10.refs_1_), channel_id=1, source_target_pairs={{0,6},{2,0},{4,2},{6,4},{1,7},{3,1},{5,3},{7,5},{8,14},{10,8},{12,... | collective-permute-start | bytes 1179656 | tf_op jit(solution)/shard_map/ppermute | solution.py:440
  93.8 1.1 collective-permute-start.13
  94.9 5.1 %collective-permute-done.14.refs_2_ = bf16[512,384]{1,0:T(8,128)(2,1)S(1)} collective-permute-done((bf16[512,384]{1,0:T(8,128)(2,1)S(1)}, bf16[512,384]{1,0:T(8,128)(2,1)S(1)}, u32[]{:S(2)}, u32[]{:S(2)}) %collective-permute-start.14) | collective-permute-done | bytes 393248 | tf_op jit(solution)/shard_map/ppermute | solution.py:440
  100.0 3.5 %collective-permute-start.17 = (bf16[256,384]{1,0:T(8,128)(2,1)S(1)}, bf16[256,384]{1,0:T(8,128)(2,1)S(1)}, u32[]{:S(2)}, u32[]{:S(2)}) collective-permute-start(bf16[256,384]{1,0:T(8,128)(2,1)S(1)} %slice.9), channel_id=1, source_target_pairs={{0,6},{2,0},{4,2},{6,4},{1,7},{3,1},{5,3},{7,5},{8,14},{10,8},{12,... | collective-permute-start | bytes 589832 | tf_op jit(solution)/shard_map/ppermute | solution.py:440
  103.8 4.6 %collective-permute-done.12.refs_3_ = bf16[512,384]{1,0:T(8,128)(2,1)S(1)} collective-permute-done((bf16[512,384]{1,0:T(8,128)(2,1)S(1)}, bf16[512,384]{1,0:T(8,128)(2,1)S(1)}, u32[]{:S(2)}, u32[]{:S(2)}) %collective-permute-start.12) | collective-permute-done | bytes 393248 | tf_op jit(solution)/shard_map/ppermute | solution.py:440
  108.4 1.7 %mlp_out_4.1.refs_0_ = f32[512,768]{1,0:T(8,128)S(1)} custom-call(bf16[512,384]{1,0:T(8,128)(2,1)S(1)} %get-tuple-element.28.refs_0_, bf16[512,384]{1,0:T(8,128)(2,1)S(1)} %collective-permute-done.10.refs_1_, bf16[512,384]{1,0:T(8,128)(2,1)S(1)} %collective-permute-done.11.refs_2_, bf16[512,384]{1,0:T(8,128)(2,1)S(1)} %collective-permute-done.12.refs_3_, ...), custom_call_target="tpu_custom_call" | custom-call | flops 1207959552 | bytes 5505024 | tf_op jit(solution)/shard_map/mlp_out_4/pallas_call | solution.py:398
  110.2 1.5 %mlp_out_3.1.refs_0_ = f32[512,768]{1,0:T(8,128)S(1)} custom-call(f32[512,768]{1,0:T(8,128)S(1)} %mlp_out_4.1.refs_0_, bf16[512,384]{1,0:T(8,128)(2,1)S(1)} %collective-permute-done.13.refs_1_, bf16[512,384]{1,0:T(8,128)(2,1)S(1)} %collective-permute-done.14.refs_2_, bf16[512,384]{1,0:T(8,128)(2,1)S(1)} %collective-permute-done.15.refs_3_, ...), custom_call_target="tpu_custom_call" | custom-call | flops 905969664 | bytes 4521984 | tf_op jit(solution)/shard_map/mlp_out_3/pallas_call | solution.py:398
  112.7 1.6 %mlp_out_1.1 = bf16[16,64,384]{2,1,0:T(8,128)(2,1)} custom-call(f32[512,768]{1,0:T(8,128)S(1)} %mlp_out_3.1.refs_0_, bf16[512,384]{1,0:T(8,128)(2,1)S(1)} %pad_maximum_fusion.refs_1_, bf16[3072,384]{1,0:T(8,128)(2,1)S(1)} %copy-done, bf16[3072,384]{1,0:T(8,128)(2,1)S(1)} %collective-permute-done.refs_5_.refs_3_), custom_call_target="tpu_custom_call" | custom-call | flops 301989888 | bytes 2555904 | tf_op jit(solution)/shard_map/mlp_out_1/pallas_call | solution.py:398
  114.3 9.3 %all-to-all-start.1 = ((bf16[16,64,384]{2,1,0:T(8,128)(2,1)}), bf16[16,64,384]{2,1,0:T(8,128)(2,1)S(1)}, u32[]{:S(2)}, u32[]{:S(2)}) async-start(bf16[16,64,384]{2,1,0:T(8,128)(2,1)} %mlp_out_1.1), calls=%async_computation.1 | async-start | bytes 1572864 | tf_op jit(solution)/shard_map/all_to_all | solution.py:476
  123.8 14.3 %all-to-all-done.1 = bf16[16,64,384]{2,1,0:T(8,128)(2,1)S(1)} async-done(((bf16[16,64,384]{2,1,0:T(8,128)(2,1)}), bf16[16,64,384]{2,1,0:T(8,128)(2,1)S(1)}, u32[]{:S(2)}, u32[]{:S(2)}) %all-to-all-start.1) | async-done | bytes 786464 | tf_op jit(solution)/shard_map/all_to_all | solution.py:476
  (39 shorter events, 7.7 us)
Async XLA Ops:
  0.6 31.2 %collective-permute-start = (bf16[3072,384]{1,0:T(8,128)(2,1)}, bf16[3072,384]{1,0:T(8,128)(2,1)S(1)}, u32[]{:S(2)}, u32[]{:S(2)}) collective-permute-start(bf16[3072,384]{1,0:T(8,128)(2,1)} %refs_2_.1), channel_id=1, source_target_pairs={{0,1},{1,0},{2,3},{3,2},{4,5},{5,4},{6,7},{7,6},{8,9},{9,8},{10,11... | collective-permute-start | bytes 7077896 | tf_op jit(solution)/shard_map/ppermute | solution.py:444
  5.3 5.7 %copy-start.3 = (bf16[256,3]{0,1:T(4,128)(2,1)S(1)}, bf16[256,3]{0,1:T(4,128)(2,1)}, u32[]{:S(2)}) copy-start(bf16[256,3]{0,1:T(4,128)(2,1)} %param.19) | copy-start | bytes 4612
  5.3 47.7 %all-to-all-start = ((bf16[8,384,384]{2,1,0:T(8,128)(2,1)}), bf16[8,384,384]{2,1,0:T(8,128)(2,1)}, u32[]{:S(2)}, u32[]{:S(2)}) async-start(bf16[8,384,384]{2,1,0:T(8,128)(2,1)} %split_columns.1), calls=%async_computation | async-start | bytes 4718592 | tf_op jit(solution)/shard_map/all_to_all | solution.py:450
  11.7 49.5 %copy-start.2 = (f32[6144]{0:T(1024)S(1)}, f32[6144]{0:T(1024)}, u32[]{:S(2)}) copy-start(f32[6144]{0:T(1024)} %param.21) | copy-start | bytes 73732
  31.8 5.6 %collective-permute-start.1 = (bf16[8,640]{1,0:T(8,128)(2,1)}, bf16[8,640]{1,0:T(8,128)(2,1)S(1)}, u32[]{:S(2)}, u32[]{:S(2)}) collective-permute-start(bf16[8,640]{1,0:T(8,128)(2,1)} %get-tuple-element.19), channel_id=1, source_target_pairs={{0,16},{16,32},{32,48},{48,0},{1,17},{17,33},{33,49},{49,1},{2,18}... | collective-permute-start | bytes 30728 | tf_op jit(solution)/shard_map/ppermute | solution.py:440
  33.1 4.6 %collective-permute-start.2 = (bf16[8,640]{1,0:T(8,128)(2,1)}, bf16[8,640]{1,0:T(8,128)(2,1)S(1)}, u32[]{:S(2)}, u32[]{:S(2)}) collective-permute-start(bf16[8,640]{1,0:T(8,128)(2,1)} %get-tuple-element.19), channel_id=1, source_target_pairs={{0,32},{16,48},{32,0},{48,16},{1,33},{17,49},{33,1},{49,17},{2,34}... | collective-permute-start | bytes 30728 | tf_op jit(solution)/shard_map/ppermute | solution.py:440
  35.5 3.1 %collective-permute-start.3 = (bf16[8,640]{1,0:T(8,128)(2,1)}, bf16[8,640]{1,0:T(8,128)(2,1)S(1)}, u32[]{:S(2)}, u32[]{:S(2)}) collective-permute-start(bf16[8,640]{1,0:T(8,128)(2,1)} %get-tuple-element.19), channel_id=1, source_target_pairs={{0,48},{16,0},{32,16},{48,32},{1,49},{17,1},{33,17},{49,33},{2,50}... | collective-permute-start | bytes 30728 | tf_op jit(solution)/shard_map/ppermute | solution.py:440
  39.4 4.7 %collective-permute-start.4 = (bf16[32,640]{1,0:T(8,128)(2,1)S(1)}, bf16[32,640]{1,0:T(8,128)(2,1)S(1)}, u32[]{:S(2)}, u32[]{:S(2)}) collective-permute-start(bf16[32,640]{1,0:T(8,128)(2,1)S(1)} %pad_maximum_fusion.1), channel_id=1, source_target_pairs={{0,64},{64,0},{1,65},{65,1},{2,66},{66,2},{3,67},{67,3},{4,68},{68... | collective-permute-start | bytes 122888 | tf_op jit(solution)/shard_map/ppermute | solution.py:440
  44.1 3.8 %collective-permute-start.5 = (bf16[64,640]{1,0:T(8,128)(2,1)S(1)}, bf16[64,640]{1,0:T(8,128)(2,1)S(1)}, u32[]{:S(2)}, u32[]{:S(2)}) collective-permute-start(bf16[64,640]{1,0:T(8,128)(2,1)S(1)} %get-tuple-element.32), channel_id=1, source_target_pairs={{0,8},{8,0},{1,9},{9,1},{2,10},{10,2},{3,11},{11,3},{4,12},{12,4},... | collective-permute-start | bytes 245768 | tf_op jit(solution)/shard_map/ppermute | solution.py:440
  47.9 5.4 %collective-permute-start.6 = (bf16[128,640]{1,0:T(8,128)(2,1)S(1)}, bf16[128,640]{1,0:T(8,128)(2,1)S(1)}, u32[]{:S(2)}, u32[]{:S(2)}) collective-permute-start(bf16[128,640]{1,0:T(8,128)(2,1)S(1)} %constant_dynamic-update-slice_fusion.5.piece0), channel_id=1, source_target_pairs={{0,2},{2,4},{4,6},{6,0},{1,3},{3,5},{5,7},{7,1},{8,10},{10,12},{12... | collective-permute-start | bytes 491528 | tf_op jit(solution)/shard_map/ppermute | solution.py:440
  49.4 7.0 %collective-permute-start.7 = (bf16[128,640]{1,0:T(8,128)(2,1)S(1)}, bf16[128,640]{1,0:T(8,128)(2,1)S(1)}, u32[]{:S(2)}, u32[]{:S(2)}) collective-permute-start(bf16[128,640]{1,0:T(8,128)(2,1)S(1)} %constant_dynamic-update-slice_fusion.5.piece0), channel_id=1, source_target_pairs={{0,4},{2,6},{4,0},{6,2},{1,5},{3,7},{5,1},{7,3},{8,12},{10,14},{12... | collective-permute-start | bytes 491528 | tf_op jit(solution)/shard_map/ppermute | solution.py:440
  51.8 4.6 %collective-permute-start.8 = (bf16[128,640]{1,0:T(8,128)(2,1)S(1)}, bf16[128,640]{1,0:T(8,128)(2,1)S(1)}, u32[]{:S(2)}, u32[]{:S(2)}) collective-permute-start(bf16[128,640]{1,0:T(8,128)(2,1)S(1)} %constant_dynamic-update-slice_fusion.5.piece0), channel_id=1, source_target_pairs={{0,6},{2,0},{4,2},{6,4},{1,7},{3,1},{5,3},{7,5},{8,14},{10,8},{12,... | collective-permute-start | bytes 491528 | tf_op jit(solution)/shard_map/ppermute | solution.py:440
  56.4 14.9 %collective-permute-start.9 = (bf16[8,384,384]{2,1,0:T(8,128)(2,1)}, bf16[8,384,384]{2,1,0:T(8,128)(2,1)S(1)}, u32[]{:S(2)}, u32[]{:S(2)}) collective-permute-start(bf16[8,384,384]{2,1,0:T(8,128)(2,1)} %all-to-all-done.mixer_hbm), channel_id=1, source_target_pairs={{0,1},{1,0},{2,3},{3,2},{4,5},{5,4},{6,7},{7,6},{8,9},{9,8},{10,11... | collective-permute-start | bytes 7077896 | tf_op jit(solution)/shard_map/ppermute | solution.py:444
  61.2 3.1 %copy-start.1 = (bf16[588,6144]{1,0:T(8,128)(2,1)S(1)}, bf16[588,6144]{1,0:T(8,128)(2,1)}, u32[]{:S(2)}) copy-start(bf16[588,6144]{1,0:T(8,128)(2,1)} %weight_hbm.3) | copy-start | bytes 21676036
  71.3 37.1 %copy-start = (bf16[3072,384]{1,0:T(8,128)(2,1)S(1)}, bf16[3072,384]{1,0:T(8,128)(2,1)}, u32[]{:S(2)}) copy-start(bf16[3072,384]{1,0:T(8,128)(2,1)} %refs_2_.1) | copy-start | bytes 7077892
  79.1 10.8 %collective-permute-start.10 = (bf16[512,384]{1,0:T(8,128)(2,1)S(1)}, bf16[512,384]{1,0:T(8,128)(2,1)S(1)}, u32[]{:S(2)}, u32[]{:S(2)}) collective-permute-start(bf16[512,384]{1,0:T(8,128)(2,1)S(1)} %get-tuple-element.28.refs_0_), channel_id=1, source_target_pairs={{0,8},{8,0},{1,9},{9,1},{2,10},{10,2},{3,11},{11,3},{4,12},{12,4},... | collective-permute-start | bytes 1179656 | tf_op jit(solution)/shard_map/ppermute | solution.py:440
  80.3 12.0 %collective-permute-start.11 = (bf16[512,384]{1,0:T(8,128)(2,1)S(1)}, bf16[512,384]{1,0:T(8,128)(2,1)S(1)}, u32[]{:S(2)}, u32[]{:S(2)}) collective-permute-start(bf16[512,384]{1,0:T(8,128)(2,1)S(1)} %get-tuple-element.28.refs_0_), channel_id=1, source_target_pairs={{0,2},{2,4},{4,6},{6,0},{1,3},{3,5},{5,7},{7,1},{8,10},{10,12},{12... | collective-permute-start | bytes 1179656 | tf_op jit(solution)/shard_map/ppermute | solution.py:440
  89.9 10.0 %collective-permute-start.14 = (bf16[512,384]{1,0:T(8,128)(2,1)S(1)}, bf16[512,384]{1,0:T(8,128)(2,1)S(1)}, u32[]{:S(2)}, u32[]{:S(2)}) collective-permute-start(bf16[512,384]{1,0:T(8,128)(2,1)S(1)} %collective-permute-done.10.refs_1_), channel_id=1, source_target_pairs={{0,6},{2,0},{4,2},{6,4},{1,7},{3,1},{5,3},{7,5},{8,14},{10,8},{12,... | collective-permute-start | bytes 1179656 | tf_op jit(solution)/shard_map/ppermute | solution.py:440
  92.3 11.2 %collective-permute-start.15 = (bf16[512,384]{1,0:T(8,128)(2,1)S(1)}, bf16[512,384]{1,0:T(8,128)(2,1)S(1)}, u32[]{:S(2)}, u32[]{:S(2)}) collective-permute-start(bf16[512,384]{1,0:T(8,128)(2,1)S(1)} %collective-permute-done.11.refs_2_), channel_id=1, source_target_pairs={{0,8},{8,0},{1,9},{9,1},{2,10},{10,2},{3,11},{11,3},{4,12},{12,4},... | collective-permute-start | bytes 1179656 | tf_op jit(solution)/shard_map/ppermute | solution.py:440
  93.4 15.0 %collective-permute-start.12 = (bf16[512,384]{1,0:T(8,128)(2,1)S(1)}, bf16[512,384]{1,0:T(8,128)(2,1)S(1)}, u32[]{:S(2)}, u32[]{:S(2)}) collective-permute-start(bf16[512,384]{1,0:T(8,128)(2,1)S(1)} %get-tuple-element.28.refs_0_), channel_id=1, source_target_pairs={{0,6},{2,0},{4,2},{6,4},{1,7},{3,1},{5,3},{7,5},{8,14},{10,8},{12,... | collective-permute-start | bytes 1179656 | tf_op jit(solution)/shard_map/ppermute | solution.py:440
  93.8 16.4 %collective-permute-start.13 = (bf16[512,384]{1,0:T(8,128)(2,1)S(1)}, bf16[512,384]{1,0:T(8,128)(2,1)S(1)}, u32[]{:S(2)}, u32[]{:S(2)}) collective-permute-start(bf16[512,384]{1,0:T(8,128)(2,1)S(1)} %collective-permute-done.11.refs_2_), channel_id=1, source_target_pairs={{0,2},{2,4},{4,6},{6,0},{1,3},{3,5},{5,7},{7,1},{8,10},{10,12},{12... | collective-permute-start | bytes 1179656 | tf_op jit(solution)/shard_map/ppermute | solution.py:440
  100.0 12.6 %collective-permute-start.17 = (bf16[256,384]{1,0:T(8,128)(2,1)S(1)}, bf16[256,384]{1,0:T(8,128)(2,1)S(1)}, u32[]{:S(2)}, u32[]{:S(2)}) collective-permute-start(bf16[256,384]{1,0:T(8,128)(2,1)S(1)} %slice.9), channel_id=1, source_target_pairs={{0,6},{2,0},{4,2},{6,4},{1,7},{3,1},{5,3},{7,5},{8,14},{10,8},{12,... | collective-permute-start | bytes 589832 | tf_op jit(solution)/shard_map/ppermute | solution.py:440
  103.5 9.1 %collective-permute-start.16 = (bf16[256,384]{1,0:T(8,128)(2,1)S(1)}, bf16[256,384]{1,0:T(8,128)(2,1)S(1)}, u32[]{:S(2)}, u32[]{:S(2)}) collective-permute-start(bf16[256,384]{1,0:T(8,128)(2,1)S(1)} %slice.8), channel_id=1, source_target_pairs={{0,2},{2,4},{4,6},{6,0},{1,3},{3,5},{5,7},{7,1},{8,10},{10,12},{12... | collective-permute-start | bytes 589832 | tf_op jit(solution)/shard_map/ppermute | solution.py:440
  114.3 23.8 %all-to-all-start.1 = ((bf16[16,64,384]{2,1,0:T(8,128)(2,1)}), bf16[16,64,384]{2,1,0:T(8,128)(2,1)S(1)}, u32[]{:S(2)}, u32[]{:S(2)}) async-start(bf16[16,64,384]{2,1,0:T(8,128)(2,1)} %mlp_out_1.1), calls=%async_computation.1 | async-start | bytes 1572864 | tf_op jit(solution)/shard_map/all_to_all | solution.py:476
  123.6 14.6 %collective-permute-start.18 = (bf16[64,384]{1,0:T(8,128)(2,1)S(1)}, bf16[64,384]{1,0:T(8,128)(2,1)S(1)}, u32[]{:S(2)}, u32[]{:S(2)}) collective-permute-start(bf16[64,384]{1,0:T(8,128)(2,1)S(1)} %get-tuple-element.31), channel_id=1, source_target_pairs={{0,1},{1,0},{2,3},{3,2},{4,5},{5,4},{6,7},{7,6},{8,9},{9,8},{10,11... | collective-permute-start | bytes 147464 | tf_op jit(solution)/shard_map/ppermute | solution.py:444

commit v8 on v7

--- a/solution.py
+++ b/solution.py
@@ -69,7 +69,7 @@
     column = lax.broadcasted_iota(jnp.int32, (8, 128), 1)
     colour = lax.broadcasted_iota(jnp.int32, (8, 128), 0)
     place = ((column == W1 * colour) & (colour < 3)).astype(bf16)
-    out_k[...] = jnp.dot(out_w[...], place[0:3, :], preferred_element_type=f32).astype(bf16)
+    out_k[...] = lax.dot_general(out_w[...], place[0:3, :], (((0,), (0,)), ((), ())), preferred_element_type=f32).astype(bf16)
 
     for y in range(side):
         for c in range(3):
@@ -241,7 +241,7 @@
         compiler_params=pltpu.CompilerParams(vmem_limit_bytes=58 << 20),
         cost_estimate=pl.CostEstimate(flops=10_000_000_000, transcendentals=3_000_000, bytes_accessed=12_000_000),
         name="score_net",
-    )(images, noise, stem_w, l1, down, l2, up, out_w)
+    )(images, noise, stem_w, l1, down, l2, up, out_w.T)
     return purified.transpose(2, 0, 3, 1), patches
 
 
@@ -454,8 +454,8 @@
                                    up_weight, out_weight)
     mate_out, patches = lax.optimization_barrier((mate_out, patches))
     patches = jnp.concatenate([patches] + [shift(patches, "x", k) for k in (1, 2, 3)], axis=0)
-    patches = jnp.concatenate([patches, shift(patches, "zh", 1)], axis=0)
-    patches = jnp.concatenate([patches, shift(patches, "zl", 1)], axis=0)
+    both = lax.ppermute(patches, ("zh", "zl"), [(i, 3 - i) for i in range(4)])
+    patches = jnp.concatenate([patches, shift(patches, "zh", 1), shift(patches, "zl", 1), both], axis=0)
     pieces = [patches] + [shift(patches, "y", k) for k in (1, 2, 3)]
     own_in, *pieces = lax.optimization_barrier((own_in, *pieces))
     mate_in = swap(own_in)
@@ -465,10 +465,12 @@
     far = shift(hidden, "zl", 1)
     below = shift(hidden, "y", 1)
     above = shift(hidden, "y", 3)
+    far, below, above = lax.optimization_barrier((far, below, above))
     across = shift(below, "y", 1)
     far_above = shift(far, "y", 3)
     far_below = shift(below, "zl", 1)
     total = mix_call(None, [((0, 0), hidden), ((1, 0), far), ((0, 3), below), ((0, 1), above)], mlp_out, mate_out)
+    far_below, far_above, total = lax.optimization_barrier((far_below, far_above, total))
     half = hidden.shape[0] // 2
     last = jnp.concatenate([shift(far_below[:half], "y", 1), shift(far_above[half:], "y", 3)], axis=0)
     total = mix_call(total, [((0, 2), across), ((1, 1), far_above), ((1, 3), far_below)], mlp_out, mate_out)

time: 139 us -> 135 us (0.971)
  starting transfers between devices: 47.3 us -> 44 us
    ppermute x16, starting transfers between devices: 25.9 us -> 23.7 us  [shift(): return lax.ppermute(value, axis, [(i, (i + k) % n) for i in range(n)])]
    ppermute x0 -> x1, waiting for transfers between devices: none -> 1.76 us  [on_device(): both = lax.ppermute(patches, ('zh', 'zl'), [(i, 3 - i) for i in range(4)])]
    unnamed x13 -> x11, local copies, waits for them, and re-layouts: 4.6 us -> 3.85 us
  transfers between devices with their start and end apart: 21 -> 22, of which waited for: 11 -> 14; matrix products, arithmetic and copies ran while one was open for 2% -> 1% of each run, Pallas kernels for 24% -> 25%
where the time goes in v8:
time: 135 us
  starting transfers between devices  44 us (33%)
  Pallas kernels  43 us (32%)
  waiting for transfers between devices  42.2 us (31%)
  local copies, waits for them, and re-layouts  4.56 us (3%)
    ppermute x16, waiting for transfers between devices, shift(): return lax.ppermute(value, axis, [(i, (i + k) % n) for i in range(n)])  26.1 us
    ppermute x16, starting transfers between devices, shift(): return lax.ppermute(value, axis, [(i, (i + k) % n) for i in range(n)])  23.7 us
    pallas_call x1, Pallas kernels, score_call(): pl.pallas_call(functools.partial(score_kernel, side, count), out_shape=(j...  20.2 us
    pallas_call x2, Pallas kernels, embed_call(): pl.pallas_call(functools.partial(embed_kernel, flip), out_shape=shapes, i...  14.8 us
    all_to_all x1, waiting for transfers between devices, on_device(): shares = lax.all_to_all(shares, ('zh', 'x', 'core'), 0, 0)  14.3 us
    all_to_all x1, starting transfers between devices, on_device(): shares = lax.all_to_all(shares, ('zh', 'x', 'core'), 0, 0)  8 us
    ppermute x3, starting transfers between devices, swap(): return lax.ppermute(value, 'core', [(0, 1), (1, 0)])  6.67 us
    all_to_all x1, starting transfers between devices, on_device(): own_in = lax.all_to_all(split_call(mlp_in, 8), ('zl', 'y'), 0, 0)  5.64 us
  transfers between devices with their start and end apart: 22, of which 14 were waited for; matrix products, arithmetic and copies ran while one was open for 1% of the time, Pallas kernels for 25%

profile of v8, /device:TPU:1, one launch (start us, length us, event | category | flops | bytes accessed | tf_op | source)
XLA Modules:
  0.0 134.7 jit_solution(1460136465988143063)
XLA Ops:
  0.6 1.5 %collective-permute-start = (bf16[3072,384]{1,0:T(8,128)(2,1)}, bf16[3072,384]{1,0:T(8,128)(2,1)S(1)}, u32[]{:S(2)}, u32[]{:S(2)}) collective-permute-start(bf16[3072,384]{1,0:T(8,128)(2,1)} %refs_2_.1), channel_id=1, source_target_pairs={{0,1},{1,0},{2,3},{3,2},{4,5},{5,4},{6,7},{7,6},{8,9},{9,8},{10,11... | collective-permute-start | bytes 7077896 | tf_op jit(solution)/shard_map/ppermute | solution.py:444
  2.1 3.1 %split_columns.1 = bf16[8,384,384]{2,1,0:T(8,128)(2,1)} custom-call(bf16[384,3072]{1,0:T(8,128)(2,1)} %whole.1), custom_call_target="tpu_custom_call" | custom-call | bytes 4718592 | tf_op jit(solution)/shard_map/split_columns/pallas_call | solution.py:426
  5.3 5.6 %all-to-all-start = ((bf16[8,384,384]{2,1,0:T(8,128)(2,1)}), bf16[8,384,384]{2,1,0:T(8,128)(2,1)}, u32[]{:S(2)}, u32[]{:S(2)}) async-start(bf16[8,384,384]{2,1,0:T(8,128)(2,1)} %split_columns.1), calls=%async_computation | async-start | bytes 4718592 | tf_op jit(solution)/shard_map/all_to_all | solution.py:450
  10.9 20.2 %score_net.1 = (f32[28,3,2,28]{3,2,1,0:T(2,128)}, bf16[8,640]{1,0:T(8,128)(2,1)}) custom-call(f32[28,3,2,28]{3,2,1,0:T(2,128)} %bitcast.18, f32[28,3,2,28]{3,2,1,0:T(2,128)} %bitcast.19, bf16[27,256]{1,0:T(8,128)(2,1)} %stem_w.1, bf16[4,2304,256]{2,1,0:T(8,128)(2,1)} %l1_hbm.1, bf16[1024,256]{1,0:T(8,128)(2,1)} %down_hbm.1, bf16[2,2304,256]{2,1,0:T(8,128)(2,1)} %l2_hbm.1, ...), custom_call_target="tpu_custom_call" | custom-call | flops 10000000000 | bytes 12000000 | tf_op jit(solution)/shard_map/score_net/pallas_call | solution.py:217
  31.1 1.3 collective-permute-start.1
  33.1 2.5 %collective-permute-start.2 = (bf16[8,640]{1,0:T(8,128)(2,1)}, bf16[8,640]{1,0:T(8,128)(2,1)S(1)}, u32[]{:S(2)}, u32[]{:S(2)}) collective-permute-start(bf16[8,640]{1,0:T(8,128)(2,1)} %get-tuple-element.25), channel_id=1, source_target_pairs={{0,32},{16,48},{32,0},{48,16},{1,33},{17,49},{33,1},{49,17},{2,34}... | collective-permute-start | bytes 30728 | tf_op jit(solution)/shard_map/ppermute | solution.py:440
  35.6 1.2 collective-permute-start.3
  38.7 3.3 %collective-permute-start.4 = (bf16[32,640]{1,0:T(8,128)(2,1)S(1)}, bf16[32,640]{1,0:T(8,128)(2,1)S(1)}, u32[]{:S(2)}, u32[]{:S(2)}) collective-permute-start(bf16[32,640]{1,0:T(8,128)(2,1)S(1)} %get-tuple-element.44), channel_id=1, source_target_pairs={{0,64},{64,0},{1,65},{65,1},{2,66},{66,2},{3,67},{67,3},{4,68},{68... | collective-permute-start | bytes 122888 | tf_op jit(solution)/shard_map/ppermute | solution.py:440
  43.5 1.7 %collective-permute-done.5 = bf16[32,640]{1,0:T(8,128)(2,1)S(1)} collective-permute-done((bf16[32,640]{1,0:T(8,128)(2,1)S(1)}, bf16[32,640]{1,0:T(8,128)(2,1)S(1)}, u32[]{:S(2)}, u32[]{:S(2)}) %collective-permute-start.5) | collective-permute-done | bytes 40992 | tf_op jit(solution)/shard_map/ppermute | solution.py:440
  45.2 1.8 %collective-permute-done.6 = bf16[32,640]{1,0:T(8,128)(2,1)S(1)} collective-permute-done((bf16[32,640]{1,0:T(8,128)(2,1)S(1)}, bf16[32,640]{1,0:T(8,128)(2,1)S(1)}, u32[]{:S(2)}, u32[]{:S(2)}) %collective-permute-start.6) | collective-permute-done | bytes 40992 | tf_op jit(solution)/shard_map/ppermute | solution.py:457
  47.0 1.2 collective-permute-start.7
  48.1 2.4 %collective-permute-start.8 = (bf16[128,640]{1,0:T(8,128)(2,1)S(1)}, bf16[128,640]{1,0:T(8,128)(2,1)S(1)}, u32[]{:S(2)}, u32[]{:S(2)}) collective-permute-start(bf16[128,640]{1,0:T(8,128)(2,1)S(1)} %constant_dynamic-update-slice_fusion.4.piece0), channel_id=1, source_target_pairs={{0,4},{2,6},{4,0},{6,2},{1,5},{3,7},{5,1},{7,3},{8,12},{10,14},{12... | collective-permute-start | bytes 491528 | tf_op jit(solution)/shard_map/ppermute | solution.py:440
  50.5 1.1 collective-permute-start.9
  52.3 2.7 %collective-permute-done.8.piece2 = bf16[128,640]{1,0:T(8,128)(2,1)S(1)} collective-permute-done((bf16[128,640]{1,0:T(8,128)(2,1)S(1)}, bf16[128,640]{1,0:T(8,128)(2,1)S(1)}, u32[]{:S(2)}, u32[]{:S(2)}) %collective-permute-start.8) | collective-permute-done | bytes 163872 | tf_op jit(solution)/shard_map/ppermute | solution.py:440
  55.0 5.0 %collective-permute-start.10 = (bf16[8,384,384]{2,1,0:T(8,128)(2,1)}, bf16[8,384,384]{2,1,0:T(8,128)(2,1)S(1)}, u32[]{:S(2)}, u32[]{:S(2)}) collective-permute-start(bf16[8,384,384]{2,1,0:T(8,128)(2,1)} %all-to-all-done.mixer_hbm), channel_id=1, source_target_pairs={{0,1},{1,0},{2,3},{3,2},{4,5},{5,4},{6,7},{7,6},{8,9},{9,8},{10,11... | collective-permute-start | bytes 7077896 | tf_op jit(solution)/shard_map/ppermute | solution.py:444
  60.0 3.1 %copy-done.1 = bf16[588,6144]{1,0:T(8,128)(2,1)S(1)} copy-done((bf16[588,6144]{1,0:T(8,128)(2,1)S(1)}, bf16[588,6144]{1,0:T(8,128)(2,1)}, u32[]{:S(2)}) %copy-start.1) | copy-done | bytes 7225368
  63.1 7.1 %embed_own.1 = (f32[528,384]{1,0:T(8,128)S(1)}, f32[512,128]{1,0:T(8,128)S(1)}, f32[512,128]{1,0:T(8,128)S(1)}, bf16[64,384]{1,0:T(8,128)(2,1)S(1)}) custom-call(bf16[128,640]{1,0:T(8,128)(2,1)S(1)} %constant_dynamic-update-slice_fusion.4.piece0, bf16[128,640]{1,0:T(8,128)(2,1)S(1)} %collective-permute-done.7.piece1, ...), custom_call_target="tpu_custom_call" | custom-call | flops 3500000000 | bytes 8000000 | tf_op jit(solution)/shard_map/embed_own/pallas_call | solution.py:334
  70.2 7.8 %embed_mate.1 = (bf16[512,384]{1,0:T(8,128)(2,1)S(1)}, bf16[64,384]{1,0:T(8,128)(2,1)S(1)}) custom-call(bf16[128,640]{1,0:T(8,128)(2,1)S(1)} %constant_dynamic-update-slice_fusion.4.piece0, bf16[128,640]{1,0:T(8,128)(2,1)S(1)} %collective-permute-done.7.piece1, bf16[128,640]{1,0:T(8,128)(2,1)S(1)} %collective-permute-done.8.piece2, ...), custom_call_target="tpu_custom_call" | custom-call | flops 3500000000 | bytes 8000000 | tf_op jit(solution)/shard_map/embed_mate/pallas_call | solution.py:334
  78.0 1.5 %collective-permute-start.12 = (bf16[512,384]{1,0:T(8,128)(2,1)S(1)}, bf16[512,384]{1,0:T(8,128)(2,1)S(1)}, u32[]{:S(2)}, u32[]{:S(2)}) collective-permute-start(bf16[512,384]{1,0:T(8,128)(2,1)S(1)} %get-tuple-element.34.refs_0_), channel_id=1, source_target_pairs={{0,2},{2,4},{4,6},{6,0},{1,3},{3,5},{5,7},{7,1},{8,10},{10,12},{12... | collective-permute-start | bytes 1179656 | tf_op jit(solution)/shard_map/ppermute | solution.py:440
  79.5 1.2 collective-permute-start.13
  80.8 8.0 %collective-permute-done.11.refs_1_ = bf16[512,384]{1,0:T(8,128)(2,1)S(1)} collective-permute-done((bf16[512,384]{1,0:T(8,128)(2,1)S(1)}, bf16[512,384]{1,0:T(8,128)(2,1)S(1)}, u32[]{:S(2)}, u32[]{:S(2)}) %collective-permute-start.11) | collective-permute-done | bytes 393248 | tf_op jit(solution)/shard_map/ppermute | solution.py:440
  88.7 1.3 collective-permute-done.12.refs_2_
  90.0 1.1 collective-permute-start.14
  91.1 2.4 %collective-permute-start.15 = (bf16[512,384]{1,0:T(8,128)(2,1)S(1)}, bf16[512,384]{1,0:T(8,128)(2,1)S(1)}, u32[]{:S(2)}, u32[]{:S(2)}) collective-permute-start(bf16[512,384]{1,0:T(8,128)(2,1)S(1)} %collective-permute-done.11.refs_1_), channel_id=1, source_target_pairs={{0,6},{2,0},{4,2},{6,4},{1,7},{3,1},{5,3},{7,5},{8,14},{10,8},{12,... | collective-permute-start | bytes 1179656 | tf_op jit(solution)/shard_map/ppermute | solution.py:440
  93.5 1.7 %mlp_out_4.1.refs_0_ = f32[512,768]{1,0:T(8,128)S(1)} custom-call(bf16[512,384]{1,0:T(8,128)(2,1)S(1)} %get-tuple-element.34.refs_0_, bf16[512,384]{1,0:T(8,128)(2,1)S(1)} %collective-permute-done.11.refs_1_, bf16[512,384]{1,0:T(8,128)(2,1)S(1)} %collective-permute-done.12.refs_2_, bf16[512,384]{1,0:T(8,128)(2,1)S(1)} %collective-permute-done.13.refs_3_, ...), custom_call_target="tpu_custom_call" | custom-call | flops 1207959552 | bytes 5505024 | tf_op jit(solution)/shard_map/mlp_out_4/pallas_call | solution.py:398
  95.2 4.4 %collective-permute-done.14.refs_3_ = bf16[512,384]{1,0:T(8,128)(2,1)S(1)} collective-permute-done((bf16[512,384]{1,0:T(8,128)(2,1)S(1)}, bf16[512,384]{1,0:T(8,128)(2,1)S(1)}, u32[]{:S(2)}, u32[]{:S(2)}) %collective-permute-start.14) | collective-permute-done | bytes 393248 | tf_op jit(solution)/shard_map/ppermute | solution.py:440
  100.2 3.7 %collective-permute-start.18 = (bf16[256,384]{1,0:T(8,128)(2,1)S(1)}, bf16[256,384]{1,0:T(8,128)(2,1)S(1)}, u32[]{:S(2)}, u32[]{:S(2)}) collective-permute-start(bf16[256,384]{1,0:T(8,128)(2,1)S(1)} %slice.7), channel_id=1, source_target_pairs={{0,6},{2,0},{4,2},{6,4},{1,7},{3,1},{5,3},{7,5},{8,14},{10,8},{12,... | collective-permute-start | bytes 589832 | tf_op jit(solution)/shard_map/ppermute | solution.py:440
  104.0 1.5 %mlp_out_3.1.refs_0_ = f32[512,768]{1,0:T(8,128)S(1)} custom-call(f32[512,768]{1,0:T(8,128)S(1)} %mlp_out_4.1.refs_0_, bf16[512,384]{1,0:T(8,128)(2,1)S(1)} %collective-permute-done.16.refs_1_, bf16[512,384]{1,0:T(8,128)(2,1)S(1)} %collective-permute-done.15.refs_2_, bf16[512,384]{1,0:T(8,128)(2,1)S(1)} %collective-permute-done.14.refs_3_, ...), custom_call_target="tpu_custom_call" | custom-call | flops 905969664 | bytes 4521984 | tf_op jit(solution)/shard_map/mlp_out_3/pallas_call | solution.py:398
  106.5 3.2 %collective-permute-done.17 = bf16[256,384]{1,0:T(8,128)(2,1)S(1)} collective-permute-done((bf16[256,384]{1,0:T(8,128)(2,1)S(1)}, bf16[256,384]{1,0:T(8,128)(2,1)S(1)}, u32[]{:S(2)}, u32[]{:S(2)}) %collective-permute-start.17) | collective-permute-done | bytes 196640 | tf_op jit(solution)/shard_map/ppermute | solution.py:440
  109.8 1.6 %mlp_out_1.1 = bf16[16,64,384]{2,1,0:T(8,128)(2,1)} custom-call(f32[512,768]{1,0:T(8,128)S(1)} %mlp_out_3.1.refs_0_, bf16[512,384]{1,0:T(8,128)(2,1)S(1)} %pad_maximum_fusion.refs_1_, bf16[3072,384]{1,0:T(8,128)(2,1)S(1)} %copy-done, bf16[3072,384]{1,0:T(8,128)(2,1)S(1)} %collective-permute-done.refs_5_.refs_3_), custom_call_target="tpu_custom_call" | custom-call | flops 301989888 | bytes 2555904 | tf_op jit(solution)/shard_map/mlp_out_1/pallas_call | solution.py:398
  111.4 8.0 %all-to-all-start.1 = ((bf16[16,64,384]{2,1,0:T(8,128)(2,1)}), bf16[16,64,384]{2,1,0:T(8,128)(2,1)S(1)}, u32[]{:S(2)}, u32[]{:S(2)}) async-start(bf16[16,64,384]{2,1,0:T(8,128)(2,1)} %mlp_out_1.1), calls=%async_computation.1 | async-start | bytes 1572864 | tf_op jit(solution)/shard_map/all_to_all | solution.py:478
  119.6 14.3 %all-to-all-done.1 = bf16[16,64,384]{2,1,0:T(8,128)(2,1)S(1)} async-done(((bf16[16,64,384]{2,1,0:T(8,128)(2,1)}), bf16[16,64,384]{2,1,0:T(8,128)(2,1)S(1)}, u32[]{:S(2)}, u32[]{:S(2)}) %all-to-all-start.1) | async-done | bytes 786464 | tf_op jit(solution)/shard_map/all_to_all | solution.py:478
  (38 shorter events, 7.7 us)
Async XLA Ops:
  0.6 30.5 %collective-permute-start = (bf16[3072,384]{1,0:T(8,128)(2,1)}, bf16[3072,384]{1,0:T(8,128)(2,1)S(1)}, u32[]{:S(2)}, u32[]{:S(2)}) collective-permute-start(bf16[3072,384]{1,0:T(8,128)(2,1)} %refs_2_.1), channel_id=1, source_target_pairs={{0,1},{1,0},{2,3},{3,2},{4,5},{5,4},{6,7},{7,6},{8,9},{9,8},{10,11... | collective-permute-start | bytes 7077896 | tf_op jit(solution)/shard_map/ppermute | solution.py:444
  5.3 46.3 %all-to-all-start = ((bf16[8,384,384]{2,1,0:T(8,128)(2,1)}), bf16[8,384,384]{2,1,0:T(8,128)(2,1)}, u32[]{:S(2)}, u32[]{:S(2)}) async-start(bf16[8,384,384]{2,1,0:T(8,128)(2,1)} %split_columns.1), calls=%async_computation | async-start | bytes 4718592 | tf_op jit(solution)/shard_map/all_to_all | solution.py:450
  10.9 49.1 %copy-start.2 = (f32[6144]{0:T(1024)S(1)}, f32[6144]{0:T(1024)}, u32[]{:S(2)}) copy-start(f32[6144]{0:T(1024)} %param.21) | copy-start | bytes 73732
  31.1 5.6 %collective-permute-start.1 = (bf16[8,640]{1,0:T(8,128)(2,1)}, bf16[8,640]{1,0:T(8,128)(2,1)S(1)}, u32[]{:S(2)}, u32[]{:S(2)}) collective-permute-start(bf16[8,640]{1,0:T(8,128)(2,1)} %get-tuple-element.25), channel_id=1, source_target_pairs={{0,16},{16,32},{32,48},{48,0},{1,17},{17,33},{33,49},{49,1},{2,18}... | collective-permute-start | bytes 30728 | tf_op jit(solution)/shard_map/ppermute | solution.py:440
  33.1 4.6 %collective-permute-start.2 = (bf16[8,640]{1,0:T(8,128)(2,1)}, bf16[8,640]{1,0:T(8,128)(2,1)S(1)}, u32[]{:S(2)}, u32[]{:S(2)}) collective-permute-start(bf16[8,640]{1,0:T(8,128)(2,1)} %get-tuple-element.25), channel_id=1, source_target_pairs={{0,32},{16,48},{32,0},{48,16},{1,33},{17,49},{33,1},{49,17},{2,34}... | collective-permute-start | bytes 30728 | tf_op jit(solution)/shard_map/ppermute | solution.py:440
  35.6 3.1 %collective-permute-start.3 = (bf16[8,640]{1,0:T(8,128)(2,1)}, bf16[8,640]{1,0:T(8,128)(2,1)S(1)}, u32[]{:S(2)}, u32[]{:S(2)}) collective-permute-start(bf16[8,640]{1,0:T(8,128)(2,1)} %get-tuple-element.25), channel_id=1, source_target_pairs={{0,48},{16,0},{32,16},{48,32},{1,49},{17,1},{33,17},{49,33},{2,50}... | collective-permute-start | bytes 30728 | tf_op jit(solution)/shard_map/ppermute | solution.py:440
  38.7 4.8 %collective-permute-start.4 = (bf16[32,640]{1,0:T(8,128)(2,1)S(1)}, bf16[32,640]{1,0:T(8,128)(2,1)S(1)}, u32[]{:S(2)}, u32[]{:S(2)}) collective-permute-start(bf16[32,640]{1,0:T(8,128)(2,1)S(1)} %get-tuple-element.44), channel_id=1, source_target_pairs={{0,64},{64,0},{1,65},{65,1},{2,66},{66,2},{3,67},{67,3},{4,68},{68... | collective-permute-start | bytes 122888 | tf_op jit(solution)/shard_map/ppermute | solution.py:440
  42.0 3.1 %collective-permute-start.5 = (bf16[32,640]{1,0:T(8,128)(2,1)S(1)}, bf16[32,640]{1,0:T(8,128)(2,1)S(1)}, u32[]{:S(2)}, u32[]{:S(2)}) collective-permute-start(bf16[32,640]{1,0:T(8,128)(2,1)S(1)} %get-tuple-element.44), channel_id=1, source_target_pairs={{0,8},{8,0},{1,9},{9,1},{2,10},{10,2},{3,11},{11,3},{4,12},{12,4},... | collective-permute-start | bytes 122888 | tf_op jit(solution)/shard_map/ppermute | solution.py:440
  42.9 4.1 %collective-permute-start.6 = (bf16[32,640]{1,0:T(8,128)(2,1)S(1)}, bf16[32,640]{1,0:T(8,128)(2,1)S(1)}, u32[]{:S(2)}, u32[]{:S(2)}) collective-permute-start(bf16[32,640]{1,0:T(8,128)(2,1)S(1)} %get-tuple-element.44), channel_id=1, source_target_pairs={{0,72},{8,64},{64,8},{72,0},{1,73},{9,65},{65,9},{73,1},{2,74},{10... | collective-permute-start | bytes 122888 | tf_op jit(solution)/shard_map/ppermute | solution.py:457
  47.0 5.4 %collective-permute-start.7 = (bf16[128,640]{1,0:T(8,128)(2,1)S(1)}, bf16[128,640]{1,0:T(8,128)(2,1)S(1)}, u32[]{:S(2)}, u32[]{:S(2)}) collective-permute-start(bf16[128,640]{1,0:T(8,128)(2,1)S(1)} %constant_dynamic-update-slice_fusion.4.piece0), channel_id=1, source_target_pairs={{0,2},{2,4},{4,6},{6,0},{1,3},{3,5},{5,7},{7,1},{8,10},{10,12},{12... | collective-permute-start | bytes 491528 | tf_op jit(solution)/shard_map/ppermute | solution.py:440
  48.1 6.9 %collective-permute-start.8 = (bf16[128,640]{1,0:T(8,128)(2,1)S(1)}, bf16[128,640]{1,0:T(8,128)(2,1)S(1)}, u32[]{:S(2)}, u32[]{:S(2)}) collective-permute-start(bf16[128,640]{1,0:T(8,128)(2,1)S(1)} %constant_dynamic-update-slice_fusion.4.piece0), channel_id=1, source_target_pairs={{0,4},{2,6},{4,0},{6,2},{1,5},{3,7},{5,1},{7,3},{8,12},{10,14},{12... | collective-permute-start | bytes 491528 | tf_op jit(solution)/shard_map/ppermute | solution.py:440
  50.5 4.5 %collective-permute-start.9 = (bf16[128,640]{1,0:T(8,128)(2,1)S(1)}, bf16[128,640]{1,0:T(8,128)(2,1)S(1)}, u32[]{:S(2)}, u32[]{:S(2)}) collective-permute-start(bf16[128,640]{1,0:T(8,128)(2,1)S(1)} %constant_dynamic-update-slice_fusion.4.piece0), channel_id=1, source_target_pairs={{0,6},{2,0},{4,2},{6,4},{1,7},{3,1},{5,3},{7,5},{8,14},{10,8},{12,... | collective-permute-start | bytes 491528 | tf_op jit(solution)/shard_map/ppermute | solution.py:440
  55.0 15.1 %collective-permute-start.10 = (bf16[8,384,384]{2,1,0:T(8,128)(2,1)}, bf16[8,384,384]{2,1,0:T(8,128)(2,1)S(1)}, u32[]{:S(2)}, u32[]{:S(2)}) collective-permute-start(bf16[8,384,384]{2,1,0:T(8,128)(2,1)} %all-to-all-done.mixer_hbm), channel_id=1, source_target_pairs={{0,1},{1,0},{2,3},{3,2},{4,5},{5,4},{6,7},{7,6},{8,9},{9,8},{10,11... | collective-permute-start | bytes 7077896 | tf_op jit(solution)/shard_map/ppermute | solution.py:444
  60.0 3.1 %copy-start.1 = (bf16[588,6144]{1,0:T(8,128)(2,1)S(1)}, bf16[588,6144]{1,0:T(8,128)(2,1)}, u32[]{:S(2)}) copy-start(bf16[588,6144]{1,0:T(8,128)(2,1)} %weight_hbm.3) | copy-start | bytes 21676036
  70.1 23.3 %copy-start = (bf16[3072,384]{1,0:T(8,128)(2,1)S(1)}, bf16[3072,384]{1,0:T(8,128)(2,1)}, u32[]{:S(2)}) copy-start(bf16[3072,384]{1,0:T(8,128)(2,1)} %refs_2_.1) | copy-start | bytes 7077892
  77.9 10.8 %collective-permute-start.11 = (bf16[512,384]{1,0:T(8,128)(2,1)S(1)}, bf16[512,384]{1,0:T(8,128)(2,1)S(1)}, u32[]{:S(2)}, u32[]{:S(2)}) collective-permute-start(bf16[512,384]{1,0:T(8,128)(2,1)S(1)} %get-tuple-element.34.refs_0_), channel_id=1, source_target_pairs={{0,8},{8,0},{1,9},{9,1},{2,10},{10,2},{3,11},{11,3},{4,12},{12,4},... | collective-permute-start | bytes 1179656 | tf_op jit(solution)/shard_map/ppermute | solution.py:440
  78.0 12.0 %collective-permute-start.12 = (bf16[512,384]{1,0:T(8,128)(2,1)S(1)}, bf16[512,384]{1,0:T(8,128)(2,1)S(1)}, u32[]{:S(2)}, u32[]{:S(2)}) collective-permute-start(bf16[512,384]{1,0:T(8,128)(2,1)S(1)} %get-tuple-element.34.refs_0_), channel_id=1, source_target_pairs={{0,2},{2,4},{4,6},{6,0},{1,3},{3,5},{5,7},{7,1},{8,10},{10,12},{12... | collective-permute-start | bytes 1179656 | tf_op jit(solution)/shard_map/ppermute | solution.py:440
  79.5 10.5 %collective-permute-start.13 = (bf16[512,384]{1,0:T(8,128)(2,1)S(1)}, bf16[512,384]{1,0:T(8,128)(2,1)S(1)}, u32[]{:S(2)}, u32[]{:S(2)}) collective-permute-start(bf16[512,384]{1,0:T(8,128)(2,1)S(1)} %get-tuple-element.34.refs_0_), channel_id=1, source_target_pairs={{0,6},{2,0},{4,2},{6,4},{1,7},{3,1},{5,3},{7,5},{8,14},{10,8},{12,... | collective-permute-start | bytes 1179656 | tf_op jit(solution)/shard_map/ppermute | solution.py:440
  90.0 9.6 %collective-permute-start.14 = (bf16[512,384]{1,0:T(8,128)(2,1)S(1)}, bf16[512,384]{1,0:T(8,128)(2,1)S(1)}, u32[]{:S(2)}, u32[]{:S(2)}) collective-permute-start(bf16[512,384]{1,0:T(8,128)(2,1)S(1)} %collective-permute-done.12.refs_2_), channel_id=1, source_target_pairs={{0,8},{8,0},{1,9},{9,1},{2,10},{10,2},{3,11},{11,3},{4,12},{12,4},... | collective-permute-start | bytes 1179656 | tf_op jit(solution)/shard_map/ppermute | solution.py:440
  91.1 9.1 %collective-permute-start.15 = (bf16[512,384]{1,0:T(8,128)(2,1)S(1)}, bf16[512,384]{1,0:T(8,128)(2,1)S(1)}, u32[]{:S(2)}, u32[]{:S(2)}) collective-permute-start(bf16[512,384]{1,0:T(8,128)(2,1)S(1)} %collective-permute-done.11.refs_1_), channel_id=1, source_target_pairs={{0,6},{2,0},{4,2},{6,4},{1,7},{3,1},{5,3},{7,5},{8,14},{10,8},{12,... | collective-permute-start | bytes 1179656 | tf_op jit(solution)/shard_map/ppermute | solution.py:440
  93.5 10.5 %collective-permute-start.16 = (bf16[512,384]{1,0:T(8,128)(2,1)S(1)}, bf16[512,384]{1,0:T(8,128)(2,1)S(1)}, u32[]{:S(2)}, u32[]{:S(2)}) collective-permute-start(bf16[512,384]{1,0:T(8,128)(2,1)S(1)} %collective-permute-done.12.refs_2_), channel_id=1, source_target_pairs={{0,2},{2,4},{4,6},{6,0},{1,3},{3,5},{5,7},{7,1},{8,10},{10,12},{12... | collective-permute-start | bytes 1179656 | tf_op jit(solution)/shard_map/ppermute | solution.py:440
  100.2 6.3 %collective-permute-start.18 = (bf16[256,384]{1,0:T(8,128)(2,1)S(1)}, bf16[256,384]{1,0:T(8,128)(2,1)S(1)}, u32[]{:S(2)}, u32[]{:S(2)}) collective-permute-start(bf16[256,384]{1,0:T(8,128)(2,1)S(1)} %slice.7), channel_id=1, source_target_pairs={{0,6},{2,0},{4,2},{6,4},{1,7},{3,1},{5,3},{7,5},{8,14},{10,8},{12,... | collective-permute-start | bytes 589832 | tf_op jit(solution)/shard_map/ppermute | solution.py:440
  103.9 5.8 %collective-permute-start.17 = (bf16[256,384]{1,0:T(8,128)(2,1)S(1)}, bf16[256,384]{1,0:T(8,128)(2,1)S(1)}, u32[]{:S(2)}, u32[]{:S(2)}) collective-permute-start(bf16[256,384]{1,0:T(8,128)(2,1)S(1)} %slice.6), channel_id=1, source_target_pairs={{0,2},{2,4},{4,6},{6,0},{1,3},{3,5},{5,7},{7,1},{8,10},{10,12},{12... | collective-permute-start | bytes 589832 | tf_op jit(solution)/shard_map/ppermute | solution.py:440
  111.4 22.5 %all-to-all-start.1 = ((bf16[16,64,384]{2,1,0:T(8,128)(2,1)}), bf16[16,64,384]{2,1,0:T(8,128)(2,1)S(1)}, u32[]{:S(2)}, u32[]{:S(2)}) async-start(bf16[16,64,384]{2,1,0:T(8,128)(2,1)} %mlp_out_1.1), calls=%async_computation.1 | async-start | bytes 1572864 | tf_op jit(solution)/shard_map/all_to_all | solution.py:478
  119.4 14.6 %collective-permute-start.19 = (bf16[64,384]{1,0:T(8,128)(2,1)S(1)}, bf16[64,384]{1,0:T(8,128)(2,1)S(1)}, u32[]{:S(2)}, u32[]{:S(2)}) collective-permute-start(bf16[64,384]{1,0:T(8,128)(2,1)S(1)} %get-tuple-element.43), channel_id=1, source_target_pairs={{0,1},{1,0},{2,3},{3,2},{4,5},{5,4},{6,7},{7,6},{8,9},{9,8},{10,11... | collective-permute-start | bytes 147464 | tf_op jit(solution)/shard_map/ppermute | solution.py:444

commit v9 on v8

--- a/solution.py
+++ b/solution.py
@@ -212,6 +212,7 @@
     rows1 = W1 + count * (side + 1) * W1
     rows2 = W2 + count * (side // 2 + 1) * W2
     images, noise = images.transpose(1, 3, 0, 2), noise.transpose(1, 3, 0, 2)
+    l1, down, l2, up = (pltpu.with_memory_space_constraint(w, pltpu.HBM) for w in (l1, down, l2, up))
     vm = pl.BlockSpec(memory_space=pltpu.VMEM)
     hb = pl.BlockSpec(memory_space=pltpu.HBM)
     purified, patches = pl.pallas_call(
@@ -238,7 +239,7 @@
             pltpu.VMEM(up.shape, bf16),
             pltpu.SemaphoreType.DMA((7,)),
         ],
-        compiler_params=pltpu.CompilerParams(vmem_limit_bytes=58 << 20),
+        compiler_params=pltpu.CompilerParams(vmem_limit_bytes=36 << 20),
         cost_estimate=pl.CostEstimate(flops=10_000_000_000, transcendentals=3_000_000, bytes_accessed=12_000_000),
         name="score_net",
     )(images, noise, stem_w, l1, down, l2, up, out_w.T)
@@ -323,6 +324,7 @@
     free = pl.BlockSpec(memory_space=pl.ANY)
     sent = jax.ShapeDtypeStruct((tokens // 8, span), bf16)
     state = [(tokens + 16, width), (tokens, 128), (tokens, 128)]
+    weight = pltpu.with_memory_space_constraint(weight, pltpu.HBM)
     vm = pl.BlockSpec(memory_space=pltpu.VMEM)
     hb = pl.BlockSpec(memory_space=pltpu.HBM)
     if flip:
@@ -429,10 +431,10 @@
         in_specs=[pl.BlockSpec(memory_space=pltpu.HBM)],
         out_specs=pl.BlockSpec(memory_space=pltpu.VMEM),
         scratch_shapes=[pltpu.SemaphoreType.DMA((count,))],
-        compiler_params=pltpu.CompilerParams(vmem_limit_bytes=58 << 20),
+        compiler_params=pltpu.CompilerParams(vmem_limit_bytes=8 << 20),
         cost_estimate=pl.CostEstimate(flops=0, transcendentals=0, bytes_accessed=2 * whole.size * 2),
         name="split_columns",
-    )(whole)
+    )(pltpu.with_memory_space_constraint(whole, pltpu.HBM))
 
 
 def shift(value, axis, k):

time: 135 us -> 131 us (0.970)
  local copies, waits for them, and re-layouts: 4.56 us -> 2.2 us
  Pallas kernels: 43 us -> 41 us
    unnamed x11 -> x19, local copies, waits for them, and re-layouts: 3.85 us -> 1.49 us
    pallas_call x1, Pallas kernels: 3.12 us -> 1.67 us  [split_call(): pl.pallas_call(split_kernel, out_shape=jax.ShapeDtypeStruct((count, depth...]
  transfers between devices with their start and end apart: 22 -> 22, of which waited for: 14 -> 13; matrix products, arithmetic and copies ran while one was open for 1% -> 0% of each run, Pallas kernels for 25% -> 24%
where the time goes in v9:
time: 131 us
  starting transfers between devices  44 us (34%)
  waiting for transfers between devices  42.3 us (32%)
  Pallas kernels  41 us (31%)
  local copies, waits for them, and re-layouts  2.2 us (2%)
    ppermute x16, waiting for transfers between devices, shift(): return lax.ppermute(value, axis, [(i, (i + k) % n) for i in range(n)])  27 us
    ppermute x16, starting transfers between devices, shift(): return lax.ppermute(value, axis, [(i, (i + k) % n) for i in range(n)])  23.8 us
    pallas_call x1, Pallas kernels, score_call(): pl.pallas_call(functools.partial(score_kernel, side, count), out_shape=(j...  19.2 us
    pallas_call x2, Pallas kernels, embed_call(): pl.pallas_call(functools.partial(embed_kernel, flip), out_shape=shapes, i...  15.2 us
    all_to_all x1, waiting for transfers between devices, on_device(): shares = lax.all_to_all(shares, ('zh', 'x', 'core'), 0, 0)  14.3 us
    all_to_all x1, starting transfers between devices, on_device(): shares = lax.all_to_all(shares, ('zh', 'x', 'core'), 0, 0)  8.2 us
    ppermute x3, starting transfers between devices, swap(): return lax.ppermute(value, 'core', [(0, 1), (1, 0)])  6.24 us
    all_to_all x1, starting transfers between devices, on_device(): own_in = lax.all_to_all(split_call(mlp_in, 8), ('zl', 'y'), 0, 0)  5.77 us
  transfers between devices with their start and end apart: 22, of which 13 were waited for; matrix products, arithmetic and copies ran while one was open for 0% of the time, Pallas kernels for 24%

profile of v9, /device:TPU:1, one launch (start us, length us, event | category | flops | bytes accessed | tf_op | source)
XLA Modules:
  0.0 130.5 jit_solution(3934393037382282230)
XLA Ops:
  0.6 1.5 %collective-permute-start = (bf16[3072,384]{1,0:T(8,128)(2,1)}, bf16[3072,384]{1,0:T(8,128)(2,1)S(1)}, u32[]{:S(2)}, u32[]{:S(2)}) collective-permute-start(bf16[3072,384]{1,0:T(8,128)(2,1)} %refs_2_.1), channel_id=1, source_target_pairs={{0,1},{1,0},{2,3},{3,2},{4,5},{5,4},{6,7},{7,6},{8,9},{9,8},{10,11... | collective-permute-start | bytes 7077896 | tf_op jit(solution)/shard_map/ppermute | solution.py:446
  2.1 1.7 %split_columns.1 = bf16[8,384,384]{2,1,0:T(8,128)(2,1)S(1)} custom-call(bf16[384,3072]{1,0:T(8,128)(2,1)} %whole.1), custom_call_target="tpu_custom_call" | custom-call | bytes 4718592 | tf_op jit(solution)/shard_map/split_columns/pallas_call | solution.py:428
  3.8 1.4 %copy-done.1 = bf16[8,384,384]{2,1,0:T(8,128)(2,1)} copy-done((bf16[8,384,384]{2,1,0:T(8,128)(2,1)}, bf16[8,384,384]{2,1,0:T(8,128)(2,1)S(1)}, u32[]{:S(2)}) %copy-start.1) | copy-done | bytes 2359320
  5.3 5.8 %all-to-all-start = ((bf16[8,384,384]{2,1,0:T(8,128)(2,1)}), bf16[8,384,384]{2,1,0:T(8,128)(2,1)}, u32[]{:S(2)}, u32[]{:S(2)}) async-start(bf16[8,384,384]{2,1,0:T(8,128)(2,1)} %copy-done.1), calls=%async_computation | async-start | bytes 4718592 | tf_op jit(solution)/shard_map/all_to_all | solution.py:452
  11.1 19.2 %score_net.1 = (f32[28,3,2,28]{3,2,1,0:T(2,128)}, bf16[8,640]{1,0:T(8,128)(2,1)S(1)}) custom-call(f32[28,3,2,28]{3,2,1,0:T(2,128)S(1)} %bitcast.13, f32[28,3,2,28]{3,2,1,0:T(2,128)S(1)} %bitcast.14, bf16[27,256]{1,0:T(8,128)(2,1)S(1)} %copy-done.5, bf16[4,2304,256]{2,1,0:T(8,128)(2,1)} %l1_hbm.1, bf16[1024,256]{1,0:T(8,128)(2,1)} %down_hbm.1, ...), custom_call_target="tpu_custom_call" | custom-call | flops 10000000000 | bytes 12000000 | tf_op jit(solution)/shard_map/score_net/pallas_call | solution.py:218
  30.3 1.3 collective-permute-start.1
  31.6 2.5 %collective-permute-start.2 = (bf16[8,640]{1,0:T(8,128)(2,1)S(1)}, bf16[8,640]{1,0:T(8,128)(2,1)S(1)}, u32[]{:S(2)}, u32[]{:S(2)}) collective-permute-start(bf16[8,640]{1,0:T(8,128)(2,1)S(1)} %get-tuple-element.25), channel_id=1, source_target_pairs={{0,32},{16,48},{32,0},{48,16},{1,33},{17,49},{33,1},{49,17},{2,34}... | collective-permute-start | bytes 30728 | tf_op jit(solution)/shard_map/ppermute | solution.py:442
  34.1 1.1 collective-permute-start.3
  36.1 0.9 collective-permute-done.3
  37.0 3.3 %collective-permute-start.4 = (bf16[32,640]{1,0:T(8,128)(2,1)S(1)}, bf16[32,640]{1,0:T(8,128)(2,1)S(1)}, u32[]{:S(2)}, u32[]{:S(2)}) collective-permute-start(bf16[32,640]{1,0:T(8,128)(2,1)S(1)} %get-tuple-element.44), channel_id=1, source_target_pairs={{0,64},{64,0},{1,65},{65,1},{2,66},{66,2},{3,67},{67,3},{4,68},{68... | collective-permute-start | bytes 122888 | tf_op jit(solution)/shard_map/ppermute | solution.py:442
  41.2 3.1 %collective-permute-done.4 = bf16[32,640]{1,0:T(8,128)(2,1)S(1)} collective-permute-done((bf16[32,640]{1,0:T(8,128)(2,1)S(1)}, bf16[32,640]{1,0:T(8,128)(2,1)S(1)}, u32[]{:S(2)}, u32[]{:S(2)}) %collective-permute-start.4) | collective-permute-done | bytes 40992 | tf_op jit(solution)/shard_map/ppermute | solution.py:442
  44.3 1.0 collective-permute-done.6
  45.2 1.2 collective-permute-start.7
  46.4 2.8 %collective-permute-start.8 = (bf16[128,640]{1,0:T(8,128)(2,1)S(1)}, bf16[128,640]{1,0:T(8,128)(2,1)S(1)}, u32[]{:S(2)}, u32[]{:S(2)}) collective-permute-start(bf16[128,640]{1,0:T(8,128)(2,1)S(1)} %constant_dynamic-update-slice_fusion.4.piece0), channel_id=1, source_target_pairs={{0,4},{2,6},{4,0},{6,2},{1,5},{3,7},{5,1},{7,3},{8,12},{10,14},{12... | collective-permute-start | bytes 491528 | tf_op jit(solution)/shard_map/ppermute | solution.py:442
  50.7 3.0 %collective-permute-done.8.piece2 = bf16[128,640]{1,0:T(8,128)(2,1)S(1)} collective-permute-done((bf16[128,640]{1,0:T(8,128)(2,1)S(1)}, bf16[128,640]{1,0:T(8,128)(2,1)S(1)}, u32[]{:S(2)}, u32[]{:S(2)}) %collective-permute-start.8) | collective-permute-done | bytes 163872 | tf_op jit(solution)/shard_map/ppermute | solution.py:442
  53.7 4.6 %collective-permute-start.10 = (bf16[8,384,384]{2,1,0:T(8,128)(2,1)}, bf16[8,384,384]{2,1,0:T(8,128)(2,1)S(1)}, u32[]{:S(2)}, u32[]{:S(2)}) collective-permute-start(bf16[8,384,384]{2,1,0:T(8,128)(2,1)} %all-to-all-done.mixer_hbm), channel_id=1, source_target_pairs={{0,1},{1,0},{2,3},{3,2},{4,5},{5,4},{6,7},{7,6},{8,9},{9,8},{10,11... | collective-permute-start | bytes 7077896 | tf_op jit(solution)/shard_map/ppermute | solution.py:446
  58.3 7.4 %embed_own.1 = (f32[528,384]{1,0:T(8,128)S(1)}, f32[512,128]{1,0:T(8,128)S(1)}, f32[512,128]{1,0:T(8,128)S(1)}, bf16[64,384]{1,0:T(8,128)(2,1)S(1)}) custom-call(bf16[128,640]{1,0:T(8,128)(2,1)S(1)} %constant_dynamic-update-slice_fusion.4.piece0, bf16[128,640]{1,0:T(8,128)(2,1)S(1)} %collective-permute-done.7.piece1, ...), custom_call_target="tpu_custom_call" | custom-call | flops 3500000000 | bytes 8000000 | tf_op jit(solution)/shard_map/embed_own/pallas_call | solution.py:336
  65.7 7.9 %embed_mate.1 = (bf16[512,384]{1,0:T(8,128)(2,1)S(1)}, bf16[64,384]{1,0:T(8,128)(2,1)S(1)}) custom-call(bf16[128,640]{1,0:T(8,128)(2,1)S(1)} %constant_dynamic-update-slice_fusion.4.piece0, bf16[128,640]{1,0:T(8,128)(2,1)S(1)} %collective-permute-done.7.piece1, bf16[128,640]{1,0:T(8,128)(2,1)S(1)} %collective-permute-done.8.piece2, ...), custom_call_target="tpu_custom_call" | custom-call | flops 3500000000 | bytes 8000000 | tf_op jit(solution)/shard_map/embed_mate/pallas_call | solution.py:336
  73.7 1.5 %collective-permute-start.12 = (bf16[512,384]{1,0:T(8,128)(2,1)S(1)}, bf16[512,384]{1,0:T(8,128)(2,1)S(1)}, u32[]{:S(2)}, u32[]{:S(2)}) collective-permute-start(bf16[512,384]{1,0:T(8,128)(2,1)S(1)} %get-tuple-element.34.refs_0_), channel_id=1, source_target_pairs={{0,2},{2,4},{4,6},{6,0},{1,3},{3,5},{5,7},{7,1},{8,10},{10,12},{12... | collective-permute-start | bytes 1179656 | tf_op jit(solution)/shard_map/ppermute | solution.py:442
  75.2 1.2 collective-permute-start.13
  76.4 8.0 %collective-permute-done.11.refs_1_ = bf16[512,384]{1,0:T(8,128)(2,1)S(1)} collective-permute-done((bf16[512,384]{1,0:T(8,128)(2,1)S(1)}, bf16[512,384]{1,0:T(8,128)(2,1)S(1)}, u32[]{:S(2)}, u32[]{:S(2)}) %collective-permute-start.11) | collective-permute-done | bytes 393248 | tf_op jit(solution)/shard_map/ppermute | solution.py:442
  84.4 1.3 collective-permute-done.12.refs_2_
  85.7 1.1 collective-permute-start.14
  86.7 2.3 %collective-permute-start.15 = (bf16[512,384]{1,0:T(8,128)(2,1)S(1)}, bf16[512,384]{1,0:T(8,128)(2,1)S(1)}, u32[]{:S(2)}, u32[]{:S(2)}) collective-permute-start(bf16[512,384]{1,0:T(8,128)(2,1)S(1)} %collective-permute-done.11.refs_1_), channel_id=1, source_target_pairs={{0,6},{2,0},{4,2},{6,4},{1,7},{3,1},{5,3},{7,5},{8,14},{10,8},{12,... | collective-permute-start | bytes 1179656 | tf_op jit(solution)/shard_map/ppermute | solution.py:442
  89.1 1.8 %mlp_out_4.1.refs_0_ = f32[512,768]{1,0:T(8,128)S(1)} custom-call(bf16[512,384]{1,0:T(8,128)(2,1)S(1)} %get-tuple-element.34.refs_0_, bf16[512,384]{1,0:T(8,128)(2,1)S(1)} %collective-permute-done.11.refs_1_, bf16[512,384]{1,0:T(8,128)(2,1)S(1)} %collective-permute-done.12.refs_2_, bf16[512,384]{1,0:T(8,128)(2,1)S(1)} %collective-permute-done.13.refs_3_, ...), custom_call_target="tpu_custom_call" | custom-call | flops 1207959552 | bytes 5505024 | tf_op jit(solution)/shard_map/mlp_out_4/pallas_call | solution.py:400
  90.9 4.4 %collective-permute-done.14.refs_3_ = bf16[512,384]{1,0:T(8,128)(2,1)S(1)} collective-permute-done((bf16[512,384]{1,0:T(8,128)(2,1)S(1)}, bf16[512,384]{1,0:T(8,128)(2,1)S(1)}, u32[]{:S(2)}, u32[]{:S(2)}) %collective-permute-start.14) | collective-permute-done | bytes 393248 | tf_op jit(solution)/shard_map/ppermute | solution.py:442
  95.8 3.5 %collective-permute-start.18 = (bf16[256,384]{1,0:T(8,128)(2,1)S(1)}, bf16[256,384]{1,0:T(8,128)(2,1)S(1)}, u32[]{:S(2)}, u32[]{:S(2)}) collective-permute-start(bf16[256,384]{1,0:T(8,128)(2,1)S(1)} %slice.7), channel_id=1, source_target_pairs={{0,6},{2,0},{4,2},{6,4},{1,7},{3,1},{5,3},{7,5},{8,14},{10,8},{12,... | collective-permute-start | bytes 589832 | tf_op jit(solution)/shard_map/ppermute | solution.py:442
  99.6 1.5 %mlp_out_3.1.refs_0_ = f32[512,768]{1,0:T(8,128)S(1)} custom-call(f32[512,768]{1,0:T(8,128)S(1)} %mlp_out_4.1.refs_0_, bf16[512,384]{1,0:T(8,128)(2,1)S(1)} %collective-permute-done.16.refs_1_, bf16[512,384]{1,0:T(8,128)(2,1)S(1)} %collective-permute-done.15.refs_2_, bf16[512,384]{1,0:T(8,128)(2,1)S(1)} %collective-permute-done.14.refs_3_, ...), custom_call_target="tpu_custom_call" | custom-call | flops 905969664 | bytes 4521984 | tf_op jit(solution)/shard_map/mlp_out_3/pallas_call | solution.py:400
  101.9 3.4 %collective-permute-done.17 = bf16[256,384]{1,0:T(8,128)(2,1)S(1)} collective-permute-done((bf16[256,384]{1,0:T(8,128)(2,1)S(1)}, bf16[256,384]{1,0:T(8,128)(2,1)S(1)}, u32[]{:S(2)}, u32[]{:S(2)}) %collective-permute-start.17) | collective-permute-done | bytes 196640 | tf_op jit(solution)/shard_map/ppermute | solution.py:442
  105.4 1.6 %mlp_out_1.1 = bf16[16,64,384]{2,1,0:T(8,128)(2,1)} custom-call(f32[512,768]{1,0:T(8,128)S(1)} %mlp_out_3.1.refs_0_, bf16[512,384]{1,0:T(8,128)(2,1)S(1)} %pad_maximum_fusion.refs_1_, bf16[3072,384]{1,0:T(8,128)(2,1)S(1)} %copy-done, bf16[3072,384]{1,0:T(8,128)(2,1)S(1)} %collective-permute-done.refs_5_.refs_3_), custom_call_target="tpu_custom_call" | custom-call | flops 301989888 | bytes 2555904 | tf_op jit(solution)/shard_map/mlp_out_1/pallas_call | solution.py:400
  107.0 8.2 %all-to-all-start.1 = ((bf16[16,64,384]{2,1,0:T(8,128)(2,1)}), bf16[16,64,384]{2,1,0:T(8,128)(2,1)S(1)}, u32[]{:S(2)}, u32[]{:S(2)}) async-start(bf16[16,64,384]{2,1,0:T(8,128)(2,1)} %mlp_out_1.1), calls=%async_computation.1 | async-start | bytes 1572864 | tf_op jit(solution)/shard_map/all_to_all | solution.py:480
  115.4 14.3 %all-to-all-done.1 = bf16[16,64,384]{2,1,0:T(8,128)(2,1)S(1)} async-done(((bf16[16,64,384]{2,1,0:T(8,128)(2,1)}), bf16[16,64,384]{2,1,0:T(8,128)(2,1)S(1)}, u32[]{:S(2)}, u32[]{:S(2)}) %all-to-all-start.1) | async-done | bytes 786464 | tf_op jit(solution)/shard_map/all_to_all | solution.py:480
  (46 shorter events, 6.0 us)
Async XLA Ops:
  0.6 29.7 %collective-permute-start = (bf16[3072,384]{1,0:T(8,128)(2,1)}, bf16[3072,384]{1,0:T(8,128)(2,1)S(1)}, u32[]{:S(2)}, u32[]{:S(2)}) collective-permute-start(bf16[3072,384]{1,0:T(8,128)(2,1)} %refs_2_.1), channel_id=1, source_target_pairs={{0,1},{1,0},{2,3},{3,2},{4,5},{5,4},{6,7},{7,6},{8,9},{9,8},{10,11... | collective-permute-start | bytes 7077896 | tf_op jit(solution)/shard_map/ppermute | solution.py:446
  3.8 1.4 %copy-start.1 = (bf16[8,384,384]{2,1,0:T(8,128)(2,1)}, bf16[8,384,384]{2,1,0:T(8,128)(2,1)S(1)}, u32[]{:S(2)}) copy-start(bf16[8,384,384]{2,1,0:T(8,128)(2,1)S(1)} %split_columns.1) | copy-start | bytes 7077892
  5.2 5.8 %copy-start.2 = (f32[2,28,28,3]{2,0,3,1:T(2,128)S(1)}, f32[2,28,28,3]{2,0,3,1:T(2,128)}, u32[]{:S(2)}) copy-start(f32[2,28,28,3]{2,0,3,1:T(2,128)} %param.12) | copy-start | bytes 56452
  5.2 5.8 %copy-start.3 = (f32[2,28,28,3]{2,0,3,1:T(2,128)S(1)}, f32[2,28,28,3]{2,0,3,1:T(2,128)}, u32[]{:S(2)}) copy-start(f32[2,28,28,3]{2,0,3,1:T(2,128)} %param.13) | copy-start | bytes 56452
  5.2 5.8 %copy-start.5 = (bf16[27,256]{1,0:T(8,128)(2,1)S(1)}, bf16[27,256]{1,0:T(8,128)(2,1)}, u32[]{:S(2)}) copy-start(bf16[27,256]{1,0:T(8,128)(2,1)} %stem_w.1) | copy-start | bytes 41476
  5.3 5.8 %copy-start.6 = (bf16[256,3]{0,1:T(4,128)(2,1)S(1)}, bf16[256,3]{0,1:T(4,128)(2,1)}, u32[]{:S(2)}) copy-start(bf16[256,3]{0,1:T(4,128)(2,1)} %param.19) | copy-start | bytes 4612
  5.3 44.7 %all-to-all-start = ((bf16[8,384,384]{2,1,0:T(8,128)(2,1)}), bf16[8,384,384]{2,1,0:T(8,128)(2,1)}, u32[]{:S(2)}, u32[]{:S(2)}) async-start(bf16[8,384,384]{2,1,0:T(8,128)(2,1)} %copy-done.1), calls=%async_computation | async-start | bytes 4718592 | tf_op jit(solution)/shard_map/all_to_all | solution.py:452
  11.1 47.2 %copy-start.4 = (f32[6144]{0:T(1024)S(1)}, f32[6144]{0:T(1024)}, u32[]{:S(2)}) copy-start(f32[6144]{0:T(1024)} %param.21) | copy-start | bytes 73732
  30.3 4.9 %collective-permute-start.1 = (bf16[8,640]{1,0:T(8,128)(2,1)S(1)}, bf16[8,640]{1,0:T(8,128)(2,1)S(1)}, u32[]{:S(2)}, u32[]{:S(2)}) collective-permute-start(bf16[8,640]{1,0:T(8,128)(2,1)S(1)} %get-tuple-element.25), channel_id=1, source_target_pairs={{0,16},{16,32},{32,48},{48,0},{1,17},{17,33},{33,49},{49,1},{2,18}... | collective-permute-start | bytes 30728 | tf_op jit(solution)/shard_map/ppermute | solution.py:442
  31.6 4.4 %collective-permute-start.2 = (bf16[8,640]{1,0:T(8,128)(2,1)S(1)}, bf16[8,640]{1,0:T(8,128)(2,1)S(1)}, u32[]{:S(2)}, u32[]{:S(2)}) collective-permute-start(bf16[8,640]{1,0:T(8,128)(2,1)S(1)} %get-tuple-element.25), channel_id=1, source_target_pairs={{0,32},{16,48},{32,0},{48,16},{1,33},{17,49},{33,1},{49,17},{2,34}... | collective-permute-start | bytes 30728 | tf_op jit(solution)/shard_map/ppermute | solution.py:442
  34.1 2.9 %collective-permute-start.3 = (bf16[8,640]{1,0:T(8,128)(2,1)S(1)}, bf16[8,640]{1,0:T(8,128)(2,1)S(1)}, u32[]{:S(2)}, u32[]{:S(2)}) collective-permute-start(bf16[8,640]{1,0:T(8,128)(2,1)S(1)} %get-tuple-element.25), channel_id=1, source_target_pairs={{0,48},{16,0},{32,16},{48,32},{1,49},{17,1},{33,17},{49,33},{2,50}... | collective-permute-start | bytes 30728 | tf_op jit(solution)/shard_map/ppermute | solution.py:442
  37.0 7.2 %collective-permute-start.4 = (bf16[32,640]{1,0:T(8,128)(2,1)S(1)}, bf16[32,640]{1,0:T(8,128)(2,1)S(1)}, u32[]{:S(2)}, u32[]{:S(2)}) collective-permute-start(bf16[32,640]{1,0:T(8,128)(2,1)S(1)} %get-tuple-element.44), channel_id=1, source_target_pairs={{0,64},{64,0},{1,65},{65,1},{2,66},{66,2},{3,67},{67,3},{4,68},{68... | collective-permute-start | bytes 122888 | tf_op jit(solution)/shard_map/ppermute | solution.py:442
  40.3 3.9 %collective-permute-start.5 = (bf16[32,640]{1,0:T(8,128)(2,1)S(1)}, bf16[32,640]{1,0:T(8,128)(2,1)S(1)}, u32[]{:S(2)}, u32[]{:S(2)}) collective-permute-start(bf16[32,640]{1,0:T(8,128)(2,1)S(1)} %get-tuple-element.44), channel_id=1, source_target_pairs={{0,8},{8,0},{1,9},{9,1},{2,10},{10,2},{3,11},{11,3},{4,12},{12,4},... | collective-permute-start | bytes 122888 | tf_op jit(solution)/shard_map/ppermute | solution.py:442
  41.2 4.1 %collective-permute-start.6 = (bf16[32,640]{1,0:T(8,128)(2,1)S(1)}, bf16[32,640]{1,0:T(8,128)(2,1)S(1)}, u32[]{:S(2)}, u32[]{:S(2)}) collective-permute-start(bf16[32,640]{1,0:T(8,128)(2,1)S(1)} %get-tuple-element.44), channel_id=1, source_target_pairs={{0,72},{8,64},{64,8},{72,0},{1,73},{9,65},{65,9},{73,1},{2,74},{10... | collective-permute-start | bytes 122888 | tf_op jit(solution)/shard_map/ppermute | solution.py:459
  45.2 5.5 %collective-permute-start.7 = (bf16[128,640]{1,0:T(8,128)(2,1)S(1)}, bf16[128,640]{1,0:T(8,128)(2,1)S(1)}, u32[]{:S(2)}, u32[]{:S(2)}) collective-permute-start(bf16[128,640]{1,0:T(8,128)(2,1)S(1)} %constant_dynamic-update-slice_fusion.4.piece0), channel_id=1, source_target_pairs={{0,2},{2,4},{4,6},{6,0},{1,3},{3,5},{5,7},{7,1},{8,10},{10,12},{12... | collective-permute-start | bytes 491528 | tf_op jit(solution)/shard_map/ppermute | solution.py:442
  46.4 7.3 %collective-permute-start.8 = (bf16[128,640]{1,0:T(8,128)(2,1)S(1)}, bf16[128,640]{1,0:T(8,128)(2,1)S(1)}, u32[]{:S(2)}, u32[]{:S(2)}) collective-permute-start(bf16[128,640]{1,0:T(8,128)(2,1)S(1)} %constant_dynamic-update-slice_fusion.4.piece0), channel_id=1, source_target_pairs={{0,4},{2,6},{4,0},{6,2},{1,5},{3,7},{5,1},{7,3},{8,12},{10,14},{12... | collective-permute-start | bytes 491528 | tf_op jit(solution)/shard_map/ppermute | solution.py:442
  49.2 4.5 %collective-permute-start.9 = (bf16[128,640]{1,0:T(8,128)(2,1)S(1)}, bf16[128,640]{1,0:T(8,128)(2,1)S(1)}, u32[]{:S(2)}, u32[]{:S(2)}) collective-permute-start(bf16[128,640]{1,0:T(8,128)(2,1)S(1)} %constant_dynamic-update-slice_fusion.4.piece0), channel_id=1, source_target_pairs={{0,6},{2,0},{4,2},{6,4},{1,7},{3,1},{5,3},{7,5},{8,14},{10,8},{12,... | collective-permute-start | bytes 491528 | tf_op jit(solution)/shard_map/ppermute | solution.py:442
  53.7 11.9 %collective-permute-start.10 = (bf16[8,384,384]{2,1,0:T(8,128)(2,1)}, bf16[8,384,384]{2,1,0:T(8,128)(2,1)S(1)}, u32[]{:S(2)}, u32[]{:S(2)}) collective-permute-start(bf16[8,384,384]{2,1,0:T(8,128)(2,1)} %all-to-all-done.mixer_hbm), channel_id=1, source_target_pairs={{0,1},{1,0},{2,3},{3,2},{4,5},{5,4},{6,7},{7,6},{8,9},{9,8},{10,11... | collective-permute-start | bytes 7077896 | tf_op jit(solution)/shard_map/ppermute | solution.py:446
  65.7 23.4 %copy-start = (bf16[3072,384]{1,0:T(8,128)(2,1)S(1)}, bf16[3072,384]{1,0:T(8,128)(2,1)}, u32[]{:S(2)}) copy-start(bf16[3072,384]{1,0:T(8,128)(2,1)} %refs_2_.1) | copy-start | bytes 7077892
  73.6 10.8 %collective-permute-start.11 = (bf16[512,384]{1,0:T(8,128)(2,1)S(1)}, bf16[512,384]{1,0:T(8,128)(2,1)S(1)}, u32[]{:S(2)}, u32[]{:S(2)}) collective-permute-start(bf16[512,384]{1,0:T(8,128)(2,1)S(1)} %get-tuple-element.34.refs_0_), channel_id=1, source_target_pairs={{0,8},{8,0},{1,9},{9,1},{2,10},{10,2},{3,11},{11,3},{4,12},{12,4},... | collective-permute-start | bytes 1179656 | tf_op jit(solution)/shard_map/ppermute | solution.py:442
  73.7 12.0 %collective-permute-start.12 = (bf16[512,384]{1,0:T(8,128)(2,1)S(1)}, bf16[512,384]{1,0:T(8,128)(2,1)S(1)}, u32[]{:S(2)}, u32[]{:S(2)}) collective-permute-start(bf16[512,384]{1,0:T(8,128)(2,1)S(1)} %get-tuple-element.34.refs_0_), channel_id=1, source_target_pairs={{0,2},{2,4},{4,6},{6,0},{1,3},{3,5},{5,7},{7,1},{8,10},{10,12},{12... | collective-permute-start | bytes 1179656 | tf_op jit(solution)/shard_map/ppermute | solution.py:442
  75.2 10.5 %collective-permute-start.13 = (bf16[512,384]{1,0:T(8,128)(2,1)S(1)}, bf16[512,384]{1,0:T(8,128)(2,1)S(1)}, u32[]{:S(2)}, u32[]{:S(2)}) collective-permute-start(bf16[512,384]{1,0:T(8,128)(2,1)S(1)} %get-tuple-element.34.refs_0_), channel_id=1, source_target_pairs={{0,6},{2,0},{4,2},{6,4},{1,7},{3,1},{5,3},{7,5},{8,14},{10,8},{12,... | collective-permute-start | bytes 1179656 | tf_op jit(solution)/shard_map/ppermute | solution.py:442
  85.7 9.6 %collective-permute-start.14 = (bf16[512,384]{1,0:T(8,128)(2,1)S(1)}, bf16[512,384]{1,0:T(8,128)(2,1)S(1)}, u32[]{:S(2)}, u32[]{:S(2)}) collective-permute-start(bf16[512,384]{1,0:T(8,128)(2,1)S(1)} %collective-permute-done.12.refs_2_), channel_id=1, source_target_pairs={{0,8},{8,0},{1,9},{9,1},{2,10},{10,2},{3,11},{11,3},{4,12},{12,4},... | collective-permute-start | bytes 1179656 | tf_op jit(solution)/shard_map/ppermute | solution.py:442
  86.7 9.0 %collective-permute-start.15 = (bf16[512,384]{1,0:T(8,128)(2,1)S(1)}, bf16[512,384]{1,0:T(8,128)(2,1)S(1)}, u32[]{:S(2)}, u32[]{:S(2)}) collective-permute-start(bf16[512,384]{1,0:T(8,128)(2,1)S(1)} %collective-permute-done.11.refs_1_), channel_id=1, source_target_pairs={{0,6},{2,0},{4,2},{6,4},{1,7},{3,1},{5,3},{7,5},{8,14},{10,8},{12,... | collective-permute-start | bytes 1179656 | tf_op jit(solution)/shard_map/ppermute | solution.py:442
  89.1 10.5 %collective-permute-start.16 = (bf16[512,384]{1,0:T(8,128)(2,1)S(1)}, bf16[512,384]{1,0:T(8,128)(2,1)S(1)}, u32[]{:S(2)}, u32[]{:S(2)}) collective-permute-start(bf16[512,384]{1,0:T(8,128)(2,1)S(1)} %collective-permute-done.12.refs_2_), channel_id=1, source_target_pairs={{0,2},{2,4},{4,6},{6,0},{1,3},{3,5},{5,7},{7,1},{8,10},{10,12},{12... | collective-permute-start | bytes 1179656 | tf_op jit(solution)/shard_map/ppermute | solution.py:442
  95.8 6.1 %collective-permute-start.18 = (bf16[256,384]{1,0:T(8,128)(2,1)S(1)}, bf16[256,384]{1,0:T(8,128)(2,1)S(1)}, u32[]{:S(2)}, u32[]{:S(2)}) collective-permute-start(bf16[256,384]{1,0:T(8,128)(2,1)S(1)} %slice.7), channel_id=1, source_target_pairs={{0,6},{2,0},{4,2},{6,4},{1,7},{3,1},{5,3},{7,5},{8,14},{10,8},{12,... | collective-permute-start | bytes 589832 | tf_op jit(solution)/shard_map/ppermute | solution.py:442
  99.3 6.0 %collective-permute-start.17 = (bf16[256,384]{1,0:T(8,128)(2,1)S(1)}, bf16[256,384]{1,0:T(8,128)(2,1)S(1)}, u32[]{:S(2)}, u32[]{:S(2)}) collective-permute-start(bf16[256,384]{1,0:T(8,128)(2,1)S(1)} %slice.6), channel_id=1, source_target_pairs={{0,2},{2,4},{4,6},{6,0},{1,3},{3,5},{5,7},{7,1},{8,10},{10,12},{12... | collective-permute-start | bytes 589832 | tf_op jit(solution)/shard_map/ppermute | solution.py:442
  107.0 22.7 %all-to-all-start.1 = ((bf16[16,64,384]{2,1,0:T(8,128)(2,1)}), bf16[16,64,384]{2,1,0:T(8,128)(2,1)S(1)}, u32[]{:S(2)}, u32[]{:S(2)}) async-start(bf16[16,64,384]{2,1,0:T(8,128)(2,1)} %mlp_out_1.1), calls=%async_computation.1 | async-start | bytes 1572864 | tf_op jit(solution)/shard_map/all_to_all | solution.py:480
  115.2 14.6 %collective-permute-start.19 = (bf16[64,384]{1,0:T(8,128)(2,1)S(1)}, bf16[64,384]{1,0:T(8,128)(2,1)S(1)}, u32[]{:S(2)}, u32[]{:S(2)}) collective-permute-start(bf16[64,384]{1,0:T(8,128)(2,1)S(1)} %get-tuple-element.43), channel_id=1, source_target_pairs={{0,1},{1,0},{2,3},{3,2},{4,5},{5,4},{6,7},{7,6},{8,9},{9,8},{10,11... | collective-permute-start | bytes 147464 | tf_op jit(solution)/shard_map/ppermute | solution.py:446

commit v10 on v9

--- a/solution.py
+++ b/solution.py
@@ -381,9 +381,10 @@
     share = out.shape[1]
     tokens = done.shape[0]
     high, across, size = lax.axis_index("zh"), lax.axis_index("x"), lax.axis_size("x")
+    near = (across, across + 1 - 2 * (across % 2), (across + 2) % size, 3 - across)
     for q in range(tokens // share):
         rows = jnp.concatenate([done[b * share + q * 8:b * share + q * 8 + 8, :] for b in range(8)], axis=0).astype(bf16)
-        r = (high + q // size) % 2 * size + (across + size - q % size) % size
+        r = (high + q // size) % 2 * size + near[q % size]
         out[2 * r + core] = rows[:, 0:span]
         out[2 * r + 1 - core] = rows[:, span:2 * span]
 
@@ -455,7 +456,9 @@
     purified, patches = score_call(images, noise_field, stem_weight, level_one, down_weight, level_two,
                                    up_weight, out_weight)
     mate_out, patches = lax.optimization_barrier((mate_out, patches))
-    patches = jnp.concatenate([patches] + [shift(patches, "x", k) for k in (1, 2, 3)], axis=0)
+    pair = lax.ppermute(patches, "x", [(0, 1), (1, 0), (2, 3), (3, 2)])
+    patches = jnp.concatenate([patches, pair], axis=0)
+    patches = jnp.concatenate([patches, shift(patches, "x", 2)], axis=0)
     both = lax.ppermute(patches, ("zh", "zl"), [(i, 3 - i) for i in range(4)])
     patches = jnp.concatenate([patches, shift(patches, "zh", 1), shift(patches, "zl", 1), both], axis=0)
     pieces = [patches] + [shift(patches, "y", k) for k in (1, 2, 3)]

time: 131 us -> 132 us (level)
  waiting for transfers between devices: 42.3 us -> 44.4 us
    ppermute x16 -> x14, starting transfers between devices: 23.8 us -> 21.3 us  [shift(): return lax.ppermute(value, axis, [(i, (i + k) % n) for i in range(n)])]
    ppermute x0 -> x1, waiting for transfers between devices: none -> 1.71 us  [on_device(): pair = lax.ppermute(patches, 'x', [(0, 1), (1, 0), (2, 3), (3, 2)])]
    ppermute x16 -> x14, waiting for transfers between devices: 27 us -> 26.6 us  [shift(): return lax.ppermute(value, axis, [(i, (i + k) % n) for i in range(n)])]
  transfers between devices with their start and end apart: 22 -> 21, of which waited for: 13 -> 14; matrix products, arithmetic and copies ran while one was open for 0% -> 0% of each run, Pallas kernels for 24% -> 24%
where the time goes in v10:
time: 132 us
  waiting for transfers between devices  44.4 us (34%)
  starting transfers between devices  43.2 us (33%)
  Pallas kernels  41 us (31%)
  local copies, waits for them, and re-layouts  2.21 us (2%)
    ppermute x14, waiting for transfers between devices, shift(): return lax.ppermute(value, axis, [(i, (i + k) % n) for i in range(n)])  26.6 us
    ppermute x14, starting transfers between devices, shift(): return lax.ppermute(value, axis, [(i, (i + k) % n) for i in range(n)])  21.3 us
    pallas_call x1, Pallas kernels, score_call(): pl.pallas_call(functools.partial(score_kernel, side, count), out_shape=(j...  19.2 us
    pallas_call x2, Pallas kernels, embed_call(): pl.pallas_call(functools.partial(embed_kernel, flip), out_shape=shapes, i...  15.2 us
    all_to_all x1, waiting for transfers between devices, on_device(): shares = lax.all_to_all(shares, ('zh', 'x', 'core'), 0, 0)  14.3 us
    all_to_all x1, starting transfers between devices, on_device(): shares = lax.all_to_all(shares, ('zh', 'x', 'core'), 0, 0)  8.41 us
    ppermute x3, starting transfers between devices, swap(): return lax.ppermute(value, 'core', [(0, 1), (1, 0)])  6.42 us
    all_to_all x1, starting transfers between devices, on_device(): own_in = lax.all_to_all(split_call(mlp_in, 8), ('zl', 'y'), 0, 0)  5.77 us
  transfers between devices with their start and end apart: 21, of which 14 were waited for; matrix products, arithmetic and copies ran while one was open for 0% of the time, Pallas kernels for 24%

profile of v10, /device:TPU:1, one launch (start us, length us, event | category | flops | bytes accessed | tf_op | source)
XLA Modules:
  0.0 131.8 jit_solution(9651555973585821512)
XLA Ops:
  0.6 1.5 %collective-permute-start = (bf16[3072,384]{1,0:T(8,128)(2,1)}, bf16[3072,384]{1,0:T(8,128)(2,1)S(1)}, u32[]{:S(2)}, u32[]{:S(2)}) collective-permute-start(bf16[3072,384]{1,0:T(8,128)(2,1)} %refs_2_.1), channel_id=1, source_target_pairs={{0,1},{1,0},{2,3},{3,2},{4,5},{5,4},{6,7},{7,6},{8,9},{9,8},{10,11... | collective-permute-start | bytes 7077896 | tf_op jit(solution)/shard_map/ppermute | solution.py:447
  2.1 1.7 %split_columns.1 = bf16[8,384,384]{2,1,0:T(8,128)(2,1)S(1)} custom-call(bf16[384,3072]{1,0:T(8,128)(2,1)} %whole.1), custom_call_target="tpu_custom_call" | custom-call | bytes 4718592 | tf_op jit(solution)/shard_map/split_columns/pallas_call | solution.py:429
  3.8 1.4 %copy-done.1 = bf16[8,384,384]{2,1,0:T(8,128)(2,1)} copy-done((bf16[8,384,384]{2,1,0:T(8,128)(2,1)}, bf16[8,384,384]{2,1,0:T(8,128)(2,1)S(1)}, u32[]{:S(2)}) %copy-start.1) | copy-done | bytes 2359320
  5.3 5.8 %all-to-all-start = ((bf16[8,384,384]{2,1,0:T(8,128)(2,1)}), bf16[8,384,384]{2,1,0:T(8,128)(2,1)}, u32[]{:S(2)}, u32[]{:S(2)}) async-start(bf16[8,384,384]{2,1,0:T(8,128)(2,1)} %copy-done.1), calls=%async_computation | async-start | bytes 4718592 | tf_op jit(solution)/shard_map/all_to_all | solution.py:453
  11.1 19.2 %score_net.1 = (f32[28,3,2,28]{3,2,1,0:T(2,128)}, bf16[8,640]{1,0:T(8,128)(2,1)S(1)}) custom-call(f32[28,3,2,28]{3,2,1,0:T(2,128)S(1)} %bitcast.13, f32[28,3,2,28]{3,2,1,0:T(2,128)S(1)} %bitcast.14, bf16[27,256]{1,0:T(8,128)(2,1)S(1)} %copy-done.5, bf16[4,2304,256]{2,1,0:T(8,128)(2,1)} %l1_hbm.1, bf16[1024,256]{1,0:T(8,128)(2,1)} %down_hbm.1, ...), custom_call_target="tpu_custom_call" | custom-call | flops 10000000000 | bytes 12000000 | tf_op jit(solution)/shard_map/score_net/pallas_call | solution.py:218
  30.3 1.3 collective-permute-start.1
  31.6 1.7 %collective-permute-done.1 = bf16[8,640]{1,0:T(8,128)(2,1)S(1)} collective-permute-done((bf16[8,640]{1,0:T(8,128)(2,1)S(1)}, bf16[8,640]{1,0:T(8,128)(2,1)S(1)}, u32[]{:S(2)}, u32[]{:S(2)}) %collective-permute-start.1) | collective-permute-done | bytes 10272 | tf_op jit(solution)/shard_map/ppermute | solution.py:459
  33.4 2.7 %collective-permute-start.2 = (bf16[16,640]{1,0:T(8,128)(2,1)S(1)}, bf16[16,640]{1,0:T(8,128)(2,1)S(1)}, u32[]{:S(2)}, u32[]{:S(2)}) collective-permute-start(bf16[16,640]{1,0:T(8,128)(2,1)S(1)} %pad_maximum_fusion.1), channel_id=1, source_target_pairs={{0,32},{16,48},{32,0},{48,16},{1,33},{17,49},{33,1},{49,17},{2,34}... | collective-permute-start | bytes 61448 | tf_op jit(solution)/shard_map/ppermute | solution.py:443
  36.1 1.8 %collective-permute-done.2 = bf16[16,640]{1,0:T(8,128)(2,1)S(1)} collective-permute-done((bf16[16,640]{1,0:T(8,128)(2,1)S(1)}, bf16[16,640]{1,0:T(8,128)(2,1)S(1)}, u32[]{:S(2)}, u32[]{:S(2)}) %collective-permute-start.2) | collective-permute-done | bytes 20512 | tf_op jit(solution)/shard_map/ppermute | solution.py:443
  37.9 3.3 %collective-permute-start.3 = (bf16[32,640]{1,0:T(8,128)(2,1)S(1)}, bf16[32,640]{1,0:T(8,128)(2,1)S(1)}, u32[]{:S(2)}, u32[]{:S(2)}) collective-permute-start(bf16[32,640]{1,0:T(8,128)(2,1)S(1)} %get-tuple-element.44), channel_id=1, source_target_pairs={{0,64},{64,0},{1,65},{65,1},{2,66},{66,2},{3,67},{67,3},{4,68},{68... | collective-permute-start | bytes 122888 | tf_op jit(solution)/shard_map/ppermute | solution.py:443
  42.1 1.6 %collective-permute-done.3 = bf16[32,640]{1,0:T(8,128)(2,1)S(1)} collective-permute-done((bf16[32,640]{1,0:T(8,128)(2,1)S(1)}, bf16[32,640]{1,0:T(8,128)(2,1)S(1)}, u32[]{:S(2)}, u32[]{:S(2)}) %collective-permute-start.3) | collective-permute-done | bytes 40992 | tf_op jit(solution)/shard_map/ppermute | solution.py:443
  44.3 1.8 %collective-permute-done.5 = bf16[32,640]{1,0:T(8,128)(2,1)S(1)} collective-permute-done((bf16[32,640]{1,0:T(8,128)(2,1)S(1)}, bf16[32,640]{1,0:T(8,128)(2,1)S(1)}, u32[]{:S(2)}, u32[]{:S(2)}) %collective-permute-start.5) | collective-permute-done | bytes 40992 | tf_op jit(solution)/shard_map/ppermute | solution.py:462
  47.2 3.0 %collective-permute-start.7 = (bf16[128,640]{1,0:T(8,128)(2,1)S(1)}, bf16[128,640]{1,0:T(8,128)(2,1)S(1)}, u32[]{:S(2)}, u32[]{:S(2)}) collective-permute-start(bf16[128,640]{1,0:T(8,128)(2,1)S(1)} %constant_dynamic-update-slice_fusion.3.piece0), channel_id=1, source_target_pairs={{0,4},{2,6},{4,0},{6,2},{1,5},{3,7},{5,1},{7,3},{8,12},{10,14},{12... | collective-permute-start | bytes 491528 | tf_op jit(solution)/shard_map/ppermute | solution.py:443
  50.5 1.1 collective-permute-done.6.piece1
  51.6 3.0 %collective-permute-done.7.piece2 = bf16[128,640]{1,0:T(8,128)(2,1)S(1)} collective-permute-done((bf16[128,640]{1,0:T(8,128)(2,1)S(1)}, bf16[128,640]{1,0:T(8,128)(2,1)S(1)}, u32[]{:S(2)}, u32[]{:S(2)}) %collective-permute-start.7) | collective-permute-done | bytes 163872 | tf_op jit(solution)/shard_map/ppermute | solution.py:443
  54.6 4.7 %collective-permute-start.9 = (bf16[8,384,384]{2,1,0:T(8,128)(2,1)}, bf16[8,384,384]{2,1,0:T(8,128)(2,1)S(1)}, u32[]{:S(2)}, u32[]{:S(2)}) collective-permute-start(bf16[8,384,384]{2,1,0:T(8,128)(2,1)} %all-to-all-done.mixer_hbm), channel_id=1, source_target_pairs={{0,1},{1,0},{2,3},{3,2},{4,5},{5,4},{6,7},{7,6},{8,9},{9,8},{10,11... | collective-permute-start | bytes 7077896 | tf_op jit(solution)/shard_map/ppermute | solution.py:447
  59.4 7.4 %embed_own.1 = (f32[528,384]{1,0:T(8,128)S(1)}, f32[512,128]{1,0:T(8,128)S(1)}, f32[512,128]{1,0:T(8,128)S(1)}, bf16[64,384]{1,0:T(8,128)(2,1)S(1)}) custom-call(bf16[128,640]{1,0:T(8,128)(2,1)S(1)} %constant_dynamic-update-slice_fusion.3.piece0, bf16[128,640]{1,0:T(8,128)(2,1)S(1)} %collective-permute-done.6.piece1, ...), custom_call_target="tpu_custom_call" | custom-call | flops 3500000000 | bytes 8000000 | tf_op jit(solution)/shard_map/embed_own/pallas_call | solution.py:336
  66.8 7.9 %embed_mate.1 = (bf16[512,384]{1,0:T(8,128)(2,1)S(1)}, bf16[64,384]{1,0:T(8,128)(2,1)S(1)}) custom-call(bf16[128,640]{1,0:T(8,128)(2,1)S(1)} %constant_dynamic-update-slice_fusion.3.piece0, bf16[128,640]{1,0:T(8,128)(2,1)S(1)} %collective-permute-done.6.piece1, bf16[128,640]{1,0:T(8,128)(2,1)S(1)} %collective-permute-done.7.piece2, ...), custom_call_target="tpu_custom_call" | custom-call | flops 3500000000 | bytes 8000000 | tf_op jit(solution)/shard_map/embed_mate/pallas_call | solution.py:336
  74.7 1.5 %collective-permute-start.11 = (bf16[512,384]{1,0:T(8,128)(2,1)S(1)}, bf16[512,384]{1,0:T(8,128)(2,1)S(1)}, u32[]{:S(2)}, u32[]{:S(2)}) collective-permute-start(bf16[512,384]{1,0:T(8,128)(2,1)S(1)} %get-tuple-element.34.refs_0_), channel_id=1, source_target_pairs={{0,2},{2,4},{4,6},{6,0},{1,3},{3,5},{5,7},{7,1},{8,10},{10,12},{12... | collective-permute-start | bytes 1179656 | tf_op jit(solution)/shard_map/ppermute | solution.py:443
  76.2 1.2 collective-permute-start.12
  77.5 8.0 %collective-permute-done.10.refs_1_ = bf16[512,384]{1,0:T(8,128)(2,1)S(1)} collective-permute-done((bf16[512,384]{1,0:T(8,128)(2,1)S(1)}, bf16[512,384]{1,0:T(8,128)(2,1)S(1)}, u32[]{:S(2)}, u32[]{:S(2)}) %collective-permute-start.10) | collective-permute-done | bytes 393248 | tf_op jit(solution)/shard_map/ppermute | solution.py:443
  85.4 1.3 collective-permute-done.11.refs_2_
  86.7 1.1 collective-permute-start.13
  87.8 2.3 %collective-permute-start.14 = (bf16[512,384]{1,0:T(8,128)(2,1)S(1)}, bf16[512,384]{1,0:T(8,128)(2,1)S(1)}, u32[]{:S(2)}, u32[]{:S(2)}) collective-permute-start(bf16[512,384]{1,0:T(8,128)(2,1)S(1)} %collective-permute-done.10.refs_1_), channel_id=1, source_target_pairs={{0,6},{2,0},{4,2},{6,4},{1,7},{3,1},{5,3},{7,5},{8,14},{10,8},{12,... | collective-permute-start | bytes 1179656 | tf_op jit(solution)/shard_map/ppermute | solution.py:443
  90.2 1.8 %mlp_out_4.1.refs_0_ = f32[512,768]{1,0:T(8,128)S(1)} custom-call(bf16[512,384]{1,0:T(8,128)(2,1)S(1)} %get-tuple-element.34.refs_0_, bf16[512,384]{1,0:T(8,128)(2,1)S(1)} %collective-permute-done.10.refs_1_, bf16[512,384]{1,0:T(8,128)(2,1)S(1)} %collective-permute-done.11.refs_2_, bf16[512,384]{1,0:T(8,128)(2,1)S(1)} %collective-permute-done.12.refs_3_, ...), custom_call_target="tpu_custom_call" | custom-call | flops 1207959552 | bytes 5505024 | tf_op jit(solution)/shard_map/mlp_out_4/pallas_call | solution.py:401
  91.9 4.4 %collective-permute-done.13.refs_3_ = bf16[512,384]{1,0:T(8,128)(2,1)S(1)} collective-permute-done((bf16[512,384]{1,0:T(8,128)(2,1)S(1)}, bf16[512,384]{1,0:T(8,128)(2,1)S(1)}, u32[]{:S(2)}, u32[]{:S(2)}) %collective-permute-start.13) | collective-permute-done | bytes 393248 | tf_op jit(solution)/shard_map/ppermute | solution.py:443
  96.9 3.5 %collective-permute-start.17 = (bf16[256,384]{1,0:T(8,128)(2,1)S(1)}, bf16[256,384]{1,0:T(8,128)(2,1)S(1)}, u32[]{:S(2)}, u32[]{:S(2)}) collective-permute-start(bf16[256,384]{1,0:T(8,128)(2,1)S(1)} %slice.7), channel_id=1, source_target_pairs={{0,6},{2,0},{4,2},{6,4},{1,7},{3,1},{5,3},{7,5},{8,14},{10,8},{12,... | collective-permute-start | bytes 589832 | tf_op jit(solution)/shard_map/ppermute | solution.py:443
  100.7 1.5 %mlp_out_3.1.refs_0_ = f32[512,768]{1,0:T(8,128)S(1)} custom-call(f32[512,768]{1,0:T(8,128)S(1)} %mlp_out_4.1.refs_0_, bf16[512,384]{1,0:T(8,128)(2,1)S(1)} %collective-permute-done.15.refs_1_, bf16[512,384]{1,0:T(8,128)(2,1)S(1)} %collective-permute-done.14.refs_2_, bf16[512,384]{1,0:T(8,128)(2,1)S(1)} %collective-permute-done.13.refs_3_, ...), custom_call_target="tpu_custom_call" | custom-call | flops 905969664 | bytes 4521984 | tf_op jit(solution)/shard_map/mlp_out_3/pallas_call | solution.py:401
  103.0 3.4 %collective-permute-done.16 = bf16[256,384]{1,0:T(8,128)(2,1)S(1)} collective-permute-done((bf16[256,384]{1,0:T(8,128)(2,1)S(1)}, bf16[256,384]{1,0:T(8,128)(2,1)S(1)}, u32[]{:S(2)}, u32[]{:S(2)}) %collective-permute-start.16) | collective-permute-done | bytes 196640 | tf_op jit(solution)/shard_map/ppermute | solution.py:443
  106.4 1.6 %mlp_out_1.1 = bf16[16,64,384]{2,1,0:T(8,128)(2,1)} custom-call(f32[512,768]{1,0:T(8,128)S(1)} %mlp_out_3.1.refs_0_, bf16[512,384]{1,0:T(8,128)(2,1)S(1)} %pad_maximum_fusion.refs_1_, bf16[3072,384]{1,0:T(8,128)(2,1)S(1)} %copy-done, bf16[3072,384]{1,0:T(8,128)(2,1)S(1)} %collective-permute-done.refs_5_.refs_3_), custom_call_target="tpu_custom_call" | custom-call | flops 301989888 | bytes 2555904 | tf_op jit(solution)/shard_map/mlp_out_1/pallas_call | solution.py:401
  108.1 8.4 %all-to-all-start.1 = ((bf16[16,64,384]{2,1,0:T(8,128)(2,1)}), bf16[16,64,384]{2,1,0:T(8,128)(2,1)S(1)}, u32[]{:S(2)}, u32[]{:S(2)}) async-start(bf16[16,64,384]{2,1,0:T(8,128)(2,1)} %mlp_out_1.1), calls=%async_computation.1 | async-start | bytes 1572864 | tf_op jit(solution)/shard_map/all_to_all | solution.py:483
  116.7 14.3 %all-to-all-done.1 = bf16[16,64,384]{2,1,0:T(8,128)(2,1)S(1)} async-done(((bf16[16,64,384]{2,1,0:T(8,128)(2,1)}), bf16[16,64,384]{2,1,0:T(8,128)(2,1)S(1)}, u32[]{:S(2)}, u32[]{:S(2)}) %all-to-all-start.1) | async-done | bytes 786464 | tf_op jit(solution)/shard_map/all_to_all | solution.py:483
  (44 shorter events, 5.9 us)
Async XLA Ops:
  0.6 29.7 %collective-permute-start = (bf16[3072,384]{1,0:T(8,128)(2,1)}, bf16[3072,384]{1,0:T(8,128)(2,1)S(1)}, u32[]{:S(2)}, u32[]{:S(2)}) collective-permute-start(bf16[3072,384]{1,0:T(8,128)(2,1)} %refs_2_.1), channel_id=1, source_target_pairs={{0,1},{1,0},{2,3},{3,2},{4,5},{5,4},{6,7},{7,6},{8,9},{9,8},{10,11... | collective-permute-start | bytes 7077896 | tf_op jit(solution)/shard_map/ppermute | solution.py:447
  3.8 1.4 %copy-start.1 = (bf16[8,384,384]{2,1,0:T(8,128)(2,1)}, bf16[8,384,384]{2,1,0:T(8,128)(2,1)S(1)}, u32[]{:S(2)}) copy-start(bf16[8,384,384]{2,1,0:T(8,128)(2,1)S(1)} %split_columns.1) | copy-start | bytes 7077892
  5.3 5.8 %copy-start.2 = (f32[2,28,28,3]{2,0,3,1:T(2,128)S(1)}, f32[2,28,28,3]{2,0,3,1:T(2,128)}, u32[]{:S(2)}) copy-start(f32[2,28,28,3]{2,0,3,1:T(2,128)} %param.12) | copy-start | bytes 56452
  5.3 5.8 %copy-start.3 = (f32[2,28,28,3]{2,0,3,1:T(2,128)S(1)}, f32[2,28,28,3]{2,0,3,1:T(2,128)}, u32[]{:S(2)}) copy-start(f32[2,28,28,3]{2,0,3,1:T(2,128)} %param.13) | copy-start | bytes 56452
  5.3 5.8 %copy-start.5 = (bf16[27,256]{1,0:T(8,128)(2,1)S(1)}, bf16[27,256]{1,0:T(8,128)(2,1)}, u32[]{:S(2)}) copy-start(bf16[27,256]{1,0:T(8,128)(2,1)} %stem_w.1) | copy-start | bytes 41476
  5.3 5.8 %copy-start.6 = (bf16[256,3]{0,1:T(4,128)(2,1)S(1)}, bf16[256,3]{0,1:T(4,128)(2,1)}, u32[]{:S(2)}) copy-start(bf16[256,3]{0,1:T(4,128)(2,1)} %param.19) | copy-start | bytes 4612
  5.3 45.2 %all-to-all-start = ((bf16[8,384,384]{2,1,0:T(8,128)(2,1)}), bf16[8,384,384]{2,1,0:T(8,128)(2,1)}, u32[]{:S(2)}, u32[]{:S(2)}) async-start(bf16[8,384,384]{2,1,0:T(8,128)(2,1)} %copy-done.1), calls=%async_computation | async-start | bytes 4718592 | tf_op jit(solution)/shard_map/all_to_all | solution.py:453
  11.1 48.3 %copy-start.4 = (f32[6144]{0:T(1024)S(1)}, f32[6144]{0:T(1024)}, u32[]{:S(2)}) copy-start(f32[6144]{0:T(1024)} %param.21) | copy-start | bytes 73732
  30.3 3.0 %collective-permute-start.1 = (bf16[8,640]{1,0:T(8,128)(2,1)S(1)}, bf16[8,640]{1,0:T(8,128)(2,1)S(1)}, u32[]{:S(2)}, u32[]{:S(2)}) collective-permute-start(bf16[8,640]{1,0:T(8,128)(2,1)S(1)} %get-tuple-element.25), channel_id=1, source_target_pairs={{0,16},{16,0},{32,48},{48,32},{1,17},{17,1},{33,49},{49,33},{2,18}... | collective-permute-start | bytes 30728 | tf_op jit(solution)/shard_map/ppermute | solution.py:459
  33.4 4.5 %collective-permute-start.2 = (bf16[16,640]{1,0:T(8,128)(2,1)S(1)}, bf16[16,640]{1,0:T(8,128)(2,1)S(1)}, u32[]{:S(2)}, u32[]{:S(2)}) collective-permute-start(bf16[16,640]{1,0:T(8,128)(2,1)S(1)} %pad_maximum_fusion.1), channel_id=1, source_target_pairs={{0,32},{16,48},{32,0},{48,16},{1,33},{17,49},{33,1},{49,17},{2,34}... | collective-permute-start | bytes 61448 | tf_op jit(solution)/shard_map/ppermute | solution.py:443
  37.9 5.7 %collective-permute-start.3 = (bf16[32,640]{1,0:T(8,128)(2,1)S(1)}, bf16[32,640]{1,0:T(8,128)(2,1)S(1)}, u32[]{:S(2)}, u32[]{:S(2)}) collective-permute-start(bf16[32,640]{1,0:T(8,128)(2,1)S(1)} %get-tuple-element.44), channel_id=1, source_target_pairs={{0,64},{64,0},{1,65},{65,1},{2,66},{66,2},{3,67},{67,3},{4,68},{68... | collective-permute-start | bytes 122888 | tf_op jit(solution)/shard_map/ppermute | solution.py:443
  41.2 3.1 %collective-permute-start.4 = (bf16[32,640]{1,0:T(8,128)(2,1)S(1)}, bf16[32,640]{1,0:T(8,128)(2,1)S(1)}, u32[]{:S(2)}, u32[]{:S(2)}) collective-permute-start(bf16[32,640]{1,0:T(8,128)(2,1)S(1)} %get-tuple-element.44), channel_id=1, source_target_pairs={{0,8},{8,0},{1,9},{9,1},{2,10},{10,2},{3,11},{11,3},{4,12},{12,4},... | collective-permute-start | bytes 122888 | tf_op jit(solution)/shard_map/ppermute | solution.py:443
  42.1 4.1 %collective-permute-start.5 = (bf16[32,640]{1,0:T(8,128)(2,1)S(1)}, bf16[32,640]{1,0:T(8,128)(2,1)S(1)}, u32[]{:S(2)}, u32[]{:S(2)}) collective-permute-start(bf16[32,640]{1,0:T(8,128)(2,1)S(1)} %get-tuple-element.44), channel_id=1, source_target_pairs={{0,72},{8,64},{64,8},{72,0},{1,73},{9,65},{65,9},{73,1},{2,74},{10... | collective-permute-start | bytes 122888 | tf_op jit(solution)/shard_map/ppermute | solution.py:462
  46.1 5.5 %collective-permute-start.6 = (bf16[128,640]{1,0:T(8,128)(2,1)S(1)}, bf16[128,640]{1,0:T(8,128)(2,1)S(1)}, u32[]{:S(2)}, u32[]{:S(2)}) collective-permute-start(bf16[128,640]{1,0:T(8,128)(2,1)S(1)} %constant_dynamic-update-slice_fusion.3.piece0), channel_id=1, source_target_pairs={{0,2},{2,4},{4,6},{6,0},{1,3},{3,5},{5,7},{7,1},{8,10},{10,12},{12... | collective-permute-start | bytes 491528 | tf_op jit(solution)/shard_map/ppermute | solution.py:443
  47.2 7.5 %collective-permute-start.7 = (bf16[128,640]{1,0:T(8,128)(2,1)S(1)}, bf16[128,640]{1,0:T(8,128)(2,1)S(1)}, u32[]{:S(2)}, u32[]{:S(2)}) collective-permute-start(bf16[128,640]{1,0:T(8,128)(2,1)S(1)} %constant_dynamic-update-slice_fusion.3.piece0), channel_id=1, source_target_pairs={{0,4},{2,6},{4,0},{6,2},{1,5},{3,7},{5,1},{7,3},{8,12},{10,14},{12... | collective-permute-start | bytes 491528 | tf_op jit(solution)/shard_map/ppermute | solution.py:443
  50.1 4.5 %collective-permute-start.8 = (bf16[128,640]{1,0:T(8,128)(2,1)S(1)}, bf16[128,640]{1,0:T(8,128)(2,1)S(1)}, u32[]{:S(2)}, u32[]{:S(2)}) collective-permute-start(bf16[128,640]{1,0:T(8,128)(2,1)S(1)} %constant_dynamic-update-slice_fusion.3.piece0), channel_id=1, source_target_pairs={{0,6},{2,0},{4,2},{6,4},{1,7},{3,1},{5,3},{7,5},{8,14},{10,8},{12,... | collective-permute-start | bytes 491528 | tf_op jit(solution)/shard_map/ppermute | solution.py:443
  54.6 12.1 %collective-permute-start.9 = (bf16[8,384,384]{2,1,0:T(8,128)(2,1)}, bf16[8,384,384]{2,1,0:T(8,128)(2,1)S(1)}, u32[]{:S(2)}, u32[]{:S(2)}) collective-permute-start(bf16[8,384,384]{2,1,0:T(8,128)(2,1)} %all-to-all-done.mixer_hbm), channel_id=1, source_target_pairs={{0,1},{1,0},{2,3},{3,2},{4,5},{5,4},{6,7},{7,6},{8,9},{9,8},{10,11... | collective-permute-start | bytes 7077896 | tf_op jit(solution)/shard_map/ppermute | solution.py:447
  66.7 23.4 %copy-start = (bf16[3072,384]{1,0:T(8,128)(2,1)S(1)}, bf16[3072,384]{1,0:T(8,128)(2,1)}, u32[]{:S(2)}) copy-start(bf16[3072,384]{1,0:T(8,128)(2,1)} %refs_2_.1) | copy-start | bytes 7077892
  74.6 10.8 %collective-permute-start.10 = (bf16[512,384]{1,0:T(8,128)(2,1)S(1)}, bf16[512,384]{1,0:T(8,128)(2,1)S(1)}, u32[]{:S(2)}, u32[]{:S(2)}) collective-permute-start(bf16[512,384]{1,0:T(8,128)(2,1)S(1)} %get-tuple-element.34.refs_0_), channel_id=1, source_target_pairs={{0,8},{8,0},{1,9},{9,1},{2,10},{10,2},{3,11},{11,3},{4,12},{12,4},... | collective-permute-start | bytes 1179656 | tf_op jit(solution)/shard_map/ppermute | solution.py:443
  74.7 12.0 %collective-permute-start.11 = (bf16[512,384]{1,0:T(8,128)(2,1)S(1)}, bf16[512,384]{1,0:T(8,128)(2,1)S(1)}, u32[]{:S(2)}, u32[]{:S(2)}) collective-permute-start(bf16[512,384]{1,0:T(8,128)(2,1)S(1)} %get-tuple-element.34.refs_0_), channel_id=1, source_target_pairs={{0,2},{2,4},{4,6},{6,0},{1,3},{3,5},{5,7},{7,1},{8,10},{10,12},{12... | collective-permute-start | bytes 1179656 | tf_op jit(solution)/shard_map/ppermute | solution.py:443
  76.2 10.5 %collective-permute-start.12 = (bf16[512,384]{1,0:T(8,128)(2,1)S(1)}, bf16[512,384]{1,0:T(8,128)(2,1)S(1)}, u32[]{:S(2)}, u32[]{:S(2)}) collective-permute-start(bf16[512,384]{1,0:T(8,128)(2,1)S(1)} %get-tuple-element.34.refs_0_), channel_id=1, source_target_pairs={{0,6},{2,0},{4,2},{6,4},{1,7},{3,1},{5,3},{7,5},{8,14},{10,8},{12,... | collective-permute-start | bytes 1179656 | tf_op jit(solution)/shard_map/ppermute | solution.py:443
  86.7 9.6 %collective-permute-start.13 = (bf16[512,384]{1,0:T(8,128)(2,1)S(1)}, bf16[512,384]{1,0:T(8,128)(2,1)S(1)}, u32[]{:S(2)}, u32[]{:S(2)}) collective-permute-start(bf16[512,384]{1,0:T(8,128)(2,1)S(1)} %collective-permute-done.11.refs_2_), channel_id=1, source_target_pairs={{0,8},{8,0},{1,9},{9,1},{2,10},{10,2},{3,11},{11,3},{4,12},{12,4},... | collective-permute-start | bytes 1179656 | tf_op jit(solution)/shard_map/ppermute | solution.py:443
  87.8 9.0 %collective-permute-start.14 = (bf16[512,384]{1,0:T(8,128)(2,1)S(1)}, bf16[512,384]{1,0:T(8,128)(2,1)S(1)}, u32[]{:S(2)}, u32[]{:S(2)}) collective-permute-start(bf16[512,384]{1,0:T(8,128)(2,1)S(1)} %collective-permute-done.10.refs_1_), channel_id=1, source_target_pairs={{0,6},{2,0},{4,2},{6,4},{1,7},{3,1},{5,3},{7,5},{8,14},{10,8},{12,... | collective-permute-start | bytes 1179656 | tf_op jit(solution)/shard_map/ppermute | solution.py:443
  90.2 10.5 %collective-permute-start.15 = (bf16[512,384]{1,0:T(8,128)(2,1)S(1)}, bf16[512,384]{1,0:T(8,128)(2,1)S(1)}, u32[]{:S(2)}, u32[]{:S(2)}) collective-permute-start(bf16[512,384]{1,0:T(8,128)(2,1)S(1)} %collective-permute-done.11.refs_2_), channel_id=1, source_target_pairs={{0,2},{2,4},{4,6},{6,0},{1,3},{3,5},{5,7},{7,1},{8,10},{10,12},{12... | collective-permute-start | bytes 1179656 | tf_op jit(solution)/shard_map/ppermute | solution.py:443
  96.9 6.1 %collective-permute-start.17 = (bf16[256,384]{1,0:T(8,128)(2,1)S(1)}, bf16[256,384]{1,0:T(8,128)(2,1)S(1)}, u32[]{:S(2)}, u32[]{:S(2)}) collective-permute-start(bf16[256,384]{1,0:T(8,128)(2,1)S(1)} %slice.7), channel_id=1, source_target_pairs={{0,6},{2,0},{4,2},{6,4},{1,7},{3,1},{5,3},{7,5},{8,14},{10,8},{12,... | collective-permute-start | bytes 589832 | tf_op jit(solution)/shard_map/ppermute | solution.py:443
  100.4 6.0 %collective-permute-start.16 = (bf16[256,384]{1,0:T(8,128)(2,1)S(1)}, bf16[256,384]{1,0:T(8,128)(2,1)S(1)}, u32[]{:S(2)}, u32[]{:S(2)}) collective-permute-start(bf16[256,384]{1,0:T(8,128)(2,1)S(1)} %slice.6), channel_id=1, source_target_pairs={{0,2},{2,4},{4,6},{6,0},{1,3},{3,5},{5,7},{7,1},{8,10},{10,12},{12... | collective-permute-start | bytes 589832 | tf_op jit(solution)/shard_map/ppermute | solution.py:443
  108.1 22.9 %all-to-all-start.1 = ((bf16[16,64,384]{2,1,0:T(8,128)(2,1)}), bf16[16,64,384]{2,1,0:T(8,128)(2,1)S(1)}, u32[]{:S(2)}, u32[]{:S(2)}) async-start(bf16[16,64,384]{2,1,0:T(8,128)(2,1)} %mlp_out_1.1), calls=%async_computation.1 | async-start | bytes 1572864 | tf_op jit(solution)/shard_map/all_to_all | solution.py:483
  116.5 14.6 %collective-permute-start.18 = (bf16[64,384]{1,0:T(8,128)(2,1)S(1)}, bf16[64,384]{1,0:T(8,128)(2,1)S(1)}, u32[]{:S(2)}, u32[]{:S(2)}) collective-permute-start(bf16[64,384]{1,0:T(8,128)(2,1)S(1)} %get-tuple-element.43), channel_id=1, source_target_pairs={{0,1},{1,0},{2,3},{3,2},{4,5},{5,4},{6,7},{7,6},{8,9},{9,8},{10,11... | collective-permute-start | bytes 147464 | tf_op jit(solution)/shard_map/ppermute | solution.py:447
